TPU v7x, 32 devices: a whole 2x2x4 slice. The times are simulated.
32 devices in a mesh: ctx: 16 (over z, y, core), fsdp: 2 (over x).
Axes of the slice: x: 2, y: 2, z: 4, core: 2. Of those that a mesh axis runs over, the one named last changes fastest.
Arguments:
- tokens: bfloat16 [2, 2048, 1024], P('fsdp', 'ctx'), may hold values from -6 to 6
- w_qkv: bfloat16 [1024, 3072], P('fsdp'), may hold values from -0.1875 to 0.1875
- w_out: bfloat16 [1024, 1024], P('fsdp'), may hold values from -0.375 to 0.375
- w_up: bfloat16 [1024, 4096], P('fsdp'), may hold values from -0.1875 to 0.1875
- w_down: bfloat16 [4096, 1024], P('fsdp'), may hold values from -0.09375 to 0.09375
- w_time: bfloat16 [256, 2048], P('fsdp'), may hold values from -0.375 to 0.375
- gain_one: bfloat16 [1024], P('fsdp'), may hold values from 0.5 to 1.5
- bias_one: bfloat16 [1024], P('fsdp'), may hold values from -3 to 3
- gain_two: bfloat16 [1024], P('fsdp'), may hold values from 0.5 to 1.5
- bias_two: bfloat16 [1024], P('fsdp'), may hold values from -3 to 3
- bias_up: bfloat16 [4096], P('fsdp'), may hold values from -3 to 3
- bias_down: bfloat16 [1024], P('fsdp'), may hold values from -3 to 3
- lengths: int32 [2, 1], P('fsdp'), may hold values from 1024 to 2048, as said below
- time_steps: int32 [2, 1], P('fsdp'), may hold values from 0 to 999
- cotangent: bfloat16 [2, 2048, 1024], P('fsdp', 'ctx'), may hold values from -6 to 6
Outputs:
- output: bfloat16 [2, 2048, 1024], P('fsdp', 'ctx')
- grad_tokens: bfloat16 [2, 2048, 1024], P('fsdp', 'ctx')
- grad_qkv: float32 [1024, 3072], P('fsdp')
- grad_out: float32 [1024, 1024], P('fsdp')
- grad_up: float32 [1024, 4096], P('fsdp')
- grad_down: float32 [4096, 1024], P('fsdp')
- grad_time: float32 [256, 2048], P('fsdp')
- grad_gain_one: float32 [1024], P('fsdp')
- grad_bias_one: float32 [1024], P('fsdp')
- grad_gain_two: float32 [1024], P('fsdp')
- grad_bias_two: float32 [1024], P('fsdp')
- grad_bias_up: float32 [4096], P('fsdp')
- grad_bias_down: float32 [1024], P('fsdp')
Inputs may be any that keep to these rules, and one draw needn't show every extreme that they name: The 1 lengths of a group add up to at most 2048; the group's tokens after them are padding; in every group some sequence has the largest length.
All inputs are finite; a program needn't handle non-finite values.
Results may differ from a plain program's by a relative error of at most 0.025.
Values may be sent and summed in bfloat16 or wider, within the bound.
No kernel may reach another device: no remote copies, remote signals or barrier semaphores. Data moves between devices by JAX's collectives and lax.ppermute only.
A program may use at most 256 MiB of HBM per device.

v0:
```python
import functools
import math

import jax
import jax.numpy as jnp
import numpy as np
from jax import lax
from jax.experimental import pallas as pl
from jax.experimental.pallas import tpu as pltpu
from jax.sharding import PartitionSpec as P

HEADS = 16
EPSILON = 1e-05
NEGATIVE = -1e30
HIGH = lax.Precision.HIGHEST
F32 = jnp.float32
BF16 = jnp.bfloat16
VMEM_BYTES = 56 << 20


def dims(left, right, left_dim, right_dim):
    return lax.dot_general(
        left, right, (((left_dim,), (right_dim,)), ((), ())), preferred_element_type=F32
    )


def segments(ends, index):
    return sum((index >= end).astype(jnp.int32) for end in ends)


def positions(ends, index, segment):
    begin = jnp.zeros_like(index)
    for at, end in enumerate(ends):
        begin = jnp.where(segment > at, end, begin)
    return index - begin


def embed(steps_given, embed_width):
    half_width = embed_width // 2
    freq = jnp.exp(-math.log(10000.0) * jnp.arange(half_width, dtype=F32) / half_width)
    angle = steps_given.astype(F32)[..., None] * freq
    return jnp.concatenate([jnp.sin(angle), jnp.cos(angle)], axis=-1)


def stats(values):
    centre = jnp.mean(values, axis=-1, keepdims=True)
    centered = values - centre
    spread = jnp.mean(centered * centered, axis=-1, keepdims=True)
    scale = lax.rsqrt(spread + EPSILON)
    return centered * scale, scale


def stats_back(grad, normal, scale):
    return (
        grad
        - jnp.mean(grad, axis=-1, keepdims=True)
        - normal * jnp.mean(grad * normal, axis=-1, keepdims=True)
    ) * scale


def gelu_parts(pre):
    below = 0.5 * (1.0 + lax.erf(pre * math.sqrt(0.5)))
    density = jnp.exp(-0.5 * pre * pre) * (1.0 / math.sqrt(2.0 * math.pi))
    return pre * below, below + pre * density


def qkv_kernel(
    rows, head_size, first, ends_ref, base_ref, tokens_ref, gains_ref, shifts_ref, w_ref,
    cos_ref, sin_ref, *refs,
):
    norm_ref, query_t_ref, key_ref, key_t_ref, value_t_ref, pair_ref = refs[-6:]
    step = pl.program_id(0) + first
    block = tokens_ref.shape[0]
    seq_count = ends_ref.shape[0]
    half = head_size // 2
    values = tokens_ref[...].astype(F32)
    normal, _ = stats(values)
    chunks = block // rows

    def token_index(shape, axis):
        within = lax.broadcasted_iota(jnp.int32, shape, axis)
        index = within + base_ref[step * chunks]
        for at in range(1, chunks):
            index = jnp.where(
                within >= at * rows,
                within - at * rows + base_ref[step * chunks + at],
                index,
            )
        return index

    ends = [ends_ref[s] for s in range(seq_count)]
    seg_col = segments(ends, token_index((block, 1), 0))
    seg_row = segments(ends, token_index((1, block), 1))
    gains = gains_ref[0:1, :]
    shifts = shifts_ref[0:1, :]
    for s in range(1, seq_count + 1):
        gains = jnp.where(seg_col == s, gains_ref[s : s + 1, :], gains)
        shifts = jnp.where(seg_col == s, shifts_ref[s : s + 1, :], shifts)
    norm = (normal * gains + shifts).astype(BF16)
    norm_ref[...] = norm
    mixed = jnp.dot(norm, w_ref[...], preferred_element_type=F32)
    turned = mixed.T
    cos = cos_ref[...]
    sin = sin_ref[...]

    def turn(at):
        upper = turned[at : at + half]
        lower = turned[at + half : at + head_size]
        return jnp.concatenate(
            [upper * cos - lower * sin, lower * cos + upper * sin], axis=0
        ).astype(BF16)

    query = turn(0).astype(F32) * (float(head_size) ** -0.5)
    key = turn(head_size).astype(F32)
    value = turned[2 * head_size : 3 * head_size].astype(BF16).astype(F32)
    spare = 128 - head_size
    row_id = lax.broadcasted_iota(jnp.int32, (spare, block), 0)
    same = row_id == seg_row
    used = row_id <= seq_count
    key_tail = jnp.where(same & used, 1.0, 0.0)
    query_tail = jnp.where(used & jnp.logical_not(same), NEGATIVE, 0.0)
    query_t_ref[...] = jnp.concatenate([query, query_tail], axis=0).astype(BF16)
    key_t_ref[...] = key.astype(BF16)
    value_t_ref[...] = value.astype(BF16)
    key_ref[...] = jnp.concatenate([key, key_tail], axis=0).T.astype(BF16)
    pair_ref[...] = jnp.concatenate([value, query], axis=0).T.astype(BF16)


def attend_kernel(
    chunk, rows, place_ref, query_ref, key_ref, value_ref, out_ref, sent_ref, lse_ref, score_ref,
):
    core = place_ref[0] % 2
    count = key_ref.shape[0]
    query = query_ref[...]
    top = None
    for at in range(0, count, chunk):
        score = jnp.dot(key_ref[at : at + chunk, :], query, preferred_element_type=F32)
        score_ref[at : at + chunk, :] = score
        high = jnp.max(score, axis=0, keepdims=True)
        top = high if top is None else jnp.maximum(top, high)
    total = jnp.zeros_like(top)
    out = jnp.zeros(out_ref.shape, F32)
    for at in range(0, count, chunk):
        weight = jnp.exp(score_ref[at : at + chunk, :] - top)
        total = total + jnp.sum(weight, axis=0, keepdims=True)
        out = out + jnp.dot(
            value_ref[:, at : at + chunk],
            weight.astype(BF16),
            preferred_element_type=F32,
        )
    out = out / total
    out_ref[...] = out
    for at in range(sent_ref.shape[0]):
        sent_ref[at ^ core] = out[:, at * rows : (at + 1) * rows].astype(BF16)
    lse_ref[...] = top + jnp.log(total)


def attend_back_kernel(
    chunk, rows, head_size, place_ref, query_ref, grad_ref, out_ref, lse_ref, key_ref, key_t_ref, pair_ref,
    pair_block_ref, cos_block_ref, sin_block_ref, cos_ref, sin_ref, mixed_ref, sent_ref, key_acc, value_acc,
):
    step = pl.program_id(0)
    core = place_ref[0] % 2
    per_step = grad_ref.shape[0]
    count = key_ref.shape[0]
    block = query_ref.shape[1]
    half = head_size // 2
    scale = float(head_size) ** -0.5

    @pl.when(step == 0)
    def _():
        key_acc[...] = jnp.zeros_like(key_acc)
        value_acc[...] = jnp.zeros_like(value_acc)

    query = query_ref[...]
    grad = jnp.concatenate(
        [grad_ref[at ^ core] for at in range(per_step)], axis=1
    ).astype(F32)
    delta = jnp.sum(grad * out_ref[...], axis=0, keepdims=True)
    lse = lse_ref[...]
    grad_t = jnp.concatenate(
        [grad, jnp.zeros((128 - head_size, block), F32)], axis=0
    )
    grad_rows = grad_t.T.astype(BF16)
    grad_t = grad_t.astype(BF16)
    pair = pair_block_ref[...]
    grad_query = jnp.zeros((head_size, block), F32)
    for at in range(0, count, chunk):
        part = slice(at, at + chunk)
        score = jnp.dot(key_ref[part, :], query, preferred_element_type=F32)
        prob = jnp.exp(score - lse)
        grad_prob = jnp.dot(pair_ref[part, :], grad_t, preferred_element_type=F32)
        grad_score = (prob * (grad_prob - delta)).astype(BF16)
        grad_query = grad_query + jnp.dot(
            key_t_ref[:, part], grad_score, preferred_element_type=F32
        )
        key_acc[part, :] += jnp.dot(grad_score, pair, preferred_element_type=F32)
        value_acc[part, :] += jnp.dot(
            prob.astype(BF16), grad_rows, preferred_element_type=F32
        )

    def turn_back(values, cos, sin):
        upper = values[:half]
        lower = values[half:]
        return jnp.concatenate(
            [upper * cos + lower * sin, lower * cos - upper * sin], axis=0
        ).astype(BF16)

    at = pl.multiple_of(step * block, block)
    query_part = turn_back(
        grad_query * scale, cos_block_ref[...], sin_block_ref[...]
    )
    mixed_ref[0:head_size, pl.ds(at, block)] = query_part
    for k in range(per_step):
        sent_ref[place_ref[step * per_step + k], 0:head_size, :] = query_part[
            :, k * rows : (k + 1) * rows
        ]

    @pl.when(step == pl.num_programs(0) - 1)
    def _():
        key_part = turn_back(
            key_acc[...].T[head_size : 2 * head_size], cos_ref[...], sin_ref[...]
        )
        value_part = value_acc[...].T[:head_size].astype(BF16)
        both = jnp.concatenate([key_part, value_part], axis=0)
        mixed_ref[head_size : 3 * head_size, :] = both
        for k in range(count // rows):
            sent_ref[place_ref[k], head_size : 3 * head_size, :] = both[
                :, k * rows : (k + 1) * rows
            ]


def whole(shape):
    return pl.BlockSpec(shape, lambda i, *_: (0,) * len(shape))


def project(
    tokens, base, ends, gains, shifts, w_head, cos, sin, rows, head_size, first=0, earlier=None,
):
    width = tokens.shape[1]
    count = base.shape[0] * rows
    block = min(count, 2 * rows)
    earlier = list(earlier or ())
    grid_spec = pltpu.PrefetchScalarGridSpec(
        num_scalar_prefetch=2,
        grid=(tokens.shape[0] // block,),
        in_specs=[
            pl.BlockSpec((block, width), lambda i, *_: (i, 0)),
            whole(gains.shape),
            whole(shifts.shape),
            whole(w_head.shape),
            pl.BlockSpec((head_size // 2, block), lambda i, *_: (0, i + first)),
            pl.BlockSpec((head_size // 2, block), lambda i, *_: (0, i + first)),
        ]
        + [pl.BlockSpec(memory_space=pl.ANY)] * len(earlier),
        out_specs=[
            pl.BlockSpec((block, width), lambda i, *_: (i + first, 0)),
            pl.BlockSpec((128, block), lambda i, *_: (0, i + first)),
            pl.BlockSpec((block, 128), lambda i, *_: (i + first, 0)),
            pl.BlockSpec((head_size, block), lambda i, *_: (0, i + first)),
            pl.BlockSpec((head_size, block), lambda i, *_: (0, i + first)),
            pl.BlockSpec((block, 128), lambda i, *_: (i + first, 0)),
        ],
    )
    return pl.pallas_call(
        functools.partial(qkv_kernel, rows, head_size, first),
        grid_spec=grid_spec,
        out_shape=[
            jax.ShapeDtypeStruct((count, width), BF16),
            jax.ShapeDtypeStruct((128, count), BF16),
            jax.ShapeDtypeStruct((count, 128), BF16),
            jax.ShapeDtypeStruct((head_size, count), BF16),
            jax.ShapeDtypeStruct((head_size, count), BF16),
            jax.ShapeDtypeStruct((count, 128), BF16),
        ],
        input_output_aliases={8 + k: k for k in range(len(earlier))},
        compiler_params=pltpu.CompilerParams(vmem_limit_bytes=VMEM_BYTES),
        cost_estimate=pl.CostEstimate(
            flops=2 * tokens.shape[0] * width * 1024,
            bytes_accessed=4 * tokens.shape[0] * width,
            transcendentals=0,
        ),
        name="project_head",
    )(ends, base, tokens, gains, shifts, w_head, cos, sin, *earlier)


def project_chunks_kernel(rows, head_size, first, chunks, who_ref, ends_ref, base_ref, *refs):
    tokens = refs[:chunks]
    gains_ref, shifts_ref, own_ref, other_ref, cos_ref, sin_ref = refs[chunks : chunks + 6]
    block_ref, w_ref = refs[-2:]
    step = pl.program_id(0)
    size = own_ref.shape[0]

    @pl.when(step == 0)
    def _():
        w_ref[:, 128:] = jnp.zeros((2 * size, 128), BF16)
        shard = who_ref[1]
        own_at = pl.multiple_of(shard * size, size)
        other_at = pl.multiple_of((1 - shard) * size, size)
        width = own_ref.shape[1]
        w_ref[pl.ds(own_at, size), :width] = own_ref[...]
        w_ref[pl.ds(other_at, size), :width] = other_ref[...]

    for at in range(chunks // 2):

        @pl.when(step == at)
        def _():
            block_ref[:rows] = tokens[2 * at][...]
            block_ref[rows:] = tokens[2 * at + 1][...]

    qkv_kernel(
        rows, head_size, first, ends_ref, base_ref, block_ref, gains_ref, shifts_ref, w_ref,
        cos_ref, sin_ref, *refs[-8:-2],
    )


def project_chunks(
    who, tokens, base, ends, gains, shifts, w_own, w_other, cos, sin, head_size, first=0, earlier=None,
):
    rows, width = tokens[0].shape
    count = base.shape[0] * rows
    block = 2 * rows
    earlier = list(earlier or ())
    grid_spec = pltpu.PrefetchScalarGridSpec(
        num_scalar_prefetch=3,
        grid=(len(tokens) // 2,),
        in_specs=[whole((rows, width))] * len(tokens)
        + [
            whole(gains.shape),
            whole(shifts.shape),
            whole(w_own.shape),
            whole(w_other.shape),
            pl.BlockSpec((head_size // 2, block), lambda i, *_: (0, i + first)),
            pl.BlockSpec((head_size // 2, block), lambda i, *_: (0, i + first)),
        ]
        + [pl.BlockSpec(memory_space=pl.ANY)] * len(earlier),
        out_specs=[
            pl.BlockSpec((block, width), lambda i, *_: (i + first, 0)),
            pl.BlockSpec((128, block), lambda i, *_: (0, i + first)),
            pl.BlockSpec((block, 128), lambda i, *_: (i + first, 0)),
            pl.BlockSpec((head_size, block), lambda i, *_: (0, i + first)),
            pl.BlockSpec((head_size, block), lambda i, *_: (0, i + first)),
            pl.BlockSpec((block, 128), lambda i, *_: (i + first, 0)),
        ],
        scratch_shapes=[
            pltpu.VMEM((block, width), BF16),
            pltpu.VMEM((width, 256), BF16),
        ],
    )
    return pl.pallas_call(
        functools.partial(project_chunks_kernel, rows, head_size, first, len(tokens)),
        grid_spec=grid_spec,
        out_shape=[
            jax.ShapeDtypeStruct((count, width), BF16),
            jax.ShapeDtypeStruct((128, count), BF16),
            jax.ShapeDtypeStruct((count, 128), BF16),
            jax.ShapeDtypeStruct((head_size, count), BF16),
            jax.ShapeDtypeStruct((head_size, count), BF16),
            jax.ShapeDtypeStruct((count, 128), BF16),
        ],
        input_output_aliases={9 + len(tokens) + k: k for k in range(len(earlier))},
        compiler_params=pltpu.CompilerParams(vmem_limit_bytes=VMEM_BYTES),
        cost_estimate=pl.CostEstimate(
            flops=2 * len(tokens) * rows * width * 1024,
            bytes_accessed=4 * len(tokens) * rows * width,
            transcendentals=0,
        ),
        name="project_chunks",
    )(who, ends, base, *tokens, gains, shifts, w_own, w_other, cos, sin, *earlier)


def attend(place, query_t, key, value_t, rows):
    count = key.shape[0]
    head_size = value_t.shape[0]
    block = min(count, 2 * rows)
    chunk = min(count, 512)
    grid_spec = pltpu.PrefetchScalarGridSpec(
        num_scalar_prefetch=1,
        grid=(count // block,),
        in_specs=[
            pl.BlockSpec((128, block), lambda i, _: (0, i)),
            whole((count, 128)),
            whole((head_size, count)),
        ],
        out_specs=[
            pl.BlockSpec((head_size, block), lambda i, _: (0, i)),
            pl.BlockSpec(
                (2, head_size, rows), lambda i, place: (place[2 * i] // 2, 0, 0)
            ),
            pl.BlockSpec((1, block), lambda i, _: (0, i)),
        ],
        scratch_shapes=[pltpu.VMEM((count, block), F32)],
    )
    return pl.pallas_call(
        functools.partial(attend_kernel, chunk, rows),
        grid_spec=grid_spec,
        out_shape=[
            jax.ShapeDtypeStruct((head_size, count), F32),
            jax.ShapeDtypeStruct((count // rows, head_size, rows), BF16),
            jax.ShapeDtypeStruct((1, count), F32),
        ],
        compiler_params=pltpu.CompilerParams(vmem_limit_bytes=VMEM_BYTES),
        cost_estimate=pl.CostEstimate(
            flops=8 * count * count * 128,
            bytes_accessed=8 * count * 128,
            transcendentals=count * count,
        ),
        name="attend_head",
    )(place, query_t, key, value_t)


def attend_back(place, query_t, grad, out, lse, key, key_t, pair, cos, sin, rows):
    count = key.shape[0]
    head_size = key_t.shape[0]
    half = head_size // 2
    block = min(count, 2 * rows)
    chunk = min(count, 512)
    grid_spec = pltpu.PrefetchScalarGridSpec(
        num_scalar_prefetch=1,
        grid=(count // block,),
        in_specs=[
            pl.BlockSpec((128, block), lambda i, _: (0, i)),
            pl.BlockSpec(
                (2, head_size, rows), lambda i, place: (place[2 * i] // 2, 0, 0)
            ),
            pl.BlockSpec((head_size, block), lambda i, _: (0, i)),
            pl.BlockSpec((1, block), lambda i, _: (0, i)),
            whole((count, 128)),
            whole((head_size, count)),
            whole((count, 128)),
            pl.BlockSpec((block, 128), lambda i, _: (i, 0)),
            pl.BlockSpec((half, block), lambda i, _: (0, i)),
            pl.BlockSpec((half, block), lambda i, _: (0, i)),
            whole((half, count)),
            whole((half, count)),
        ],
        out_specs=[
            whole((3 * head_size, count)),
            whole((count // rows, 3 * head_size, rows)),
        ],
        scratch_shapes=[pltpu.VMEM((count, 128), F32), pltpu.VMEM((count, 128), F32)],
    )
    return pl.pallas_call(
        functools.partial(attend_back_kernel, chunk, rows, head_size),
        grid_spec=grid_spec,
        out_shape=[
            jax.ShapeDtypeStruct((3 * head_size, count), BF16),
            jax.ShapeDtypeStruct((count // rows, 3 * head_size, rows), BF16),
        ],
        compiler_params=pltpu.CompilerParams(vmem_limit_bytes=VMEM_BYTES),
        cost_estimate=pl.CostEstimate(
            flops=20 * count * count * 128,
            bytes_accessed=16 * count * 128,
            transcendentals=count * count,
        ),
        name="attend_head_back",
    )(place, query_t, grad, out, lse, key, key_t, pair, pair, cos, sin, cos, sin)


def slices_kernel(
    who_ref, norm_ref, grad_ref, up_own, up_other, down_own, down_other, bias_ref, keep_ref,
    give_ref, down_w, down_acc, up_acc, up_t,
):
    step = pl.program_id(0)
    shard = who_ref[1]
    size, units = up_own.shape
    width = 2 * size
    half = units // 2
    own_at = pl.multiple_of(shard * size, size)
    other_at = pl.multiple_of((1 - shard) * size, size)

    @pl.when(step == 0)
    def _():
        down_w[:half] = down_own[...]
        down_w[half:] = down_other[...]
        down_acc[...] = jnp.zeros_like(down_acc)
        up_acc[...] = jnp.zeros_like(up_acc)

    pre = jnp.dot(
        norm_ref[:, pl.ds(own_at, size)], up_own[...], preferred_element_type=F32
    )
    pre = pre + jnp.dot(
        norm_ref[:, pl.ds(other_at, size)], up_other[...], preferred_element_type=F32
    )
    act, slope = gelu_parts(pre + bias_ref[...])
    grad_y = grad_ref[...]
    grad = dims(grad_y, down_w[...], 1, 1) * slope
    down_acc[...] += jnp.dot(act.T.astype(BF16), grad_y, preferred_element_type=F32)
    up_acc[...] += jnp.dot(
        grad.T.astype(BF16), norm_ref[...], preferred_element_type=F32
    )

    @pl.when(step == pl.num_programs(0) - 1)
    def _():
        up_t[...] = up_acc[...].T
        for at, (rows, out_ref) in enumerate(((own_at, keep_ref), (other_at, give_ref))):
            values = up_t[pl.ds(rows, size), :].astype(out_ref.dtype)
            out_ref[pl.ds(own_at, size), :] = values[:, :half]
            out_ref[pl.ds(other_at, size), :] = values[:, half:]
            for k in range(width // half):
                out_ref[width + k * half : width + (k + 1) * half, :] = down_acc[
                    at * half : (at + 1) * half, k * half : (k + 1) * half
                ].astype(out_ref.dtype)


def slices(
    who, norm, grad_y, up_own, up_other, down_own, down_other, bias,
):
    count, width = norm.shape
    size, units = up_own.shape
    block = 256
    tall = 2 * width
    token = pl.BlockSpec((block, width), lambda i: (i, 0))
    return pl.pallas_call(
        slices_kernel,
        grid=(count // block,),
        in_specs=[pl.BlockSpec(memory_space=pltpu.SMEM), token, token]
        + [
            pl.BlockSpec(v.shape, lambda i: (0, 0))
            for v in (up_own, up_other, down_own, down_other, bias)
        ],
        out_specs=[pl.BlockSpec((tall, units // 2), lambda i: (0, 0))] * 2,
        out_shape=[
            jax.ShapeDtypeStruct((tall, units // 2), F32),
            jax.ShapeDtypeStruct((tall, units // 2), BF16),
        ],
        scratch_shapes=[
            pltpu.VMEM((units, width), BF16),
            pltpu.VMEM((units, width), F32),
            pltpu.VMEM((units, width), F32),
            pltpu.VMEM((width, units), F32),
        ],
        compiler_params=pltpu.CompilerParams(vmem_limit_bytes=VMEM_BYTES),
        cost_estimate=pl.CostEstimate(
            flops=8 * count * width * units,
            bytes_accessed=6 * count * width,
            transcendentals=2 * count * units,
        ),
        name="weight_slices",
    )(
        who, norm, grad_y, up_own, up_other, down_own, down_other, bias
    )


def head_of(device, devices):
    return device % 2 * (devices // 2) + device // 2


def row_starts(who_ref, size):
    core = who_ref[0] % 2
    shard = who_ref[1]
    half = size // 2
    other = (1 - shard) * size
    return (
        pl.multiple_of(shard * size, size),
        pl.multiple_of(other + core * half, half),
        pl.multiple_of(other + (1 - core) * half, half),
    )


def middle_kernel(
    who_ref, att_ref, own_ref, mine_ref, flip_ref, tokens_ref, gain_ref, bias_ref,
    resid_ref, normal_ref, scale_ref, norm_ref, turned,
):
    devices, head_size, _ = att_ref.shape
    for d in range(devices):
        at = head_of(d, devices) * head_size
        turned[:, at : at + head_size] = att_ref[d].astype(F32).T.astype(BF16)
    resid = tokens_ref[...].astype(F32)
    pieces = (own_ref, mine_ref, flip_ref)
    for at, piece in zip(row_starts(who_ref, own_ref.shape[0]), pieces):
        resid = resid + jnp.dot(
            turned[:, pl.ds(at, piece.shape[0])],
            piece[...],
            preferred_element_type=F32,
        )
    resid_ref[...] = resid
    normal, scale = stats(resid)
    normal_ref[...] = normal
    scale_ref[...] = scale
    norm_ref[...] = (normal * gain_ref[...] + bias_ref[...]).astype(BF16)


def middle(who, attended, pieces, tokens, gain, bias):
    rows, width = tokens.shape
    vmem = pl.BlockSpec(memory_space=pltpu.VMEM)
    return pl.pallas_call(
        middle_kernel,
        in_specs=[pl.BlockSpec(memory_space=pltpu.SMEM)] + [vmem] * 7,
        out_specs=[vmem] * 4,
        out_shape=[
            jax.ShapeDtypeStruct((rows, width), F32),
            jax.ShapeDtypeStruct((rows, width), F32),
            jax.ShapeDtypeStruct((rows, 1), F32),
            jax.ShapeDtypeStruct((rows, width), BF16),
        ],
        scratch_shapes=[pltpu.VMEM((rows, width), BF16)],
        compiler_params=pltpu.CompilerParams(vmem_limit_bytes=VMEM_BYTES),
        cost_estimate=pl.CostEstimate(
            flops=8 * rows * width * width,
            bytes_accessed=4 * width * width,
            transcendentals=0,
        ),
        name="output_projection",
    )(who, attended, *pieces, tokens, gain, bias)


def feed_kernel(parts, who_ref, norm_ref, own_ref, *refs):
    pieces = refs[: 4 * parts]
    (
        near_ref, far_ref, bias_ref, normal_ref, scale_ref, gain_ref, grad_y_ref, out_own, out_mine,
        out_flip, act_ref, resid_ref, resid_b_ref, sent_ref, sums_ref, grad_ref, att_ref,
    ) = refs[4 * parts :]
    side = who_ref[0] % 4
    shard = who_ref[1]
    size, hidden = own_ref.shape
    quarter = hidden // 4
    deep = size // parts
    own_at = pl.multiple_of(shard * size, size)
    other_at = pl.multiple_of((1 - shard) * size, size)
    own_norm = norm_ref[:, pl.ds(own_at, size)]
    part_at = [pl.multiple_of(other_at + p * deep, deep) for p in range(parts)]
    norms = [norm_ref[:, pl.ds(at, deep)] for at in part_at]
    for k in range(4):
        block = side ^ k
        columns = pl.ds(pl.multiple_of(block * quarter, quarter), quarter)
        weight = own_ref[:, columns]
        pre = jnp.dot(own_norm, weight, preferred_element_type=F32)
        for p in range(parts):
            pre = pre + jnp.dot(
                norms[p], pieces[4 * p + k][...], preferred_element_type=F32
            )
        act, slope = gelu_parts(pre + bias_ref[:, columns])
        act_ref[:, columns] = act.astype(BF16)
        within = pl.ds(pl.multiple_of((block % 2) * quarter, quarter), quarter)
        near = near_ref[:, within]
        far = far_ref[:, within].astype(F32)
        grad = jnp.where(block // 2 == shard, near, far) * slope
        sums_ref[pl.ds(3 + block, 1), :] = jnp.sum(grad, axis=0, keepdims=True)
        grad = grad.astype(BF16)
        terms = [(own_at, size, weight)]
        terms += [(part_at[p], deep, pieces[4 * p + k][...]) for p in range(parts)]
        for at, length, piece in terms:
            term = dims(grad, piece, 1, 1)
            if k == 0:
                grad_ref[:, pl.ds(at, length)] = term
            else:
                grad_ref[:, pl.ds(at, length)] += term
    grad = grad_ref[...]
    normal = normal_ref[...]
    grad_y = grad_y_ref[...].astype(F32)
    sums_ref[0:1, :] = jnp.sum(grad * normal, axis=0, keepdims=True)
    sums_ref[1:2, :] = jnp.sum(grad, axis=0, keepdims=True)
    sums_ref[2:3, :] = jnp.sum(grad_y, axis=0, keepdims=True)
    sums_ref[7:8, :] = jnp.zeros((1, quarter), F32)
    resid = grad_y + stats_back(grad * gain_ref[...], normal, scale_ref[...])
    resid_ref[...] = resid
    resid = resid.astype(BF16)
    resid_b_ref[...] = resid
    out_pieces = (out_own, out_mine, out_flip)
    for at, piece in zip(row_starts(who_ref, out_own.shape[0]), out_pieces):
        att_ref[pl.ds(at, piece.shape[0]), :] = dims(piece[...], resid, 1, 1).astype(
            BF16
        )
    devices, head_size, _ = sent_ref.shape
    for d in range(devices):
        at = head_of(d, devices) * head_size
        sent_ref[d] = att_ref[at : at + head_size, :]


def feed(who, norm, own, pieces, near, far, bias, normal, scale, gain, grad_y, out_pieces):
    rows, width = norm.shape
    hidden = own.shape[1]
    vmem = pl.BlockSpec(memory_space=pltpu.VMEM)
    return pl.pallas_call(
        functools.partial(feed_kernel, len(pieces) // 4),
        in_specs=[pl.BlockSpec(memory_space=pltpu.SMEM)] + [vmem] * (12 + len(pieces)),
        out_specs=[vmem] * 5,
        out_shape=[
            jax.ShapeDtypeStruct((rows, hidden), BF16),
            jax.ShapeDtypeStruct((rows, width), F32),
            jax.ShapeDtypeStruct((rows, width), BF16),
            jax.ShapeDtypeStruct((HEADS, width // HEADS, rows), BF16),
            jax.ShapeDtypeStruct((8, width), F32),
        ],
        scratch_shapes=[pltpu.VMEM((rows, width), F32), pltpu.VMEM((width, rows), BF16)],
        compiler_params=pltpu.CompilerParams(vmem_limit_bytes=VMEM_BYTES),
        cost_estimate=pl.CostEstimate(
            flops=16 * rows * width * hidden,
            bytes_accessed=4 * width * hidden,
            transcendentals=2 * rows * hidden,
        ),
        name="feed_forward",
    )(who, norm, own, *pieces, near, far, bias, normal, scale, gain, grad_y, *out_pieces)


def first_back_kernel(
    head_size, who_ref, ends_ref, got_ref, own_ref, mine_0, mine_1, flip_0, flip_1, tokens_ref,
    resid_ref, gains_ref, sums_ref, grad_ref, total_ref, mixed, turned,
):
    heads = got_ref.shape[0]
    rows, width = tokens_ref.shape
    seq_count = ends_ref.shape[0]
    for d in range(heads):
        for k in range(3):
            at = k * width + head_of(d, heads) * head_size
            mixed[at : at + head_size, :] = got_ref[
                d, k * head_size : (k + 1) * head_size, :
            ]
    own_at, mine_at, flip_at = row_starts(who_ref, own_ref.shape[0])
    part = mine_0.shape[0]
    starts = (own_at, mine_at, mine_at + part, flip_at, flip_at + part)
    for at, piece in zip(starts, (own_ref, mine_0, mine_1, flip_0, flip_1)):
        turned[pl.ds(at, piece.shape[0]), :] = jnp.dot(
            piece[...], mixed[...], preferred_element_type=F32
        )
    grad = turned[...].T
    normal, scale = stats(tokens_ref[...].astype(F32))
    index = who_ref[0] * rows + lax.broadcasted_iota(jnp.int32, (rows, 1), 0)
    segment = segments([ends_ref[s] for s in range(seq_count)], index)
    gains = gains_ref[0:1, :]
    for s in range(1, seq_count + 1):
        gains = jnp.where(segment == s, gains_ref[s : s + 1, :], gains)
    grad_ref[...] = (
        resid_ref[...] + stats_back(grad * gains, normal, scale)
    ).astype(BF16)
    total_ref[0:8, :] = sums_ref[...]
    product = grad * normal
    for s in range(seq_count + 1):
        here = segment == s
        for k, terms in enumerate((product, grad)):
            total_ref[8 + 2 * s + k : 9 + 2 * s + k, :] = jnp.sum(
                jnp.where(here, terms, 0.0), axis=0, keepdims=True
            )


def first_back(who, ends, got, pieces, tokens, resid, gains, sums):
    rows, width = tokens.shape
    heads, tall, _ = got.shape
    seq_count = ends.shape[0]
    lines = 8 + 2 * (seq_count + 1)
    vmem = pl.BlockSpec(memory_space=pltpu.VMEM)
    return pl.pallas_call(
        functools.partial(first_back_kernel, tall // 3),
        in_specs=[pl.BlockSpec(memory_space=pltpu.SMEM)] * 2 + [vmem] * 10,
        out_specs=[vmem] * 2,
        out_shape=[
            jax.ShapeDtypeStruct((rows, width), BF16),
            jax.ShapeDtypeStruct((lines, width), F32),
        ],
        scratch_shapes=[
            pltpu.VMEM((3 * width, rows), BF16),
            pltpu.VMEM((width, rows), F32),
        ],
        compiler_params=pltpu.CompilerParams(vmem_limit_bytes=VMEM_BYTES),
        cost_estimate=pl.CostEstimate(
            flops=12 * rows * width * width,
            bytes_accessed=8 * width * width,
            transcendentals=0,
        ),
        name="first_norm_back",
    )(who, ends, got, *pieces, tokens, resid, gains, sums)


def small_kernel(seq_count, chunks, who_ref, own_embed, other_embed, *refs):
    parts = refs[:chunks]
    (
        time_ref, gain_one, bias_one, gain_two, bias_two, bias_up, bias_down, total,
    ) = refs[chunks:]
    lines, width = total.shape
    half = width // 2
    shard = who_ref[1]
    for k in range(width // 128):
        at = k * lines
        value = parts[0][at : at + lines, :].astype(F32)
        for ref in parts[1:]:
            value = value + ref[at : at + lines, :].astype(F32)
        total[:, k * 128 : (k + 1) * 128] = value
    part = pl.ds(pl.multiple_of(shard * half, half), half)
    gain_two[...] = total[0:1, part]
    bias_two[...] = total[1:2, part]
    bias_down[...] = total[2:3, part]
    bias_up[:, :width] = total[pl.ds(3 + 2 * shard, 1), :]
    bias_up[:, width:] = total[pl.ds(4 + 2 * shard, 1), :]
    films = 2 * (seq_count + 1)
    gain = total[8:9, part]
    bias = total[9:10, part]
    for s in range(1, films):
        gain = gain + total[8 + 2 * s : 9 + 2 * s, part]
        bias = bias + total[9 + 2 * s : 10 + 2 * s, part]
    gain_one[...] = gain
    bias_one[...] = bias
    embeds = []
    for embed_ref in (own_embed, other_embed):
        columns = []
        for s in range(seq_count):
            line = embed_ref[s : s + 1, :]
            columns.append(jnp.broadcast_to(line, (8, line.shape[1])).T[:, 0:1])
        embeds.append(columns)
    for k in range(2):
        value = None
        for g, columns in enumerate(embeds):
            for s in range(seq_count):
                line = 8 + g * films + 2 * s + k
                term = columns[s] * total[line : line + 1, :]
                value = term if value is None else value + term
        time_ref[:, k * width : (k + 1) * width] = value


def small_sums(who, own_embed, other_embed, parts, top, lines, width):
    vmem = pl.BlockSpec(memory_space=pltpu.VMEM)
    tall = lines * width // 128
    tail = pl.BlockSpec((tall, 128), lambda i: (top // tall, 0))
    return pl.pallas_call(
        functools.partial(small_kernel, own_embed.shape[0], len(parts)),
        grid=(1,),
        in_specs=[pl.BlockSpec(memory_space=pltpu.SMEM)]
        + [vmem] * 2
        + [tail] * len(parts),
        out_specs=[vmem] * 7,
        out_shape=[jax.ShapeDtypeStruct((own_embed.shape[1], 2 * width), F32)]
        + [jax.ShapeDtypeStruct((1, width // 2), F32)] * 4
        + [
            jax.ShapeDtypeStruct((1, 2 * width), F32),
            jax.ShapeDtypeStruct((1, width // 2), F32),
        ],
        scratch_shapes=[pltpu.VMEM((lines, width), F32)],
        compiler_params=pltpu.CompilerParams(vmem_limit_bytes=VMEM_BYTES),
        cost_estimate=pl.CostEstimate(
            flops=1000000, bytes_accessed=2000000, transcendentals=0
        ),
        name="small_gradients",
    )(who, own_embed, other_embed, *parts)


def stream(chips, copies_of, fill):
    pending = [None, None]
    for at in range(chips):
        slot = at % 2
        if pending[slot] is not None:
            for copy in pending[slot]:
                copy.wait()
        fill(at, slot)
        pending[slot] = copies_of(at, slot)
        for copy in pending[slot]:
            copy.start()
    for copies in pending:
        if copies is not None:
            for copy in copies:
                copy.wait()


def wide_kernel(first, chunks, place_ref, *refs):
    parts = refs[:chunks]
    up_ref, down_ref, out_ref, up_slots, down_slots, out_slots, sems = refs[-7:]
    core = place_ref[0] % 2
    deep = out_slots.shape[1] // 2
    size = up_ref.shape[0]
    hidden = up_ref.shape[1]
    width = down_ref.shape[1]

    def fill(at, slot):
        for j in range(2):
            ref = parts[2 * at + j]
            column = pl.ds(pl.multiple_of((j ^ core) * 128, 128), 128)
            for k in range(2):
                up_slots[slot, k, :, column] = ref[k * size : (k + 1) * size, :].astype(
                    F32
                )
            row = pl.ds(pl.multiple_of((j ^ core) * 128, 128), 128)
            for k in range(width // 128):
                top = 2 * size + k * 128
                down_slots[slot, row, k * 128 : (k + 1) * 128] = ref[
                    top : top + 128, :
                ].astype(F32)
            row = pl.ds(pl.multiple_of((j ^ core) * deep, deep), deep)
            for k in range(width // 128):
                top = 2 * size + width + k * deep
                out_slots[slot, row, k * 128 : (k + 1) * 128] = ref[
                    top : top + deep, :
                ].astype(F32)

    def copies_of(at, slot):
        chip = place_ref[2 * (at + first)] // 2
        copies = []
        for k in range(2):
            column = pl.multiple_of(k * (hidden // 2) + chip * 256, 256)
            copies.append(
                pltpu.make_async_copy(
                    up_slots.at[slot, k],
                    up_ref.at[:, pl.ds(column, 256)],
                    sems.at[slot, k],
                )
            )
        row = pl.multiple_of(chip * 256, 256)
        copies.append(
            pltpu.make_async_copy(
                down_slots.at[slot], down_ref.at[pl.ds(row, 256), :], sems.at[slot, 2]
            )
        )
        row = pl.multiple_of(chip * 2 * deep, 2 * deep)
        copies.append(
            pltpu.make_async_copy(
                out_slots.at[slot], out_ref.at[pl.ds(row, 2 * deep), :], sems.at[slot, 3]
            )
        )
        return copies

    stream(chunks // 2, copies_of, fill)


def expand_wide(place, first, parts, width, earlier):
    devices = place.shape[0]
    size = width // 2
    vmem = pl.BlockSpec(memory_space=pltpu.VMEM)
    hbm = pl.BlockSpec(memory_space=pl.ANY)
    return pl.pallas_call(
        functools.partial(wide_kernel, first, len(parts)),
        in_specs=[pl.BlockSpec(memory_space=pltpu.SMEM)]
        + [vmem] * len(parts)
        + [hbm] * len(earlier),
        out_specs=[hbm, hbm, hbm],
        out_shape=[
            jax.ShapeDtypeStruct((size, 2 * devices * 128), F32),
            jax.ShapeDtypeStruct((devices * 128, width), F32),
            jax.ShapeDtypeStruct((size, width), F32),
        ],
        scratch_shapes=[
            pltpu.VMEM((2, 2, size, 256), F32),
            pltpu.VMEM((2, 256, width), F32),
            pltpu.VMEM((2, 2 * size // devices, width), F32),
            pltpu.SemaphoreType.DMA((2, 4)),
        ],
        input_output_aliases={1 + len(parts) + k: k for k in range(len(earlier))},
        compiler_params=pltpu.CompilerParams(vmem_limit_bytes=VMEM_BYTES),
        cost_estimate=pl.CostEstimate(
            flops=parts[0].size * len(parts),
            bytes_accessed=6 * parts[0].size * len(parts),
            transcendentals=0,
        ),
        name="expand_wide",
    )(place, *parts, *earlier)


def last_kernel(head_size, in_ref, out_ref):
    pairs = []
    for j in range(2):
        for k in range(in_ref.shape[0] // 4):
            pairs.append((in_ref[4 * k + j], in_ref[4 * k + 2 + j]))
    for at, (first, second) in enumerate(pairs):
        both = jnp.concatenate([first, second], axis=0).astype(F32)
        out_ref[:, at * 2 * head_size : (at + 1) * 2 * head_size] = both.T


def expand_last(parts, head_size):
    devices, tall, depth = parts.shape
    width = devices * head_size
    return pl.pallas_call(
        functools.partial(last_kernel, head_size),
        grid=(3,),
        in_specs=[pl.BlockSpec((devices, head_size, depth), lambda k: (0, k, 0))],
        out_specs=pl.BlockSpec((depth, width), lambda k: (0, k)),
        out_shape=jax.ShapeDtypeStruct((depth, 3 * width), F32),
        compiler_params=pltpu.CompilerParams(vmem_limit_bytes=VMEM_BYTES),
        cost_estimate=pl.CostEstimate(
            flops=parts.size, bytes_accessed=6 * parts.size, transcendentals=0
        ),
        name="expand_last",
    )(parts)


def times_rows(values, pieces):
    return sum(
        jnp.dot(
            lax.dynamic_slice_in_dim(values, at, piece.shape[0], 1),
            piece,
            preferred_element_type=F32,
        )
        for piece, at in pieces
    )


def times_rows_t(values_t, pieces):
    return sum(
        dims(lax.dynamic_slice_in_dim(values_t, at, piece.shape[0], 0), piece, 0, 0)
        for piece, at in pieces
    )


def joined(parts, pieces, dim):
    if len(parts) == 1:
        return parts[0]
    shape = list(parts[0].shape)
    shape[dim] = sum(part.shape[dim] for part in parts)
    out = jnp.zeros(shape, parts[0].dtype)
    for part, (_, at) in zip(parts, pieces):
        out = lax.dynamic_update_slice_in_dim(out, part, at, dim)
    return out


def rows_of(pieces, start, size):
    out = None
    for piece, at in pieces:
        length = piece.shape[0]
        local = jnp.clip(start - at, 0, length - size)
        found = lax.dynamic_slice_in_dim(piece, local, size, 0)
        inside = (start >= at) & (start < at + length)
        out = found if out is None else jnp.where(inside, found, out)
    return out


def body_general(
    ctx_size, fsdp_size,
    tokens, w_qkv, w_out, w_up, w_down, w_time, gain_one, bias_one, gain_two, bias_two, bias_up,
    bias_down, lengths, time_steps, cotangent,
):
    me = lax.axis_index("ctx")
    shard = lax.axis_index("fsdp")
    rows = tokens.shape[1]
    width = tokens.shape[2]
    count = rows * ctx_size
    head_size = width // HEADS
    repeats = ctx_size // HEADS
    columns = head_size // repeats
    seq_count = lengths.shape[1]
    hidden = w_up.shape[1]

    def gather_small(values):
        return lax.all_gather(values, "fsdp", axis=0, tiled=True)

    def fetch(weight):
        return [(gather_small(weight), 0)]

    def scatter_sum(values, dim):
        return lax.psum_scatter(
            values.astype(BF16), "fsdp", scatter_dimension=dim, tiled=True
        )

    def gather(values):
        return lax.all_gather(values, "ctx", axis=0, tiled=False)

    ends = []
    for s in range(seq_count):
        ends.append(lengths[0, s] + (ends[-1] if ends else 0))
    ends_vector = jnp.stack(ends)
    index = me * rows + jnp.arange(rows, dtype=jnp.int32)
    segment = segments(ends, index)
    live = (segment < seq_count).astype(F32)[:, None]
    all_index = jnp.arange(count, dtype=jnp.int32)
    all_position = positions(ends, all_index, segments(ends, all_index))
    half_width = head_size // 2
    inverse = jnp.exp(
        -math.log(10000.0) * jnp.arange(half_width, dtype=F32) / half_width
    )
    angle = inverse[:, None] * all_position.astype(F32)[None, :]
    cos = jnp.cos(angle)
    sin = jnp.sin(angle)

    all_tokens = gather(tokens[0]).reshape(count, width)
    inputs = tokens[0].astype(F32)
    grad_y = cotangent[0].astype(F32) * live
    grad_y_b = grad_y.astype(BF16)
    all_grad_y = gather(grad_y_b).reshape(count, width)

    small = [gain_one, bias_one, gain_two, bias_two, bias_down, bias_up]
    packed = gather_small(jnp.concatenate(small)[None, :])
    vectors = []
    at = 0
    for vector in small:
        size = vector.shape[0]
        vectors.append(packed[:, at : at + size].reshape(1, -1).astype(F32))
        at += size
    gain_first, bias_first, gain_second, bias_second, bias_output, bias_hidden = vectors

    all_steps = lax.all_gather(time_steps.astype(F32), "fsdp", axis=0, tiled=True)
    all_embedded = embed(all_steps, w_time.shape[0] * fsdp_size).astype(BF16)
    embedded = lax.dynamic_index_in_dim(all_embedded, shard, 0, keepdims=False)
    film = times_rows(embedded, fetch(w_time))
    film = jnp.concatenate([film, jnp.zeros((1, 2 * width), F32)], axis=0)
    gains = gain_first + film[:, :width]
    shifts = bias_first + film[:, width:]

    head = me // repeats
    w_head = jnp.concatenate(
        [
            lax.dynamic_slice_in_dim(w_qkv, k * width + head * head_size, head_size, 1)
            for k in range(3)
        ]
        + [jnp.zeros((w_qkv.shape[0], head_size), BF16)],
        axis=1,
    )
    w_head = gather_small(w_head)

    base = jnp.arange(ctx_size, dtype=jnp.int32) * rows
    all_norm, query_t, key, key_t, value_t, pair = project(
        all_tokens, base, ends_vector, gains, shifts, w_head, cos, sin, rows, head_size
    )
    place = jnp.arange(ctx_size, dtype=jnp.int32)
    out_t, sent, lse = attend(place, query_t, key, value_t, rows)

    part = (me % repeats) * columns
    if repeats > 1:
        sent = lax.dynamic_slice_in_dim(sent, part, columns, 1)
    attended_t = lax.all_to_all(sent, "ctx", 0, 0, tiled=True).reshape(width, rows)

    out_pieces = fetch(w_out)
    up_pieces = fetch(w_up)
    down_pieces = fetch(w_down)
    qkv_pieces = fetch(w_qkv)
    resid = inputs + times_rows_t(attended_t, out_pieces)
    normal_two, scale_two = stats(resid)
    norm_two_b = (normal_two * gain_second + bias_second).astype(BF16)
    all_norm_two = gather(norm_two_b).reshape(count, width)
    pre = times_rows(norm_two_b, up_pieces) + bias_hidden
    act, slope = gelu_parts(pre)
    branch = times_rows(act.astype(BF16), down_pieces) + bias_output
    output = (live * (resid + branch)).astype(BF16)
    grad_act = joined([dims(grad_y_b, p, 1, 1) for p, _ in down_pieces], down_pieces, 1)
    grad_pre = grad_act * slope
    grad_bias_up = jnp.sum(grad_pre, axis=0)
    grad_pre_b = grad_pre.astype(BF16)
    grad_norm_two = joined([dims(grad_pre_b, p, 1, 1) for p, _ in up_pieces], up_pieces, 1)
    grad_resid = grad_y + stats_back(grad_norm_two * gain_second, normal_two, scale_two)
    grad_resid_b = grad_resid.astype(BF16)
    grad_att_t = joined(
        [dims(p, grad_resid_b, 1, 1) for p, _ in out_pieces], out_pieces, 0
    ).astype(BF16)
    grad_att_t = grad_att_t.reshape(HEADS, head_size, rows)
    if repeats > 1:
        grad_att_t = jnp.repeat(grad_att_t, repeats, axis=0)
    grad_att = lax.all_to_all(grad_att_t, "ctx", 0, 0, tiled=True)

    mixed_t, _ = attend_back(
        place, query_t, grad_att, out_t, lse, key, key_t, pair, cos, sin, rows
    )
    mixed_t = mixed_t.reshape(3, head_size, count)
    if repeats > 1:
        mixed_t = lax.dynamic_slice_in_dim(mixed_t, part, columns, 1)
    mixed_t = mixed_t.reshape(3 * columns, count)
    mixed_sent = mixed_t.reshape(3 * columns, ctx_size, rows).transpose(1, 0, 2)
    mixed_got = lax.all_to_all(mixed_sent, "ctx", 0, 0, tiled=True)
    grad_mixed_t = (
        mixed_got.reshape(ctx_size, 3, columns, rows)
        .transpose(1, 0, 2, 3)
        .reshape(3 * width, rows)
    )
    grad_norm_one = joined(
        [dims(grad_mixed_t, p, 0, 1) for p, _ in qkv_pieces], qkv_pieces, 1
    )
    normal_one, scale_one = stats(inputs)
    seg_col = segment[:, None]
    gain_tok = gains[0:1]
    for s in range(1, seq_count + 1):
        gain_tok = jnp.where(seg_col == s, gains[s : s + 1], gain_tok)
    grad_tokens = (
        grad_resid + stats_back(grad_norm_one * gain_tok, normal_one, scale_one)
    ).astype(BF16)
    film_terms = jnp.concatenate([grad_norm_one * normal_one, grad_norm_one], axis=1)
    film_sums = [
        jnp.sum(jnp.where(seg_col == s, film_terms, 0.0), axis=0)
        for s in range(seq_count + 1)
    ]

    sums = [
        jnp.sum(grad_norm_two * normal_two, axis=0),
        jnp.sum(grad_norm_two, axis=0),
        jnp.sum(grad_y, axis=0),
        grad_bias_up,
    ] + film_sums
    sizes = [vector.shape[0] for vector in sums]
    total = lax.psum(jnp.concatenate(sums)[None, :], "ctx")
    total = lax.all_gather(total, "fsdp", axis=0, tiled=True)
    split = []
    at = 0
    for size in sizes:
        split.append(total[:, at : at + size])
        at += size

    def own(vector):
        size = vector.shape[0] // fsdp_size
        return lax.dynamic_slice_in_dim(vector, shard * size, size, 0)

    sum_gain_two, sum_bias_two, sum_bias_down, sum_bias_up = (
        own(jnp.sum(vector, axis=0)) for vector in split[:4]
    )
    film_all = jnp.sum(sum(split[4:]), axis=0)
    sum_gain_one = own(film_all[:width])
    sum_bias_one = own(film_all[width:])
    film_grad = jnp.stack(split[4 : 4 + seq_count], axis=1).reshape(-1, 2 * width)
    embedded_rows = lax.dynamic_slice_in_dim(
        all_embedded.astype(F32).reshape(film_grad.shape[0], -1),
        shard * w_time.shape[0],
        w_time.shape[0],
        1,
    )
    grad_time = sum(
        embedded_rows[g][:, None] * film_grad[g][None, :]
        for g in range(film_grad.shape[0])
    )

    slice_width = hidden // (ctx_size * fsdp_size)
    starts = [
        k * (hidden // fsdp_size) + me * slice_width for k in range(fsdp_size)
    ]
    w_up_cols = []
    for piece, _ in up_pieces:
        w_up_cols.append(
            jnp.concatenate(
                [
                    lax.dynamic_slice_in_dim(piece, start, slice_width, 1)
                    for start in starts
                ],
                axis=1,
            )
        )
    w_up_slice = joined(w_up_cols, up_pieces, 0)
    w_down_slice = jnp.concatenate(
        [rows_of(down_pieces, start, slice_width) for start in starts], axis=0
    )
    bias_slice = jnp.concatenate(
        [
            lax.dynamic_slice_in_dim(bias_hidden, start, slice_width, 1)
            for start in starts
        ],
        axis=1,
    )
    pre_slice = dims(all_norm_two, w_up_slice, 1, 0) + bias_slice
    act_slice, slope_slice = gelu_parts(pre_slice)
    grad_pre_slice = (dims(all_grad_y, w_down_slice, 1, 1) * slope_slice).astype(BF16)
    down_slice = dims(act_slice.astype(BF16), all_grad_y, 0, 0)
    up_slice = dims(all_norm_two, grad_pre_slice, 0, 0)
    grad_down = gather(scatter_sum(down_slice, 0)).reshape(-1, width).astype(F32)
    up_parts = gather(scatter_sum(up_slice, 0))
    grad_up = (
        up_parts.reshape(ctx_size, width // fsdp_size, fsdp_size, slice_width)
        .transpose(1, 2, 0, 3)
        .reshape(width // fsdp_size, hidden)
        .astype(F32)
    )
    out_part = jnp.dot(attended_t, grad_resid_b, preferred_element_type=F32)
    out_rows = lax.psum_scatter(
        out_part.astype(BF16), ("fsdp", "ctx"), scatter_dimension=0, tiled=True
    )
    grad_out = gather(out_rows).reshape(-1, width).astype(F32)
    qkv_slice = jnp.dot(mixed_t, all_norm, preferred_element_type=F32)
    qkv_parts = gather(scatter_sum(qkv_slice, 1))
    grad_qkv = (
        qkv_parts.reshape(ctx_size, 3, columns, width // fsdp_size)
        .transpose(3, 1, 0, 2)
        .reshape(width // fsdp_size, 3 * width)
        .astype(F32)
    )
    return (
        output[None],
        grad_tokens[None],
        grad_qkv,
        grad_out,
        grad_up,
        grad_down,
        grad_time,
        sum_gain_one,
        sum_bias_one,
        sum_gain_two,
        sum_bias_two,
        sum_bias_up,
        sum_bias_down,
    )


def ring_tables(ctx_size):
    chips = ctx_size // 2
    order = list(range(0, chips, 2)) + list(range(1, chips, 2))[::-1]
    offsets = [0]
    for step in range(1, chips // 2 + 1):
        offsets.append(-step)
        if step <= (chips - 1) // 2:
            offsets.append(step)
    place = np.zeros((ctx_size, ctx_size), np.int32)
    for me in range(ctx_size):
        at = order.index(me // 2)
        for k, offset in enumerate(offsets):
            chip = order[(at + offset) % chips]
            place[me, 2 * k] = 2 * chip + me % 2
            place[me, 2 * k + 1] = 2 * chip + 1 - me % 2
    return order, place


def fence(*values):
    return lax.optimization_barrier(values)


def after(values, *earlier):
    return lax.optimization_barrier((values, *earlier))[0]


def body(
    ctx_size, fsdp_size,
    tokens, w_qkv, w_out, w_up, w_down, w_time, gain_one, bias_one, gain_two, bias_two, bias_up,
    bias_down, lengths, time_steps, cotangent,
):
    me = lax.axis_index("ctx")
    shard = lax.axis_index("fsdp")
    core = me % 2
    rows = tokens.shape[1]
    width = tokens.shape[2]
    head_size = width // HEADS
    seq_count = lengths.shape[1]
    hidden = w_up.shape[1]
    other = 1 - shard
    chips = ctx_size // 2
    half = width // 2
    units = hidden // (ctx_size * fsdp_size)
    order, place_table = ring_tables(ctx_size)
    place = jnp.asarray(place_table)[me]
    who = jnp.stack([me, shard]).astype(jnp.int32)

    def across(values):
        return lax.ppermute(values, "fsdp", [(0, 1), (1, 0)])

    def gather(values):
        return lax.all_gather(values, "ctx", axis=0, tiled=True)

    def flip(values, bit=0):
        return lax.ppermute(
            values, "ctx", [(i, i ^ (1 << bit)) for i in range(ctx_size)]
        )

    def hop(values, step):
        return lax.ppermute(
            values,
            "ctx",
            [
                (2 * order[at] + c, 2 * order[(at + step) % chips] + c)
                for at in range(chips)
                for c in range(2)
            ],
        )

    def by_shard(mine, others, axis):
        first = jnp.where(shard == 0, mine, others)
        second = jnp.where(shard == 0, others, mine)
        return jnp.concatenate([first, second], axis=axis)

    def cut(values, start, size, axis):
        return lax.dynamic_slice_in_dim(values, start, size, axis)

    def halve(values, axis, mine, send):
        keep = lax.dynamic_index_in_dim(values, mine, axis, keepdims=False)
        give = lax.dynamic_index_in_dim(values, 1 - mine, axis, keepdims=False)
        return keep + send(give.astype(BF16)).astype(F32)

    ends = []
    for s in range(seq_count):
        ends.append(lengths[0, s] + (ends[-1] if ends else 0))
    ends_vector = jnp.stack(ends)
    base = place * rows
    index = me * rows + jnp.arange(rows, dtype=jnp.int32)
    segment = segments(ends, index)
    seg_col = segment[:, None]
    live = (segment < seq_count).astype(F32)[:, None]
    own_tokens = tokens[0]
    steps_row = time_steps.reshape(1, seq_count)
    high = (steps_row // 256).astype(BF16)
    low = (steps_row % 256).astype(BF16)
    head = core * chips + me // 2
    w_head = jnp.concatenate(
        [cut(w_qkv, k * width + head * head_size, head_size, 1) for k in range(3)], axis=1
    )
    class Ring:
        def __init__(self, values):
            self.right = self.left = values
            self.parts = [values]
            self.step = 0

        def go(self, *earlier):
            right, left = self.right, self.left
            if earlier:
                right, left = (
                    after(right, *earlier),
                    after(left, *earlier),
                )
            self.step += 1
            self.right = hop(right, 1)
            if self.step <= (chips - 1) // 2:
                self.left = hop(left, -1)
                return [self.right, self.left]
            return [self.right]

        def came(self, values):
            self.right = values[0]
            if len(values) > 1:
                self.left = values[1]
            self.parts += values

    def fenced(groups):
        flat = [v for group in groups for v in group]
        flat = list(fence(*flat))
        out = []
        for group in groups:
            out.append(flat[: len(group)])
            flat = flat[len(group) :]
        return out

    def with_flips(values):
        return [part for v in values for part in (v, flip(v))]

    tok = Ring(own_tokens)
    tok_new = tok.go()
    packed = jnp.concatenate([gain_one[None, :], bias_one[None, :], high, low], axis=1)
    tok_new, (packed, w_head) = fenced([tok_new, [packed, w_head]])
    tok.came(tok_new)

    tok_new = tok.go()
    packed_other = across(packed)
    w_head_other = across(w_head)
    base = after(base, packed)
    all_index = (base[:, None] + jnp.arange(rows, dtype=jnp.int32)[None, :]).reshape(-1)
    all_position = positions(ends, all_index, segments(ends, all_index))
    half_width = head_size // 2
    inverse = jnp.exp(
        -math.log(10000.0) * jnp.arange(half_width, dtype=F32) / half_width
    )
    angle = inverse[:, None] * all_position.astype(F32)[None, :]
    cos = jnp.cos(angle)
    sin = jnp.sin(angle)

    inputs = own_tokens.astype(F32)
    grad_y = cotangent[0].astype(F32) * live
    grad_y_b = grad_y.astype(BF16)
    out_half = w_out.shape[0] // 2
    me_1 = after(me, packed)
    out_mine = across(cut(w_out, (me_1 % 2) * out_half, out_half, 0))
    tok_new, (packed_other, w_head, cos, sin, grad_y_b, me_2, place, who, base, w_head_other) = fenced(
        [tok_new, [packed_other, w_head, cos, sin, grad_y_b, me, place, who, base, w_head_other]]
    )
    tok.came(tok_new)

    tok_new = tok.go()
    packed_all = by_shard(packed, packed_other, 0)

    def vector_of(values, at, size):
        return values[:, at : at + size].reshape(1, -1).astype(F32)

    gain_first = vector_of(packed_all, 0, half)
    bias_first = vector_of(packed_all, half, half)
    all_steps = packed_all[:, width : width + seq_count].astype(F32) * 256.0 + packed_all[
        :, width + seq_count :
    ].astype(F32)
    all_embedded = embed(all_steps, w_time.shape[0] * fsdp_size).astype(BF16)
    own_part = cut(all_embedded, shard * w_time.shape[0], w_time.shape[0], 2)
    film_part = jnp.dot(
        own_part.reshape(fsdp_size * seq_count, -1), w_time, preferred_element_type=F32
    ).reshape(fsdp_size, seq_count, 2 * width)
    film_other = across(lax.dynamic_index_in_dim(film_part, other, 0, keepdims=False))
    film = film_other + lax.dynamic_index_in_dim(film_part, shard, 0, keepdims=False)
    film = jnp.concatenate([film, jnp.zeros((1, 2 * width), F32)], axis=0)
    gains = gain_first + film[:, :width]
    shifts = bias_first + film[:, width:]
    up_parts = 2
    up_deep = w_up.shape[0] // up_parts
    quarter = hidden // 4
    up_send = [
        lax.dynamic_slice(w_up, (p * up_deep, (me_2 % 4) * quarter), (up_deep, quarter))
        for p in range(up_parts)
    ]
    tok_new, (gains, shifts, out_mine), up_send = fenced(
        [tok_new, [gains, shifts, out_mine], up_send]
    )
    tok_flips = with_flips(tok.parts)
    tok.came(tok_new)

    tok_last = tok.go()
    all_grad_y = gather(after(grad_y_b, gains))
    grad_y_other = across(grad_y_b)
    up_mine = [across(after(up_send[0], gains))]
    tok_flips += with_flips(tok_new)
    constants = (base, ends_vector, gains, shifts, w_head, w_head_other, cos, sin, head_size)
    head_values = project_chunks(who, tok_flips, *constants)
    head_values, tok_last, (grad_y_other, gain_two, up_send[1]) = fenced(
        [head_values, tok_last, [grad_y_other, gain_two, up_send[1]]]
    )

    up_mine.append(across(up_send[1]))
    all_norm, query_t, key, key_t, value_t, pair = project_chunks(
        who, with_flips(tok_last), *constants, first=chips - 1, earlier=head_values
    )
    out_t, sent, lse = attend(place, query_t, key, value_t, rows)
    rest = jnp.concatenate(
        [v[None, :] for v in (gain_two, bias_two, bias_down, bias_up)], axis=1
    )
    out_t, sent, lse, *up_mine, rest, me_5, grad_y_other = fence(
        out_t, sent, lse, *up_mine, rest, me, grad_y_other
    )

    attended = lax.all_to_all(sent, "ctx", 0, 0, tiled=True)
    rest_other = across(rest)
    up_side = [flip(up_mine[0], 1), flip(up_mine[1], 1)]
    qkv_half = w_qkv.shape[0] // 2
    qkv_send = [
        cut(w_qkv, (me_5 % 2) * qkv_half + k * (qkv_half // 2), qkv_half // 2, 0)
        for k in range(2)
    ]
    qkv_mine = [across(qkv_send[0])]
    far_grad = across(dims(grad_y_other, w_down, 1, 1).astype(BF16))
    near_grad = dims(after(grad_y_b, lse), w_down, 1, 1)
    out_pieces = (w_out, out_mine, flip(out_mine))
    pieces = [with_flips([v]) for v in up_mine]
    rest_5 = [rest_other, me_5, qkv_send[1], qkv_mine[0]]
    (attended, up_side[0], near_grad), rest_5, *pieces = fenced(
        [[attended, up_side[0], near_grad], rest_5, *pieces]
    )
    rest_other, me_6, qkv_send[1], qkv_mine[0] = rest_5

    rest = by_shard(rest, rest_other, 0)
    gain_second = vector_of(rest, 0, half)
    bias_second = vector_of(rest, half, half)
    bias_output = vector_of(rest, width, half)
    bias_hidden = vector_of(rest, width + half, hidden // 2)
    resid, normal_two, scale_two, norm_two_b = middle(
        who, attended, out_pieces, own_tokens, gain_second, bias_second
    )
    first_units = shard * (hidden // 2) + me_6 * units
    second_units = other * (hidden // 2) + me_6 * units
    up_first = cut(w_up, first_units, units, 1)
    up_second = cut(w_up, second_units, units, 1)
    up_own = jnp.concatenate([up_first, up_second], axis=1)
    down_own = cut(w_down, me_6 * units, units, 0)
    up_give = jnp.concatenate([up_second, up_first], axis=1)
    pieces[0] = pieces[0] + with_flips([up_side[0]])
    rest_6 = [up_own, up_give, down_own]
    (norm_two_b, far_grad, up_side[1]), rest_6, *pieces = fenced(
        [[norm_two_b, far_grad, up_side[1]], rest_6, *pieces]
    )
    up_own, up_give, down_own = rest_6
    pieces = pieces[0] + pieces[1] + with_flips([up_side[1]])

    all_norm_two = gather(norm_two_b)
    up_other = across(after(up_give, norm_two_b))
    down_other = across(after(down_own, norm_two_b))
    act_b, grad_resid, grad_resid_b, grad_att, sums = feed(
        who, norm_two_b, w_up, pieces, near_grad, far_grad, bias_hidden, normal_two, scale_two,
        gain_second, grad_y_b, out_pieces,
    )
    grad_att, grad_resid_b, me_8, up_other, down_other = fence(
        grad_att, grad_resid_b, me, up_other, down_other
    )

    grad_att = grad_att.reshape(HEADS, head_size, rows)
    grad_att = lax.all_to_all(grad_att, "ctx", 0, 0, tiled=True)
    qkv_mine.append(across(after(qkv_send[1], up_other, down_other)))
    deep = width // (ctx_size * fsdp_size)
    out_part = jnp.dot(
        attended.reshape(width, rows), grad_resid_b, preferred_element_type=F32
    )
    out_part = out_part.reshape(chips, fsdp_size, 2, deep, width)
    out_part = halve(out_part, 2, core, flip)
    down_half = w_down.shape[0] // 2
    down_send = cut(w_down, (me_8 % 2) * down_half, down_half, 0)
    grad_att, down_send, out_part = fence(grad_att, down_send, out_part)

    out_part = halve(out_part, 1, shard, across)
    mixed, mixed_sent = attend_back(
        place, query_t, grad_att, out_t, lse, key, key_t, pair, cos, sin, rows
    )
    mixed, mixed_sent, out_part, qkv_mine[1] = fence(
        mixed, mixed_sent, out_part, qkv_mine[1]
    )

    mixed_got = lax.all_to_all(mixed_sent, "ctx", 0, 0, tiled=True)
    qkv_slice = jnp.dot(mixed, all_norm, preferred_element_type=F32)
    qkv_keep = cut(qkv_slice, shard * half, half, 1)
    qkv_give = cut(qkv_slice, other * half, half, 1).astype(BF16)
    bias_slice = jnp.concatenate(
        [cut(bias_hidden, at, units, 1) for at in (first_units, second_units)], axis=1
    )
    qkv_other = across(qkv_give)
    out_part = halve(
        out_part.reshape(-1, 2, deep, width), 1, (me >> 1) % 2, lambda v: flip(v, 1)
    )
    qkv_sum = (qkv_keep + qkv_other.astype(F32)).astype(BF16)
    qkv_sum, bias_slice, all_norm_two, all_grad_y, out_part = fence(
        qkv_sum, bias_slice, all_norm_two, all_grad_y, out_part
    )

    all_qkv = gather(qkv_sum)
    out_part = halve(
        out_part.reshape(-1, 2, deep, width), 1, (me >> 2) % 2, lambda v: flip(v, 2)
    )
    wide_keep, wide_give = slices(
        who, all_norm_two, all_grad_y, up_own, up_other, down_own, down_other, bias_slice
    )
    wide_keep, wide_give, mixed_got, out_part = fence(
        wide_keep, wide_give, mixed_got, out_part
    )

    wide_other = across(wide_give)
    qkv_mine = fence(*qkv_mine, wide_give)[:-1]
    qkv_pieces = (w_qkv, *qkv_mine, *[flip(v) for v in qkv_mine])
    grad_tokens, total = first_back(
        who, ends_vector, mixed_got, qkv_pieces, own_tokens, grad_resid, gains, sums
    )
    total_other = across(total)
    out_part = halve(
        out_part.reshape(-1, 2, deep, width), 1, (me >> 3) % 2, lambda v: flip(v, 3)
    )
    wide_other, total, total_other, out_part = fence(
        wide_other, total, total_other, out_part
    )

    total = jnp.concatenate(
        [total[:8] + total_other[:8], total[8:], total_other[8:]], axis=0
    )
    total = jnp.pad(total, ((0, -total.shape[0] % 16), (0, 0))).astype(BF16)
    lines = total.shape[0]

    def narrow(values):
        return [values[:, k * 128 : (k + 1) * 128] for k in range(width // 128)]

    wide = jnp.concatenate(
        [(wide_keep + wide_other.astype(F32)).astype(BF16)]
        + narrow(out_part.reshape(deep, width).astype(BF16))
        + narrow(total),
        axis=0,
    )
    wide_ring = Ring(wide)
    wide_new = wide_ring.go()
    down_mine = across(after(down_send, wide))
    wide_new = list(fence(*wide_new))
    wide_flips = with_flips(wide_ring.parts)
    wide_ring.came(wide_new)

    wide_flips += with_flips(wide_new)
    wide_new = wide_ring.go()
    grads = expand_wide(place, 0, wide_flips, width, ())
    own_embed = lax.dynamic_index_in_dim(own_part, shard, 0, keepdims=False)
    other_embed = lax.dynamic_index_in_dim(own_part, other, 0, keepdims=False)
    own_embed = own_embed.astype(F32)
    other_embed = other_embed.astype(F32)
    wide_new, grads, (down_mine, own_embed, other_embed, all_qkv) = fenced(
        [wide_new, grads, [down_mine, own_embed, other_embed, all_qkv]]
    )
    wide_ring.came(wide_new)

    more_flips = with_flips(wide_new)
    wide_new = wide_ring.go()
    grad_qkv = expand_last(all_qkv.reshape(ctx_size, 3 * head_size, half), head_size)
    down_flip = flip(down_mine)
    branch = bias_output
    for b, row in (
        (w_down, shard * (hidden // 2)),
        (down_mine, other * (hidden // 2) + core * down_half),
        (down_flip, other * (hidden // 2) + (1 - core) * down_half),
    ):
        branch = branch + jnp.dot(
            cut(act_b, row, b.shape[0], 1), b, preferred_element_type=F32
        )
    output = (live * (resid + branch)).astype(BF16)
    wide_new, (output, grad_qkv), more_flips = fenced(
        [wide_new, [output, grad_qkv], more_flips]
    )

    tall = wide.shape[0] // 2
    last_top = hop(wide_new[0][:tall], 1)
    last_low = hop(wide_new[1][tall:], -1)
    more_flips += with_flips(wide_new)
    grads = expand_wide(place, len(wide_flips) // 2, more_flips, width, grads)
    grads, (last_top, last_low) = fenced([grads, [last_top, last_low]])

    wide_last = with_flips([jnp.concatenate([last_top, last_low], axis=0)])
    grad_up, grad_down, grad_out = expand_wide(
        place, chips - 1, wide_last, width, grads
    )
    grad_time, *vectors = small_sums(
        who, own_embed, other_embed, wide_flips + more_flips + wide_last,
        wide.shape[0] - lines * width // 128, lines, width,
    )
    return (
        output[None],
        grad_tokens[None],
        grad_qkv,
        grad_out,
        grad_up,
        grad_down,
        grad_time,
        *[vector.reshape(-1) for vector in vectors],
    )


def solution(mesh):
    in_specs = (
        (P("fsdp", "ctx", None),)
        + (P("fsdp", None),) * 5
        + (P("fsdp"),) * 6
        + (P("fsdp", None), P("fsdp", None), P("fsdp", "ctx", None))
    )
    out_specs = (
        (P("fsdp", "ctx", None),) * 2 + (P("fsdp", None),) * 5 + (P("fsdp"),) * 6
    )
    ctx_size, fsdp_size = mesh.shape["ctx"], mesh.shape["fsdp"]
    paired = ctx_size == HEADS and fsdp_size == 2
    return jax.shard_map(
        functools.partial(body if paired else body_general, ctx_size, fsdp_size),
        mesh=mesh,
        in_specs=in_specs,
        out_specs=out_specs,
        check_vma=False,
    )
```

profile of v0, /device:TPU:0, one launch (start us, length us, event | category | flops | bytes accessed | tf_op | source)
XLA Modules:
  0.0 322.0 jit_solution(1231694855132059480)
XLA Ops:
  7.3 3.1 collective-permute-start
  11.1 1.2 fusion.27.place_ref
  13.6 1.2 constant_dynamic-slice_fusion.21
  17.2 1.8 fusion.5.refs_14_
  19.0 2.0 collective-permute-start.4
  21.0 1.6 collective-permute-start.2
  24.2 2.0 collective-permute-start.14
  26.3 1.8 multiply_sine_fusion
  28.0 4.2 %collective-permute-done.5.refs_17_.refs_5_ = bf16[512,192]{1,0:T(8,128)(2,1)S(1)} collective-permute-done((bf16[512,192]{1,0:T(8,128)(2,1)S(1)}, bf16[512,192]{1,0:T(8,128)(2,1)S(1)}, u32[]{:S(2)}, u32[]{:S(2)}) %collective-permute-start.5) | collective-permute-done | bytes 196640 | tf_op jit(solution)/shard_map/ppermute | solution.py:1318
  33.0 2.0 collective-permute-start.11
  35.0 1.3 constant_dynamic-slice_fusion.22
  36.3 4.8 %collective-permute-done.13 = f32[1,2048]{1,0:T(1,128)S(1)} collective-permute-done((f32[1,2048]{1,0:T(1,128)S(1)}, f32[1,2048]{1,0:T(1,128)S(1)}, u32[]{:S(2)}, u32[]{:S(2)}) %collective-permute-start.13) | collective-permute-done | bytes 8224 | tf_op jit(solution)/shard_map/ppermute | solution.py:1318
  44.3 1.5 collective-permute-start.18
  45.8 1.6 collective-permute-start.17
  48.8 10.3 %project_chunks.2 = (bf16[2048,1024]{1,0:T(8,128)(2,1)}, bf16[128,2048]{1,0:T(8,128)(2,1)}, bf16[2048,128]{1,0:T(8,128)(2,1)}, bf16[64,2048]{1,0:T(8,128)(2,1)},...) custom-call(s32[2]{0:T(128)} %pad_add_fusion.who_ref, s32[1]{0:T(128)} %bitcast.110.ends_ref, s32[16]{0:T(128)} %copy-done.36, ...), custom_call_target="tpu_custom_call" | custom-call | flops 3758096384 | bytes 7340032 | tf_op jit(solution)/shard_map/project_chunks/pallas_call | solution.py:350
  59.1 1.6 collective-permute-start.21
  61.5 3.4 %project_chunks.3 = (bf16[2048,1024]{1,0:T(8,128)(2,1)}, bf16[128,2048]{1,0:T(8,128)(2,1)}, bf16[2048,128]{1,0:T(8,128)(2,1)}, bf16[64,2048]{1,0:T(8,128)(2,1)},...) custom-call(s32[2]{0:T(128)} %pad_add_fusion.who_ref, ...), custom_call_target="tpu_custom_call", output_to_operand_aliasing={{0}: (11, {}), {1}: (12, {}), {2}: (13, {}), {3}: (14, {}),... | custom-call | flops 536870912 | bytes 1048576 | tf_op jit(solution)/shard_map/project_chunks/pallas_call | solution.py:350
  64.9 12.9 %attend_head.1 = (f32[64,2048]{1,0:T(8,128)}, bf16[16,64,128]{2,1,0:T(8,128)(2,1)}, f32[1,2048]{1,0:T(1,128)}) custom-call(s32[16]{0:T(128)} %fusion.27.place_ref, bf16[128,2048]{1,0:T(8,128)(2,1)} %get-tuple-element.219.query_ref, bf16[2048,128]{1,0:T(8,128)(2,1)} %get-tuple-element.220.key_ref, bf16[64,2048]{1,0:T(8,128)(2,1)} %get-tuple-element.221.value_ref), custom_call_target="tpu_custom_call" | custom-call | flops 4294967296 | bytes 2097152 | tf_op jit(solution)/shard_map/attend_head/pallas_call | solution.py:394
  78.6 2.4 constant_dynamic-slice_fusion.11
  81.0 1.4 collective-permute-start.24
  84.0 6.9 %all-to-all-start = ((bf16[16,64,128]{2,1,0:T(8,128)(2,1)}), bf16[16,64,128]{2,1,0:T(8,128)(2,1)S(1)}, u32[]{:S(2)}, u32[]{:S(2)}) async-start(bf16[16,64,128]{2,1,0:T(8,128)(2,1)} %get-tuple-element.230), calls=%async_computation | async-start | bytes 524288 | tf_op jit(solution)/shard_map/all_to_all | solution.py:1495
  91.1 4.9 %fusion.35.refs_8_ = f32[128,2048]{1,0:T(8,128)} fusion(bf16[128,1024]{1,0:T(8,128)(2,1)S(1)} %copy-done.20, bf16[2048,1024]{1,0:T(8,128)(2,1)} %param.20), kind=kOutput, calls=%fused_computation.135 | convolution fusion | flops 536870912 | bytes 5505024 | tf_op jit(solution)/shard_map/dot_general | solution.py:22
  96.1 1.5 convolution_convert_fusion
  97.6 3.3 %collective-permute-done.23 = bf16[1,3584]{1,0:T(2,128)(2,1)S(1)} collective-permute-done((bf16[1,3584]{1,0:T(2,128)(2,1)S(1)}, bf16[1,3584]{1,0:T(2,128)(2,1)S(1)}, u32[]{:S(2)}, u32[]{:S(2)}) %collective-permute-start.23) | collective-permute-done | bytes 7200 | tf_op jit(solution)/shard_map/ppermute | solution.py:1318
  101.4 1.4 collective-permute-start.28
  105.1 3.6 %output_projection.1 = (f32[128,1024]{1,0:T(8,128)}, f32[128,1024]{1,0:T(8,128)}, f32[128,1]{1,0:T(8,128)}, bf16[128,1024]{1,0:T(8,128)(2,1)}) custom-call(s32[2]{0:T(128)} %pad_add_fusion.who_ref, bf16[16,64,128]{2,1,0:T(8,128)(2,1)} %copy-done.23, bf16[512,1024]{1,0:T(8,128)(2,1)} %refs_15_.1, bf16[256,1024]{1,0:T(8,128)(2,1)} %collective-permute-done.14.mine_ref.refs_16_, ...), custom_call_target="tpu_custom_call" | custom-call | flops 1073741824 | bytes 4194304 | tf_op jit(solution)/shard_map/output_projection/pallas_call | solution.py:587
  111.5 4.1 %collective-permute-done.28.refs_9_ = bf16[128,2048]{1,0:T(8,128)(2,1)} collective-permute-done((bf16[128,2048]{1,0:T(8,128)(2,1)S(1)}, bf16[128,2048]{1,0:T(8,128)(2,1)}, u32[]{:S(2)}, u32[]{:S(2)}) %collective-permute-start.28) | collective-permute-done | bytes 524320 | tf_op jit(solution)/shard_map/ppermute | solution.py:1318
  116.3 1.4 collective-permute-start.33
  119.2 10.9 %feed_forward.1 = (bf16[128,4096]{1,0:T(8,128)(2,1)}, f32[128,1024]{1,0:T(8,128)}, bf16[128,1024]{1,0:T(8,128)(2,1)}, bf16[16,64,128]{2,1,0:T(8,128)(2,1)}, f32[8,1024]{1,0:T(8,128)}) custom-call(s32[2]{0:T(128)} %pad_add_fusion.who_ref, bf16[128,1024]{1,0:T(8,128)(2,1)} %get-tuple-element.248.norm_ref, bf16[512,4096]{1,0:T(8,128)(2,1)} %own_ref.4, ...), custom_call_target="tpu_custom_call" | custom-call | flops 8589934592 | bytes 16777216 | tf_op jit(solution)/shard_map/feed_forward/pallas_call | solution.py:675
  130.6 1.7 fusion.8
  132.4 2.0 copy-done.4
  134.7 7.0 %all-to-all-start.1 = ((bf16[16,64,128]{2,1,0:T(8,128)(2,1)}), bf16[16,64,128]{2,1,0:T(8,128)(2,1)}, u32[]{:S(2)}, u32[]{:S(2)}) async-start(bf16[16,64,128]{2,1,0:T(8,128)(2,1)} %get-tuple-element.266), calls=%async_computation.1 | async-start | bytes 524288 | tf_op jit(solution)/shard_map/all_to_all | solution.py:1549
  143.0 3.6 %constant_dynamic-slice_fusion.7 = bf16[1024,1024]{1,0:T(8,128)(2,1)} fusion(bf16[2048,1024]{1,0:T(8,128)(2,1)} %param.20, s32[]{:T(128)S(6)} %select_n.219), kind=kLoop, calls=%fused_computation.78 | loop fusion | bytes 4194308 | tf_op jit(solution)/shard_map/dynamic_slice | solution.py:1345
  146.6 1.6 bitcast_add_fusion
  148.1 7.2 %all-to-all-done.1.grad_ref = bf16[16,64,128]{2,1,0:T(8,128)(2,1)} async-done(((bf16[16,64,128]{2,1,0:T(8,128)(2,1)}), bf16[16,64,128]{2,1,0:T(8,128)(2,1)}, u32[]{:S(2)}, u32[]{:S(2)}) %all-to-all-start.1) | async-done | bytes 262176 | tf_op jit(solution)/shard_map/all_to_all | solution.py:1549
  155.5 19.0 %attend_head_back.1 = (bf16[192,2048]{1,0:T(8,128)(2,1)}, bf16[16,192,128]{2,1,0:T(8,128)(2,1)}) custom-call(s32[16]{0:T(128)} %fusion.27.place_ref, bf16[128,2048]{1,0:T(8,128)(2,1)} %get-tuple-element.219.query_ref, bf16[16,64,128]{2,1,0:T(8,128)(2,1)} %all-to-all-done.1.grad_ref, f32[64,2048]{1,0:T(8,128)} %get-tuple-element.270.out_ref, ...), custom_call_target="tpu_custom_call" | custom-call | flops 10737418240 | bytes 4194304 | tf_op jit(solution)/shard_map/attend_head_back/pallas_call | solution.py:443
  175.7 6.8 %all-to-all-start.2 = ((bf16[16,192,128]{2,1,0:T(8,128)(2,1)}), bf16[16,192,128]{2,1,0:T(8,128)(2,1)S(1)}, u32[]{:S(2)}, u32[]{:S(2)}) async-start(bf16[16,192,128]{2,1,0:T(8,128)(2,1)} %get-tuple-element.290), calls=%async_computation.2 | async-start | bytes 1572864 | tf_op jit(solution)/shard_map/all_to_all | solution.py:1569
  182.5 3.4 %fusion.36 = f32[192,1024]{1,0:T(8,128)S(1)} fusion(bf16[192,2048]{1,0:T(8,128)(2,1)} %get-tuple-element.280, bf16[2048,1024]{1,0:T(8,128)(2,1)} %get-tuple-element.281), kind=kOutput, calls=%fused_computation.136 | convolution fusion | flops 805306368 | bytes 5767168 | tf_op jit(solution)/shard_map/dot_general | solution.py:1570
  186.0 1.2 collective-permute-start.37
  187.3 2.0 collective-permute-start.38
  189.8 3.5 %collective-permute-done.37 = bf16[192,512]{1,0:T(8,128)(2,1)S(1)} collective-permute-done((bf16[192,512]{1,0:T(8,128)(2,1)S(1)}, bf16[192,512]{1,0:T(8,128)(2,1)S(1)}, u32[]{:S(2)}, u32[]{:S(2)}) %collective-permute-start.37) | collective-permute-done | bytes 196640 | tf_op jit(solution)/shard_map/ppermute | solution.py:1318
  194.0 4.3 %collective-permute-done.38 = bf16[4,32,1024]{2,1,0:T(8,128)(2,1)S(1)} collective-permute-done((bf16[4,32,1024]{2,1,0:T(8,128)(2,1)S(1)}, bf16[4,32,1024]{2,1,0:T(8,128)(2,1)S(1)}, u32[]{:S(2)}, u32[]{:S(2)}) %collective-permute-start.38) | collective-permute-done | bytes 262176 | tf_op jit(solution)/shard_map/ppermute | solution.py:1324
  198.5 3.2 %collective-permute-start.39 = (bf16[2,32,1024]{2,1,0:T(8,128)(2,1)S(1)}, bf16[2,32,1024]{2,1,0:T(8,128)(2,1)S(1)}, u32[]{:S(2)}, u32[]{:S(2)}) collective-permute-start(bf16[2,32,1024]{2,1,0:T(8,128)(2,1)S(1)} %fusion.14), channel_id=1, source_target_pairs={{0,8},{2,10},{4,12},{6,14},{8,0},{10,2},{12,4},{14,6},{16,24},{18,... | collective-permute-start | bytes 393224 | tf_op jit(solution)/shard_map/ppermute | solution.py:1324
  201.8 11.8 %weight_slices.1 = (f32[2048,128]{1,0:T(8,128)}, bf16[2048,128]{1,0:T(8,128)(2,1)}) custom-call(s32[2]{0:T(128)} %pad_add_fusion.who_ref, bf16[2048,1024]{1,0:T(8,128)(2,1)} %all-gather.4.cloned.1.call-done.norm_ref, bf16[2048,1024]{1,0:T(8,128)(2,1)} %all-gather.6.cloned.1.call-done.grad_ref, bf16[512,256]{1,0:T(8,128)(2,1)} %get-tuple-element.286.up_own, ...), custom_call_target="tpu_custom_call" | custom-call | flops 4294967296 | bytes 12582912 | tf_op jit(solution)/shard_map/weight_slices/pallas_call | solution.py:514
  215.3 1.2 collective-permute-start.44
  217.3 6.3 %first_norm_back.1 = (bf16[128,1024]{1,0:T(8,128)(2,1)}, f32[12,1024]{1,0:T(8,128)}) custom-call(s32[2]{0:T(128)} %pad_add_fusion.who_ref, s32[1]{0:T(128)} %bitcast.112.ends_ref, bf16[16,192,128]{2,1,0:T(8,128)(2,1)} %copy-done.11, bf16[512,3072]{1,0:T(8,128)(2,1)} %own_ref.5, bf16[128,3072]{1,0:T(8,128)(2,1)} %copy-done.26, bf16[128,3072]{1,0:T(8,128)(2,1)} %copy-done.28, ...), custom_call_target="tpu_custom_call" | custom-call | flops 1610612736 | bytes 8388608 | tf_op jit(solution)/shard_map/first_norm_back/pallas_call | solution.py:743
  224.6 4.6 %collective-permute-done.40 = bf16[2048,128]{1,0:T(8,128)(2,1)S(1)} collective-permute-done((bf16[2048,128]{1,0:T(8,128)(2,1)}, bf16[2048,128]{1,0:T(8,128)(2,1)S(1)}, u32[]{:S(2)}, u32[]{:S(2)}) %collective-permute-start.40) | collective-permute-done | bytes 524320 | tf_op jit(solution)/shard_map/ppermute | solution.py:1318
  232.8 1.9 collective-permute-start.46
  234.8 18.7 %collective-permute-done.45.refs_2_ = bf16[2432,128]{1,0:T(8,128)(2,1)S(1)} collective-permute-done((bf16[2432,128]{1,0:T(8,128)(2,1)S(1)}, bf16[2432,128]{1,0:T(8,128)(2,1)S(1)}, u32[]{:S(2)}, u32[]{:S(2)}) %collective-permute-start.45) | collective-permute-done | bytes 622624 | tf_op jit(solution)/shard_map/ppermute | solution.py:1329
  253.5 7.2 %collective-permute-done.46.refs_4_ = bf16[2432,128]{1,0:T(8,128)(2,1)} collective-permute-done((bf16[2432,128]{1,0:T(8,128)(2,1)S(1)}, bf16[2432,128]{1,0:T(8,128)(2,1)}, u32[]{:S(2)}, u32[]{:S(2)}) %collective-permute-start.46) | collective-permute-done | bytes 622624 | tf_op jit(solution)/shard_map/ppermute | solution.py:1329
  261.3 2.0 collective-permute-start.48
  264.1 5.1 %expand_wide.3 = (f32[512,4096]{1,0:T(8,128)}, f32[2048,1024]{1,0:T(8,128)}, f32[512,1024]{1,0:T(8,128)}) custom-call(s32[16]{0:T(128)} %fusion.27.place_ref, bf16[2432,128]{1,0:T(8,128)(2,1)} %copy-done.6, bf16[2432,128]{1,0:T(8,128)(2,1)} %collective-permute-done.49.refs_1_, bf16[2432,128]{1,0:T(8,128)(2,1)} %copy-done.19, ...), custom_call_target="tpu_custom_call" | custom-call | flops 1867776 | bytes 11206656 | tf_op jit(solution)/shard_map/expand_wide/pallas_call | solution.py:917
  269.2 8.0 %collective-permute-done.47.refs_0_.refs_6_ = bf16[2432,128]{1,0:T(8,128)(2,1)S(1)} collective-permute-done((bf16[2432,128]{1,0:T(8,128)(2,1)S(1)}, bf16[2432,128]{1,0:T(8,128)(2,1)S(1)}, u32[]{:S(2)}, u32[]{:S(2)}) %collective-permute-start.47) | collective-permute-done | bytes 622624 | tf_op jit(solution)/shard_map/ppermute | solution.py:1329
  277.5 1.4 collective-permute-done.52
  279.4 1.7 collective-permute-start.54
  281.2 5.4 %expand_last.1 = f32[512,3072]{1,0:T(8,128)} custom-call(bf16[16,192,512]{2,1,0:T(8,128)(2,1)} %bitcast.115), custom_call_target="tpu_custom_call" | custom-call | flops 1572864 | bytes 9437184 | tf_op jit(solution)/shard_map/expand_last/pallas_call | solution.py:958
  286.6 2.2 fusion.12
  288.9 2.1 fusion.10
  292.6 2.8 collective-permute-done.53.refs_4_.refs_10_
  296.3 1.4 collective-permute-start.60
  300.1 6.3 %expand_wide.4 = (f32[512,4096]{1,0:T(8,128)}, f32[2048,1024]{1,0:T(8,128)}, f32[512,1024]{1,0:T(8,128)}) custom-call(s32[16]{0:T(128)} %fusion.27.place_ref, bf16[2432,128]{1,0:T(8,128)(2,1)} %copy-done.12, bf16[2432,128]{1,0:T(8,128)(2,1)} %copy-done.14, ...), custom_call_target="tpu_custom_call", output_to_operand_aliasing={{0}: (9, {}), {1}: (10, {}), {2}: (11, {})} | custom-call | flops 2490368 | bytes 14942208 | tf_op jit(solution)/shard_map/expand_wide/pallas_call | solution.py:917
  307.2 2.0 collective-permute-done.62.refs_1_.refs_15_
  310.1 2.4 small_gradients.1
  312.4 3.0 expand_wide.5
  (289 shorter events, 41.7 us)
Async XLA Ops:
  7.2 191.2 %all-gather.6.cloned.1.call-start = ((), (), s32[]{:S(2)}) async-start(), calls=%async_computation.4 | async-start | bytes 4456448 | tf_op jit(solution)/shard_map/all_gather | solution.py:1321
  7.3 11.7 %collective-permute-start = (bf16[128,1024]{1,0:T(8,128)(2,1)}, bf16[128,1024]{1,0:T(8,128)(2,1)S(1)}, u32[]{:S(2)}, u32[]{:S(2)}) collective-permute-start(bf16[128,1024]{1,0:T(8,128)(2,1)} %bitcast.119), channel_id=1, source_target_pairs={{0,8},{2,10},{8,16},{10,18},{16,24},{18,26},{24,28},{26,30},{28,20... | collective-permute-start | bytes 786440 | tf_op jit(solution)/shard_map/ppermute | solution.py:1329
  10.4 8.6 %collective-permute-start.1 = (bf16[128,1024]{1,0:T(8,128)(2,1)}, bf16[128,1024]{1,0:T(8,128)(2,1)S(1)}, u32[]{:S(2)}, u32[]{:S(2)}) collective-permute-start(bf16[128,1024]{1,0:T(8,128)(2,1)} %bitcast.120), channel_id=1, source_target_pairs={{0,4},{2,6},{8,0},{10,2},{16,8},{18,10},{24,16},{26,18},{28,24},{3... | collective-permute-start | bytes 786440 | tf_op jit(solution)/shard_map/ppermute | solution.py:1329
  19.0 9.1 %collective-permute-start.4 = (bf16[1,1026]{1,0:T(2,128)(2,1)S(1)}, bf16[1,1026]{1,0:T(2,128)(2,1)S(1)}, u32[]{:S(2)}, u32[]{:S(2)}) collective-permute-start(bf16[1,1026]{1,0:T(2,128)(2,1)S(1)} %concatenate.53), channel_id=1, source_target_pairs={{0,1},{1,0},{2,3},{3,2},{4,5},{5,4},{6,7},{7,6},{8,9},{9,8},{10,11... | collective-permute-start | bytes 6164 | tf_op jit(solution)/shard_map/ppermute | solution.py:1318
  21.0 11.3 %collective-permute-start.2 = (bf16[128,1024]{1,0:T(8,128)(2,1)S(1)}, bf16[128,1024]{1,0:T(8,128)(2,1)}, u32[]{:S(2)}, u32[]{:S(2)}) collective-permute-start(bf16[128,1024]{1,0:T(8,128)(2,1)S(1)} %collective-permute-done.refs_2_), channel_id=1, source_target_pairs={{0,8},{2,10},{8,16},{10,18},{16,24},{18,26},{24,28},{26,30},{28,20... | collective-permute-start | bytes 786440 | tf_op jit(solution)/shard_map/ppermute | solution.py:1329
  22.6 9.7 %collective-permute-start.3 = (bf16[128,1024]{1,0:T(8,128)(2,1)S(1)}, bf16[128,1024]{1,0:T(8,128)(2,1)}, u32[]{:S(2)}, u32[]{:S(2)}) collective-permute-start(bf16[128,1024]{1,0:T(8,128)(2,1)S(1)} %collective-permute-done.1.refs_4_), channel_id=1, source_target_pairs={{0,4},{2,6},{8,0},{10,2},{16,8},{18,10},{24,16},{26,18},{28,24},{3... | collective-permute-start | bytes 786440 | tf_op jit(solution)/shard_map/ppermute | solution.py:1329
  23.0 9.2 %collective-permute-start.5 = (bf16[512,192]{1,0:T(8,128)(2,1)S(1)}, bf16[512,192]{1,0:T(8,128)(2,1)S(1)}, u32[]{:S(2)}, u32[]{:S(2)}) collective-permute-start(bf16[512,192]{1,0:T(8,128)(2,1)S(1)} %pad_maximum_fusion.refs_16_.refs_4_), channel_id=1, source_target_pairs={{0,1},{1,0},{2,3},{3,2},{4,5},{5,4},{6,7},{7,6},{8,9},{9,8},{10,11... | collective-permute-start | bytes 589832 | tf_op jit(solution)/shard_map/ppermute | solution.py:1318
  24.2 17.5 %collective-permute-start.14 = (bf16[256,1024]{1,0:T(8,128)(2,1)S(1)}, bf16[256,1024]{1,0:T(8,128)(2,1)}, u32[]{:S(2)}, u32[]{:S(2)}) collective-permute-start(bf16[256,1024]{1,0:T(8,128)(2,1)S(1)} %constant_dynamic-slice_fusion.14), channel_id=1, source_target_pairs={{0,1},{1,0},{2,3},{3,2},{4,5},{5,4},{6,7},{7,6},{8,9},{9,8},{10,11... | collective-permute-start | bytes 1572872 | tf_op jit(solution)/shard_map/ppermute | solution.py:1318
  32.8 8.3 %collective-permute-start.13 = (f32[1,2048]{1,0:T(1,128)S(1)}, f32[1,2048]{1,0:T(1,128)S(1)}, u32[]{:S(2)}, u32[]{:S(2)}) collective-permute-start(f32[1,2048]{1,0:T(1,128)S(1)} %constant_dynamic-slice_fusion.16), channel_id=1, source_target_pairs={{0,1},{1,0},{2,3},{3,2},{4,5},{5,4},{6,7},{7,6},{8,9},{9,8},{10,11... | collective-permute-start | bytes 24584 | tf_op jit(solution)/shard_map/ppermute | solution.py:1318
  33.0 8.7 %collective-permute-start.11 = (bf16[128,1024]{1,0:T(8,128)(2,1)}, bf16[128,1024]{1,0:T(8,128)(2,1)}, u32[]{:S(2)}, u32[]{:S(2)}) collective-permute-start(bf16[128,1024]{1,0:T(8,128)(2,1)} %collective-permute-done.2.refs_6_), channel_id=1, source_target_pairs={{0,8},{2,10},{8,16},{10,18},{16,24},{18,26},{24,28},{26,30},{28,20... | collective-permute-start | bytes 786440 | tf_op jit(solution)/shard_map/ppermute | solution.py:1329
  35.0 6.7 %collective-permute-start.12 = (bf16[128,1024]{1,0:T(8,128)(2,1)}, bf16[128,1024]{1,0:T(8,128)(2,1)}, u32[]{:S(2)}, u32[]{:S(2)}) collective-permute-start(bf16[128,1024]{1,0:T(8,128)(2,1)} %collective-permute-done.3.refs_8_), channel_id=1, source_target_pairs={{0,4},{2,6},{8,0},{10,2},{16,8},{18,10},{24,16},{26,18},{28,24},{3... | collective-permute-start | bytes 786440 | tf_op jit(solution)/shard_map/ppermute | solution.py:1329
  42.4 3.4 %collective-permute-start.10 = (bf16[128,1024]{1,0:T(8,128)(2,1)}, bf16[128,1024]{1,0:T(8,128)(2,1)S(1)}, u32[]{:S(2)}, u32[]{:S(2)}) collective-permute-start(bf16[128,1024]{1,0:T(8,128)(2,1)} %collective-permute-done.3.refs_8_), channel_id=1, source_target_pairs={{0,2},{2,0},{4,6},{6,4},{8,10},{10,8},{12,14},{14,12},{16,18},{18,... | collective-permute-start | bytes 786440 | tf_op jit(solution)/shard_map/ppermute | solution.py:1324
  42.8 4.5 %collective-permute-start.9 = (bf16[128,1024]{1,0:T(8,128)(2,1)}, bf16[128,1024]{1,0:T(8,128)(2,1)S(1)}, u32[]{:S(2)}, u32[]{:S(2)}) collective-permute-start(bf16[128,1024]{1,0:T(8,128)(2,1)} %collective-permute-done.2.refs_6_), channel_id=1, source_target_pairs={{0,2},{2,0},{4,6},{6,4},{8,10},{10,8},{12,14},{14,12},{16,18},{18,... | collective-permute-start | bytes 786440 | tf_op jit(solution)/shard_map/ppermute | solution.py:1324
  43.4 4.6 %collective-permute-start.15 = (bf16[128,1024]{1,0:T(8,128)(2,1)}, bf16[128,1024]{1,0:T(8,128)(2,1)S(1)}, u32[]{:S(2)}, u32[]{:S(2)}) collective-permute-start(bf16[128,1024]{1,0:T(8,128)(2,1)} %collective-permute-done.11.refs_10_), channel_id=1, source_target_pairs={{0,2},{2,0},{4,6},{6,4},{8,10},{10,8},{12,14},{14,12},{16,18},{18,... | collective-permute-start | bytes 786440 | tf_op jit(solution)/shard_map/ppermute | solution.py:1324
  43.7 4.2 %collective-permute-start.16 = (bf16[128,1024]{1,0:T(8,128)(2,1)}, bf16[128,1024]{1,0:T(8,128)(2,1)S(1)}, u32[]{:S(2)}, u32[]{:S(2)}) collective-permute-start(bf16[128,1024]{1,0:T(8,128)(2,1)} %collective-permute-done.12.refs_12_), channel_id=1, source_target_pairs={{0,2},{2,0},{4,6},{6,4},{8,10},{10,8},{12,14},{14,12},{16,18},{18,... | collective-permute-start | bytes 786440 | tf_op jit(solution)/shard_map/ppermute | solution.py:1324
  44.3 14.7 %collective-permute-start.18 = (bf16[128,1024]{1,0:T(8,128)(2,1)S(1)}, bf16[128,1024]{1,0:T(8,128)(2,1)S(1)}, u32[]{:S(2)}, u32[]{:S(2)}) collective-permute-start(bf16[128,1024]{1,0:T(8,128)(2,1)S(1)} %copy-done.20), channel_id=1, source_target_pairs={{0,1},{1,0},{2,3},{3,2},{4,5},{5,4},{6,7},{7,6},{8,9},{9,8},{10,11... | collective-permute-start | bytes 786440 | tf_op jit(solution)/shard_map/ppermute | solution.py:1318
  45.8 13.3 %collective-permute-start.17 = (bf16[128,1024]{1,0:T(8,128)(2,1)}, bf16[128,1024]{1,0:T(8,128)(2,1)S(1)}, u32[]{:S(2)}, u32[]{:S(2)}) collective-permute-start(bf16[128,1024]{1,0:T(8,128)(2,1)} %collective-permute-done.11.refs_10_), channel_id=1, source_target_pairs={{0,8},{2,10},{8,16},{10,18},{16,24},{18,26},{24,28},{26,30},{28,20... | collective-permute-start | bytes 786440 | tf_op jit(solution)/shard_map/ppermute | solution.py:1329
  47.4 30.4 %collective-permute-start.20 = (bf16[256,1024]{1,0:T(8,128)(2,1)S(1)}, bf16[256,1024]{1,0:T(8,128)(2,1)S(1)}, u32[]{:S(2)}, u32[]{:S(2)}) collective-permute-start(bf16[256,1024]{1,0:T(8,128)(2,1)S(1)} %get-tuple-element.226), channel_id=1, source_target_pairs={{0,1},{1,0},{2,3},{3,2},{4,5},{5,4},{6,7},{7,6},{8,9},{9,8},{10,11... | collective-permute-start | bytes 1572872 | tf_op jit(solution)/shard_map/ppermute | solution.py:1318
  59.1 18.7 %collective-permute-start.21 = (bf16[256,1024]{1,0:T(8,128)(2,1)S(1)}, bf16[256,1024]{1,0:T(8,128)(2,1)}, u32[]{:S(2)}, u32[]{:S(2)}) collective-permute-start(bf16[256,1024]{1,0:T(8,128)(2,1)S(1)} %get-tuple-element.227), channel_id=1, source_target_pairs={{0,1},{1,0},{2,3},{3,2},{4,5},{5,4},{6,7},{7,6},{8,9},{9,8},{10,11... | collective-permute-start | bytes 1572872 | tf_op jit(solution)/shard_map/ppermute | solution.py:1318
  81.0 21.8 %collective-permute-start.24 = (bf16[128,3072]{1,0:T(8,128)(2,1)S(1)}, bf16[128,3072]{1,0:T(8,128)(2,1)S(1)}, u32[]{:S(2)}, u32[]{:S(2)}) collective-permute-start(bf16[128,3072]{1,0:T(8,128)(2,1)S(1)} %get-tuple-element.357), channel_id=1, source_target_pairs={{0,1},{1,0},{2,3},{3,2},{4,5},{5,4},{6,7},{7,6},{8,9},{9,8},{10,11... | collective-permute-start | bytes 2359304 | tf_op jit(solution)/shard_map/ppermute | solution.py:1318
  82.4 18.5 %collective-permute-start.22 = (bf16[256,1024]{1,0:T(8,128)(2,1)}, bf16[256,1024]{1,0:T(8,128)(2,1)}, u32[]{:S(2)}, u32[]{:S(2)}) collective-permute-start(bf16[256,1024]{1,0:T(8,128)(2,1)} %copy-done.40), channel_id=1, source_target_pairs={{0,4},{2,6},{4,0},{6,2},{8,12},{10,14},{12,8},{14,10},{16,20},{18,... | collective-permute-start | bytes 1572872 | tf_op jit(solution)/shard_map/ppermute | solution.py:1324
  82.9 18.5 %collective-permute-start.25 = (bf16[256,1024]{1,0:T(8,128)(2,1)}, bf16[256,1024]{1,0:T(8,128)(2,1)}, u32[]{:S(2)}, u32[]{:S(2)}) collective-permute-start(bf16[256,1024]{1,0:T(8,128)(2,1)} %copy-done.40), channel_id=1, source_target_pairs={{0,2},{2,0},{4,6},{6,4},{8,10},{10,8},{12,14},{14,12},{16,18},{18,... | collective-permute-start | bytes 1572872 | tf_op jit(solution)/shard_map/ppermute | solution.py:1324
  82.9 19.9 %collective-permute-start.26 = (bf16[256,1024]{1,0:T(8,128)(2,1)}, bf16[256,1024]{1,0:T(8,128)(2,1)}, u32[]{:S(2)}, u32[]{:S(2)}) collective-permute-start(bf16[256,1024]{1,0:T(8,128)(2,1)} %collective-permute-done.21.refs_4_), channel_id=1, source_target_pairs={{0,2},{2,0},{4,6},{6,4},{8,10},{10,8},{12,14},{14,12},{16,18},{18,... | collective-permute-start | bytes 1572872 | tf_op jit(solution)/shard_map/ppermute | solution.py:1324
  83.4 17.5 %collective-permute-start.23 = (bf16[1,3584]{1,0:T(2,128)(2,1)S(1)}, bf16[1,3584]{1,0:T(2,128)(2,1)S(1)}, u32[]{:S(2)}, u32[]{:S(2)}) collective-permute-start(bf16[1,3584]{1,0:T(2,128)(2,1)S(1)} %pad_maximum_fusion.4), channel_id=1, source_target_pairs={{0,1},{1,0},{2,3},{3,2},{4,5},{5,4},{6,7},{7,6},{8,9},{9,8},{10,11... | collective-permute-start | bytes 21512 | tf_op jit(solution)/shard_map/ppermute | solution.py:1318
  84.0 18.8 %all-to-all-start = ((bf16[16,64,128]{2,1,0:T(8,128)(2,1)}), bf16[16,64,128]{2,1,0:T(8,128)(2,1)S(1)}, u32[]{:S(2)}, u32[]{:S(2)}) async-start(bf16[16,64,128]{2,1,0:T(8,128)(2,1)} %get-tuple-element.230), calls=%async_computation | async-start | bytes 524288 | tf_op jit(solution)/shard_map/all_to_all | solution.py:1495
  90.9 107.6 %all-gather.4.cloned.1.call-start = ((), (), s32[]{:S(2)}) async-start(), calls=%async_computation.3 | async-start | bytes 4456448 | tf_op jit(solution)/shard_map/all_gather | solution.py:1321
  100.9 3.4 %collective-permute-start.27 = (bf16[256,1024]{1,0:T(8,128)(2,1)}, bf16[256,1024]{1,0:T(8,128)(2,1)S(1)}, u32[]{:S(2)}, u32[]{:S(2)}) collective-permute-start(bf16[256,1024]{1,0:T(8,128)(2,1)} %collective-permute-done.14.mine_ref.refs_16_), channel_id=1, source_target_pairs={{0,2},{2,0},{4,6},{6,4},{8,10},{10,8},{12,14},{14,12},{16,18},{18,... | collective-permute-start | bytes 1572872 | tf_op jit(solution)/shard_map/ppermute | solution.py:1324
  100.9 14.7 %collective-permute-start.29 = (bf16[256,1024]{1,0:T(8,128)(2,1)}, bf16[256,1024]{1,0:T(8,128)(2,1)}, u32[]{:S(2)}, u32[]{:S(2)}) collective-permute-start(bf16[256,1024]{1,0:T(8,128)(2,1)} %collective-permute-done.21.refs_4_), channel_id=1, source_target_pairs={{0,4},{2,6},{4,0},{6,2},{8,12},{10,14},{12,8},{14,10},{16,20},{18,... | collective-permute-start | bytes 1572872 | tf_op jit(solution)/shard_map/ppermute | solution.py:1324
  101.4 14.2 %collective-permute-start.28 = (bf16[128,2048]{1,0:T(8,128)(2,1)S(1)}, bf16[128,2048]{1,0:T(8,128)(2,1)}, u32[]{:S(2)}, u32[]{:S(2)}) collective-permute-start(bf16[128,2048]{1,0:T(8,128)(2,1)S(1)} %convolution_convert_fusion), channel_id=1, source_target_pairs={{0,1},{1,0},{2,3},{3,2},{4,5},{5,4},{6,7},{7,6},{8,9},{9,8},{10,11... | collective-permute-start | bytes 1572872 | tf_op jit(solution)/shard_map/ppermute | solution.py:1318
  102.8 12.7 %collective-permute-start.30 = (bf16[256,1024]{1,0:T(8,128)(2,1)}, bf16[256,1024]{1,0:T(8,128)(2,1)}, u32[]{:S(2)}, u32[]{:S(2)}) collective-permute-start(bf16[256,1024]{1,0:T(8,128)(2,1)} %collective-permute-done.22.refs_2_), channel_id=1, source_target_pairs={{0,2},{2,0},{4,6},{6,4},{8,10},{10,8},{12,14},{14,12},{16,18},{18,... | collective-permute-start | bytes 1572872 | tf_op jit(solution)/shard_map/ppermute | solution.py:1324
  115.6 2.8 collective-permute-start.31
  116.3 13.8 %collective-permute-start.33 = (bf16[128,1024]{1,0:T(8,128)(2,1)S(1)}, bf16[128,1024]{1,0:T(8,128)(2,1)S(1)}, u32[]{:S(2)}, u32[]{:S(2)}) collective-permute-start(bf16[128,1024]{1,0:T(8,128)(2,1)S(1)} %constant_dynamic-slice_fusion.8.down_own), channel_id=1, source_target_pairs={{0,1},{1,0},{2,3},{3,2},{4,5},{5,4},{6,7},{7,6},{8,9},{9,8},{10,11... | collective-permute-start | bytes 786440 | tf_op jit(solution)/shard_map/ppermute | solution.py:1318
  117.7 12.9 %collective-permute-start.32 = (bf16[512,256]{1,0:T(8,128)(2,1)S(1)}, bf16[512,256]{1,0:T(8,128)(2,1)S(1)}, u32[]{:S(2)}, u32[]{:S(2)}) collective-permute-start(bf16[512,256]{1,0:T(8,128)(2,1)S(1)} %get-tuple-element.263), channel_id=1, source_target_pairs={{0,1},{1,0},{2,3},{3,2},{4,5},{5,4},{6,7},{7,6},{8,9},{9,8},{10,11... | collective-permute-start | bytes 786440 | tf_op jit(solution)/shard_map/ppermute | solution.py:1318
  134.5 12.0 %collective-permute-start.34 = (bf16[8,2,32,1024]{3,2,1,0:T(8,128)(2,1)S(1)}, bf16[8,2,32,1024]{3,2,1,0:T(8,128)(2,1)}, u32[]{:S(2)}, u32[]{:S(2)}) collective-permute-start(bf16[8,2,32,1024]{3,2,1,0:T(8,128)(2,1)S(1)} %fusion.2), channel_id=1, source_target_pairs={{0,2},{2,0},{4,6},{6,4},{8,10},{10,8},{12,14},{14,12},{16,18},{18,... | collective-permute-start | bytes 3145736 | tf_op jit(solution)/shard_map/ppermute | solution.py:1324
  134.7 20.7 %all-to-all-start.1 = ((bf16[16,64,128]{2,1,0:T(8,128)(2,1)}), bf16[16,64,128]{2,1,0:T(8,128)(2,1)}, u32[]{:S(2)}, u32[]{:S(2)}) async-start(bf16[16,64,128]{2,1,0:T(8,128)(2,1)} %get-tuple-element.266), calls=%async_computation.1 | async-start | bytes 524288 | tf_op jit(solution)/shard_map/all_to_all | solution.py:1549
  142.4 33.3 %collective-permute-start.36 = (bf16[128,3072]{1,0:T(8,128)(2,1)}, bf16[128,3072]{1,0:T(8,128)(2,1)S(1)}, u32[]{:S(2)}, u32[]{:S(2)}) collective-permute-start(bf16[128,3072]{1,0:T(8,128)(2,1)} %get-tuple-element.279), channel_id=1, source_target_pairs={{0,1},{1,0},{2,3},{3,2},{4,5},{5,4},{6,7},{7,6},{8,9},{9,8},{10,11... | collective-permute-start | bytes 2359304 | tf_op jit(solution)/shard_map/ppermute | solution.py:1318
  155.4 19.1 %collective-permute-start.35 = (bf16[8,32,1024]{2,1,0:T(8,128)(2,1)S(1)}, bf16[8,32,1024]{2,1,0:T(8,128)(2,1)S(1)}, u32[]{:S(2)}, u32[]{:S(2)}) collective-permute-start(bf16[8,32,1024]{2,1,0:T(8,128)(2,1)S(1)} %fusion.3), channel_id=1, source_target_pairs={{0,1},{1,0},{2,3},{3,2},{4,5},{5,4},{6,7},{7,6},{8,9},{9,8},{10,11... | collective-permute-start | bytes 1572872 | tf_op jit(solution)/shard_map/ppermute | solution.py:1318
  175.7 38.0 %all-to-all-start.2 = ((bf16[16,192,128]{2,1,0:T(8,128)(2,1)}), bf16[16,192,128]{2,1,0:T(8,128)(2,1)S(1)}, u32[]{:S(2)}, u32[]{:S(2)}) async-start(bf16[16,192,128]{2,1,0:T(8,128)(2,1)} %get-tuple-element.290), calls=%async_computation.2 | async-start | bytes 1572864 | tf_op jit(solution)/shard_map/all_to_all | solution.py:1569
  182.5 96.4 %all-gather.8.cloned.1.call-start = ((), (), s32[]{:S(2)}) async-start(), calls=%async_computation.5 | async-start | bytes 3342336 | tf_op jit(solution)/shard_map/all_gather | solution.py:1321
  186.0 7.3 %collective-permute-start.37 = (bf16[192,512]{1,0:T(8,128)(2,1)S(1)}, bf16[192,512]{1,0:T(8,128)(2,1)S(1)}, u32[]{:S(2)}, u32[]{:S(2)}) collective-permute-start(bf16[192,512]{1,0:T(8,128)(2,1)S(1)} %dynamic-slice_convert_fusion.2), channel_id=1, source_target_pairs={{0,1},{1,0},{2,3},{3,2},{4,5},{5,4},{6,7},{7,6},{8,9},{9,8},{10,11... | collective-permute-start | bytes 589832 | tf_op jit(solution)/shard_map/ppermute | solution.py:1318
  187.3 11.1 %collective-permute-start.38 = (bf16[4,32,1024]{2,1,0:T(8,128)(2,1)S(1)}, bf16[4,32,1024]{2,1,0:T(8,128)(2,1)S(1)}, u32[]{:S(2)}, u32[]{:S(2)}) collective-permute-start(bf16[4,32,1024]{2,1,0:T(8,128)(2,1)S(1)} %fusion.7), channel_id=1, source_target_pairs={{0,4},{2,6},{4,0},{6,2},{8,12},{10,14},{12,8},{14,10},{16,20},{18,... | collective-permute-start | bytes 786440 | tf_op jit(solution)/shard_map/ppermute | solution.py:1324
  198.5 15.1 %collective-permute-start.39 = (bf16[2,32,1024]{2,1,0:T(8,128)(2,1)S(1)}, bf16[2,32,1024]{2,1,0:T(8,128)(2,1)S(1)}, u32[]{:S(2)}, u32[]{:S(2)}) collective-permute-start(bf16[2,32,1024]{2,1,0:T(8,128)(2,1)S(1)} %fusion.14), channel_id=1, source_target_pairs={{0,8},{2,10},{4,12},{6,14},{8,0},{10,2},{12,4},{14,6},{16,24},{18,... | collective-permute-start | bytes 393224 | tf_op jit(solution)/shard_map/ppermute | solution.py:1324
  213.7 2.8 collective-permute-start.41
  213.8 3.5 %collective-permute-start.42 = (bf16[128,3072]{1,0:T(8,128)(2,1)S(1)}, bf16[128,3072]{1,0:T(8,128)(2,1)}, u32[]{:S(2)}, u32[]{:S(2)}) collective-permute-start(bf16[128,3072]{1,0:T(8,128)(2,1)S(1)} %collective-permute-done.36.mine_1), channel_id=1, source_target_pairs={{0,2},{2,0},{4,6},{6,4},{8,10},{10,8},{12,14},{14,12},{16,18},{18,... | collective-permute-start | bytes 2359304 | tf_op jit(solution)/shard_map/ppermute | solution.py:1324
  214.3 14.8 %collective-permute-start.40 = (bf16[2048,128]{1,0:T(8,128)(2,1)}, bf16[2048,128]{1,0:T(8,128)(2,1)S(1)}, u32[]{:S(2)}, u32[]{:S(2)}) collective-permute-start(bf16[2048,128]{1,0:T(8,128)(2,1)} %get-tuple-element.293), channel_id=1, source_target_pairs={{0,1},{1,0},{2,3},{3,2},{4,5},{5,4},{6,7},{7,6},{8,9},{9,8},{10,11... | collective-permute-start | bytes 1572872 | tf_op jit(solution)/shard_map/ppermute | solution.py:1318
  215.3 9.2 %collective-permute-start.44 = (bf16[1,32,1024]{2,1,0:T(8,128)(2,1)S(1)}, bf16[1,32,1024]{2,1,0:T(8,128)(2,1)S(1)}, u32[]{:S(2)}, u32[]{:S(2)}) collective-permute-start(bf16[1,32,1024]{2,1,0:T(8,128)(2,1)S(1)} %dynamic-slice_convert_fusion.3), channel_id=1, source_target_pairs={{0,16},{2,18},{4,20},{6,22},{8,24},{10,26},{12,28},{14,30},{16,0},... | collective-permute-start | bytes 196616 | tf_op jit(solution)/shard_map/ppermute | solution.py:1324
  223.6 6.2 %collective-permute-start.43 = (f32[12,1024]{1,0:T(8,128)}, f32[12,1024]{1,0:T(8,128)S(1)}, u32[]{:S(2)}, u32[]{:S(2)}) collective-permute-start(f32[12,1024]{1,0:T(8,128)} %get-tuple-element.305), channel_id=1, source_target_pairs={{0,1},{1,0},{2,3},{3,2},{4,5},{5,4},{6,7},{7,6},{8,9},{9,8},{10,11... | collective-permute-start | bytes 147464 | tf_op jit(solution)/shard_map/ppermute | solution.py:1318
  231.7 47.2 %collective-permute-start.52 = (bf16[1024,1024]{1,0:T(8,128)(2,1)}, bf16[1024,1024]{1,0:T(8,128)(2,1)}, u32[]{:S(2)}, u32[]{:S(2)}) collective-permute-start(bf16[1024,1024]{1,0:T(8,128)(2,1)} %constant_dynamic-slice_fusion.7), channel_id=1, source_target_pairs={{0,1},{1,0},{2,3},{3,2},{4,5},{5,4},{6,7},{7,6},{8,9},{9,8},{10,11... | collective-permute-start | bytes 6291464 | tf_op jit(solution)/shard_map/ppermute | solution.py:1318
  232.7 20.8 %collective-permute-start.45 = (bf16[2432,128]{1,0:T(8,128)(2,1)S(1)}, bf16[2432,128]{1,0:T(8,128)(2,1)S(1)}, u32[]{:S(2)}, u32[]{:S(2)}) collective-permute-start(bf16[2432,128]{1,0:T(8,128)(2,1)S(1)} %constant_dynamic-update-slice_fusion.refs_0_), channel_id=1, source_target_pairs={{0,8},{2,10},{8,16},{10,18},{16,24},{18,26},{24,28},{26,30},{28,20... | collective-permute-start | bytes 1867784 | tf_op jit(solution)/shard_map/ppermute | solution.py:1329
  232.8 27.9 %collective-permute-start.46 = (bf16[2432,128]{1,0:T(8,128)(2,1)S(1)}, bf16[2432,128]{1,0:T(8,128)(2,1)}, u32[]{:S(2)}, u32[]{:S(2)}) collective-permute-start(bf16[2432,128]{1,0:T(8,128)(2,1)S(1)} %constant_dynamic-update-slice_fusion.refs_0_), channel_id=1, source_target_pairs={{0,4},{2,6},{8,0},{10,2},{16,8},{18,10},{24,16},{26,18},{28,24},{3... | collective-permute-start | bytes 1867784 | tf_op jit(solution)/shard_map/ppermute | solution.py:1329
  234.8 26.5 %collective-permute-start.49 = (bf16[2432,128]{1,0:T(8,128)(2,1)S(1)}, bf16[2432,128]{1,0:T(8,128)(2,1)}, u32[]{:S(2)}, u32[]{:S(2)}) collective-permute-start(bf16[2432,128]{1,0:T(8,128)(2,1)S(1)} %constant_dynamic-update-slice_fusion.refs_0_), channel_id=1, source_target_pairs={{0,2},{2,0},{4,6},{6,4},{8,10},{10,8},{12,14},{14,12},{16,18},{18,... | collective-permute-start | bytes 1867784 | tf_op jit(solution)/shard_map/ppermute | solution.py:1324
  260.8 3.2 collective-permute-start.50
  260.8 3.3 %collective-permute-start.51 = (bf16[2432,128]{1,0:T(8,128)(2,1)}, bf16[2432,128]{1,0:T(8,128)(2,1)}, u32[]{:S(2)}, u32[]{:S(2)}) collective-permute-start(bf16[2432,128]{1,0:T(8,128)(2,1)} %collective-permute-done.46.refs_4_), channel_id=1, source_target_pairs={{0,2},{2,0},{4,6},{6,4},{8,10},{10,8},{12,14},{14,12},{16,18},{18,... | collective-permute-start | bytes 1867784 | tf_op jit(solution)/shard_map/ppermute | solution.py:1324
  261.3 15.9 %collective-permute-start.47 = (bf16[2432,128]{1,0:T(8,128)(2,1)S(1)}, bf16[2432,128]{1,0:T(8,128)(2,1)S(1)}, u32[]{:S(2)}, u32[]{:S(2)}) collective-permute-start(bf16[2432,128]{1,0:T(8,128)(2,1)S(1)} %collective-permute-done.45.refs_2_), channel_id=1, source_target_pairs={{0,8},{2,10},{8,16},{10,18},{16,24},{18,26},{24,28},{26,30},{28,20... | collective-permute-start | bytes 1867784 | tf_op jit(solution)/shard_map/ppermute | solution.py:1329
  261.3 16.2 %collective-permute-start.48 = (bf16[2432,128]{1,0:T(8,128)(2,1)}, bf16[2432,128]{1,0:T(8,128)(2,1)S(1)}, u32[]{:S(2)}, u32[]{:S(2)}) collective-permute-start(bf16[2432,128]{1,0:T(8,128)(2,1)} %collective-permute-done.46.refs_4_), channel_id=1, source_target_pairs={{0,4},{2,6},{8,0},{10,2},{16,8},{18,10},{24,16},{26,18},{28,24},{3... | collective-permute-start | bytes 1867784 | tf_op jit(solution)/shard_map/ppermute | solution.py:1329
  278.9 10.0 %collective-permute-start.55 = (bf16[1024,1024]{1,0:T(8,128)(2,1)}, bf16[1024,1024]{1,0:T(8,128)(2,1)}, u32[]{:S(2)}, u32[]{:S(2)}) collective-permute-start(bf16[1024,1024]{1,0:T(8,128)(2,1)} %collective-permute-done.52), channel_id=1, source_target_pairs={{0,2},{2,0},{4,6},{6,4},{8,10},{10,8},{12,14},{14,12},{16,18},{18,... | collective-permute-start | bytes 6291464 | tf_op jit(solution)/shard_map/ppermute | solution.py:1324
  278.9 16.4 %collective-permute-start.53 = (bf16[2432,128]{1,0:T(8,128)(2,1)S(1)}, bf16[2432,128]{1,0:T(8,128)(2,1)S(1)}, u32[]{:S(2)}, u32[]{:S(2)}) collective-permute-start(bf16[2432,128]{1,0:T(8,128)(2,1)S(1)} %collective-permute-done.47.refs_0_.refs_6_), channel_id=1, source_target_pairs={{0,8},{2,10},{8,16},{10,18},{16,24},{18,26},{24,28},{26,30},{28,20... | collective-permute-start | bytes 1867784 | tf_op jit(solution)/shard_map/ppermute | solution.py:1329
  279.1 16.5 %collective-permute-start.56 = (bf16[2432,128]{1,0:T(8,128)(2,1)S(1)}, bf16[2432,128]{1,0:T(8,128)(2,1)S(1)}, u32[]{:S(2)}, u32[]{:S(2)}) collective-permute-start(bf16[2432,128]{1,0:T(8,128)(2,1)S(1)} %collective-permute-done.47.refs_0_.refs_6_), channel_id=1, source_target_pairs={{0,2},{2,0},{4,6},{6,4},{8,10},{10,8},{12,14},{14,12},{16,18},{18,... | collective-permute-start | bytes 1867784 | tf_op jit(solution)/shard_map/ppermute | solution.py:1324
  279.4 16.3 %collective-permute-start.54 = (bf16[2432,128]{1,0:T(8,128)(2,1)S(1)}, bf16[2432,128]{1,0:T(8,128)(2,1)S(1)}, u32[]{:S(2)}, u32[]{:S(2)}) collective-permute-start(bf16[2432,128]{1,0:T(8,128)(2,1)S(1)} %collective-permute-done.48.refs_2_.refs_8_), channel_id=1, source_target_pairs={{0,4},{2,6},{8,0},{10,2},{16,8},{18,10},{24,16},{26,18},{28,24},{3... | collective-permute-start | bytes 1867784 | tf_op jit(solution)/shard_map/ppermute | solution.py:1329
  281.2 14.5 %collective-permute-start.57 = (bf16[2432,128]{1,0:T(8,128)(2,1)S(1)}, bf16[2432,128]{1,0:T(8,128)(2,1)S(1)}, u32[]{:S(2)}, u32[]{:S(2)}) collective-permute-start(bf16[2432,128]{1,0:T(8,128)(2,1)S(1)} %collective-permute-done.48.refs_2_.refs_8_), channel_id=1, source_target_pairs={{0,2},{2,0},{4,6},{6,4},{8,10},{10,8},{12,14},{14,12},{16,18},{18,... | collective-permute-start | bytes 1867784 | tf_op jit(solution)/shard_map/ppermute | solution.py:1324
  295.7 2.7 collective-permute-start.58
  295.8 2.9 collective-permute-start.59
  296.3 10.1 %collective-permute-start.60 = (bf16[1216,128]{1,0:T(8,128)(2,1)S(1)}, bf16[1216,128]{1,0:T(8,128)(2,1)S(1)}, u32[]{:S(2)}, u32[]{:S(2)}) collective-permute-start(bf16[1216,128]{1,0:T(8,128)(2,1)S(1)} %slice.128), channel_id=1, source_target_pairs={{0,8},{2,10},{8,16},{10,18},{16,24},{18,26},{24,28},{26,30},{28,20... | collective-permute-start | bytes 933896 | tf_op jit(solution)/shard_map/ppermute | solution.py:1329
  297.7 9.3 %collective-permute-start.61 = (bf16[1216,128]{1,0:T(8,128)(2,1)S(1)}, bf16[1216,128]{1,0:T(8,128)(2,1)S(1)}, u32[]{:S(2)}, u32[]{:S(2)}) collective-permute-start(bf16[1216,128]{1,0:T(8,128)(2,1)S(1)} %slice.129), channel_id=1, source_target_pairs={{0,4},{2,6},{8,0},{10,2},{16,8},{18,10},{24,16},{26,18},{28,24},{3... | collective-permute-start | bytes 933896 | tf_op jit(solution)/shard_map/ppermute | solution.py:1329
  (59 other events, 646.3 us)
Sparse Core Ops, SparseCore 0:
  41.9 51.4 all-gather.5
  115.7 54.1 all-gather.3
  215.4 49.4 all-gather.7
where the time goes:
time: 324 us; the launch traced here: 322 us
  Pallas kernels  100 us (31%)
  waiting for transfers between devices  81 us (25%)
  starting transfers between devices  67.6 us (21%)
  local copies, waits for them, and re-layouts  26.5 us (8%)
  matrix products  16.8 us (5%)
  between operations  16.3 us (5%)
  other arithmetic  13.3 us (4%)
    ppermute x15, waiting for transfers between devices, hop(): lax.ppermute(values, 'ctx', [(2 * order[at] + c, 2 * order[(at + step) %...  38 us
    ppermute x18, waiting for transfers between devices, across(): return lax.ppermute(values, 'fsdp', [(0, 1), (1, 0)])  27 us
    pallas_call x1, Pallas kernels, attend_back(): pl.pallas_call(functools.partial(attend_back_kernel, chunk, rows, head_si...  19 us
    ppermute x18, starting transfers between devices, across(): return lax.ppermute(values, 'fsdp', [(0, 1), (1, 0)])  18.1 us
    ppermute x15, starting transfers between devices, hop(): lax.ppermute(values, 'ctx', [(2 * order[at] + c, 2 * order[(at + step) %...  16.8 us
    pallas_call x3, Pallas kernels, expand_wide(): pl.pallas_call(functools.partial(wide_kernel, first, len(parts)), in_spec...  14.4 us
    pallas_call x2, Pallas kernels, project_chunks(): pl.pallas_call(functools.partial(project_chunks_kernel, rows, head_size,...  13.7 us
    pallas_call x1, Pallas kernels, attend(): pl.pallas_call(functools.partial(attend_kernel, chunk, rows), grid_spec=g...  12.9 us
  transfers between devices with their start and end apart: 69, of which 25 were waited for; matrix products, arithmetic and copies ran while one was open for 15% of the time, Pallas kernels for 30%

commit v1 on v0

--- a/solution.py
+++ b/solution.py
@@ -117,7 +117,7 @@
     row_id = lax.broadcasted_iota(jnp.int32, (spare, block), 0)
     same = row_id == seg_row
     used = row_id <= seq_count
-    key_tail = jnp.where(same & used, 1.0, 0.0)
+    key_tail = jnp.where((same & used) | ((row_id >= 8) & (row_id < 11)), 1.0, 0.0)
     query_tail = jnp.where(used & jnp.logical_not(same), NEGATIVE, 0.0)
     query_t_ref[...] = jnp.concatenate([query, query_tail], axis=0).astype(BF16)
     key_t_ref[...] = key.astype(BF16)
@@ -127,37 +127,43 @@
 
 
 def attend_kernel(
-    chunk, rows, place_ref, query_ref, key_ref, value_ref, out_ref, sent_ref, lse_ref, score_ref,
+    chunk, rows, place_ref, query_ref, key_ref, value_ref, out_ref, sent_ref, lse_ref, score_ref, top_ref,
 ):
     core = place_ref[0] % 2
     count = key_ref.shape[0]
+    step = pl.program_id(0)
+    now = step % 2
+    before = 1 - now
     query = query_ref[...]
+    last_top = top_ref[before]
     top = None
+    total = jnp.zeros_like(last_top)
+    out = jnp.zeros(out_ref.shape, F32)
     for at in range(0, count, chunk):
-        score = jnp.dot(key_ref[at : at + chunk, :], query, preferred_element_type=F32)
-        score_ref[at : at + chunk, :] = score
+        part = slice(at, at + chunk)
+        score = jnp.dot(key_ref[part, :], query, preferred_element_type=F32)
+        weight = jnp.exp(score_ref[before, part, :] - last_top)
+        score_ref[now, part, :] = score
         high = jnp.max(score, axis=0, keepdims=True)
         top = high if top is None else jnp.maximum(top, high)
-    total = jnp.zeros_like(top)
-    out = jnp.zeros(out_ref.shape, F32)
-    for at in range(0, count, chunk):
-        weight = jnp.exp(score_ref[at : at + chunk, :] - top)
         total = total + jnp.sum(weight, axis=0, keepdims=True)
         out = out + jnp.dot(
-            value_ref[:, at : at + chunk],
-            weight.astype(BF16),
-            preferred_element_type=F32,
+            value_ref[:, part], weight.astype(BF16), preferred_element_type=F32
         )
-    out = out / total
-    out_ref[...] = out
-    for at in range(sent_ref.shape[0]):
-        sent_ref[at ^ core] = out[:, at * rows : (at + 1) * rows].astype(BF16)
-    lse_ref[...] = top + jnp.log(total)
+    top_ref[now] = top
+
+    @pl.when(step > 0)
+    def _():
+        result = out / total
+        out_ref[...] = result
+        for at in range(sent_ref.shape[0]):
+            sent_ref[at ^ core] = result[:, at * rows : (at + 1) * rows].astype(BF16)
+        lse_ref[...] = last_top + jnp.log(total)
 
 
 def attend_back_kernel(
     chunk, rows, head_size, place_ref, query_ref, grad_ref, out_ref, lse_ref, key_ref, key_t_ref, pair_ref,
-    pair_block_ref, cos_block_ref, sin_block_ref, cos_ref, sin_ref, mixed_ref, sent_ref, key_acc, value_acc,
+    pair_block_ref, cos_block_ref, sin_block_ref, cos_ref, sin_ref, mixed_ref, sent_ref, acc_ref,
 ):
     step = pl.program_id(0)
     core = place_ref[0] % 2
@@ -169,34 +175,40 @@
 
     @pl.when(step == 0)
     def _():
-        key_acc[...] = jnp.zeros_like(key_acc)
-        value_acc[...] = jnp.zeros_like(value_acc)
-
-    query = query_ref[...]
+        acc_ref[...] = jnp.zeros_like(acc_ref)
+
+    rest = -lse_ref[...]
+    query = query_ref[...].astype(F32)
+    row_id = lax.broadcasted_iota(jnp.int32, query.shape, 0)
+    for k in range(3):
+        piece = rest.astype(BF16).astype(F32)
+        query = jnp.where(row_id == head_size + 8 + k, piece, query)
+        rest = rest - piece
+    query = query.astype(BF16)
     grad = jnp.concatenate(
         [grad_ref[at ^ core] for at in range(per_step)], axis=1
     ).astype(F32)
     delta = jnp.sum(grad * out_ref[...], axis=0, keepdims=True)
-    lse = lse_ref[...]
-    grad_t = jnp.concatenate(
-        [grad, jnp.zeros((128 - head_size, block), F32)], axis=0
-    )
-    grad_rows = grad_t.T.astype(BF16)
+    grad_t = jnp.concatenate([grad, jnp.zeros((128 - head_size, block), F32)], axis=0)
+    pair = pair_block_ref[...]
+    lane = lax.broadcasted_iota(jnp.int32, pair.shape, 1)
+    queries = jnp.where(lane >= head_size, pair.astype(F32), 0.0).astype(BF16)
+    both = jnp.concatenate([queries, grad_t.T.astype(BF16)], axis=0)
     grad_t = grad_t.astype(BF16)
-    pair = pair_block_ref[...]
     grad_query = jnp.zeros((head_size, block), F32)
     for at in range(0, count, chunk):
         part = slice(at, at + chunk)
         score = jnp.dot(key_ref[part, :], query, preferred_element_type=F32)
-        prob = jnp.exp(score - lse)
+        prob = jnp.exp(score)
         grad_prob = jnp.dot(pair_ref[part, :], grad_t, preferred_element_type=F32)
         grad_score = (prob * (grad_prob - delta)).astype(BF16)
         grad_query = grad_query + jnp.dot(
             key_t_ref[:, part], grad_score, preferred_element_type=F32
         )
-        key_acc[part, :] += jnp.dot(grad_score, pair, preferred_element_type=F32)
-        value_acc[part, :] += jnp.dot(
-            prob.astype(BF16), grad_rows, preferred_element_type=F32
+        acc_ref[part, :] += jnp.dot(
+            jnp.concatenate([grad_score, prob.astype(BF16)], axis=1),
+            both,
+            preferred_element_type=F32,
         )
 
     def turn_back(values, cos, sin):
@@ -218,14 +230,13 @@
 
     @pl.when(step == pl.num_programs(0) - 1)
     def _():
-        key_part = turn_back(
-            key_acc[...].T[head_size : 2 * head_size], cos_ref[...], sin_ref[...]
-        )
-        value_part = value_acc[...].T[:head_size].astype(BF16)
-        both = jnp.concatenate([key_part, value_part], axis=0)
-        mixed_ref[head_size : 3 * head_size, :] = both
+        acc = acc_ref[...].T
+        key_part = turn_back(acc[head_size : 2 * head_size], cos_ref[...], sin_ref[...])
+        value_part = acc[:head_size].astype(BF16)
+        parts = jnp.concatenate([key_part, value_part], axis=0)
+        mixed_ref[head_size : 3 * head_size, :] = parts
         for k in range(count // rows):
-            sent_ref[place_ref[k], head_size : 3 * head_size, :] = both[
+            sent_ref[place_ref[k], head_size : 3 * head_size, :] = parts[
                 :, k * rows : (k + 1) * rows
             ]
 
@@ -374,22 +385,30 @@
     head_size = value_t.shape[0]
     block = min(count, 2 * rows)
     chunk = min(count, 512)
+    blocks = count // block
+
+    def before(i):
+        return jnp.maximum(i - 1, 0)
+
     grid_spec = pltpu.PrefetchScalarGridSpec(
         num_scalar_prefetch=1,
-        grid=(count // block,),
+        grid=(blocks + 1,),
         in_specs=[
-            pl.BlockSpec((128, block), lambda i, _: (0, i)),
+            pl.BlockSpec((128, block), lambda i, _: (0, jnp.minimum(i, blocks - 1))),
             whole((count, 128)),
             whole((head_size, count)),
         ],
         out_specs=[
-            pl.BlockSpec((head_size, block), lambda i, _: (0, i)),
+            pl.BlockSpec((head_size, block), lambda i, _: (0, before(i))),
             pl.BlockSpec(
-                (2, head_size, rows), lambda i, place: (place[2 * i] // 2, 0, 0)
+                (2, head_size, rows), lambda i, place: (place[2 * before(i)] // 2, 0, 0)
             ),
-            pl.BlockSpec((1, block), lambda i, _: (0, i)),
-        ],
-        scratch_shapes=[pltpu.VMEM((count, block), F32)],
+            pl.BlockSpec((1, block), lambda i, _: (0, before(i))),
+        ],
+        scratch_shapes=[
+            pltpu.VMEM((2, count, block), F32),
+            pltpu.VMEM((2, 1, block), F32),
+        ],
     )
     return pl.pallas_call(
         functools.partial(attend_kernel, chunk, rows),
@@ -438,7 +457,7 @@
             whole((3 * head_size, count)),
             whole((count // rows, 3 * head_size, rows)),
         ],
-        scratch_shapes=[pltpu.VMEM((count, 128), F32), pltpu.VMEM((count, 128), F32)],
+        scratch_shapes=[pltpu.VMEM((count, 128), F32)],
     )
     return pl.pallas_call(
         functools.partial(attend_back_kernel, chunk, rows, head_size),
@@ -1428,8 +1447,6 @@
     grad_y = cotangent[0].astype(F32) * live
     grad_y_b = grad_y.astype(BF16)
     out_half = w_out.shape[0] // 2
-    me_1 = after(me, packed)
-    out_mine = across(cut(w_out, (me_1 % 2) * out_half, out_half, 0))
     tok_new, (packed_other, w_head, cos, sin, grad_y_b, me_2, place, who, base, w_head_other) = fenced(
         [tok_new, [packed_other, w_head, cos, sin, grad_y_b, me, place, who, base, w_head_other]]
     )
@@ -1463,9 +1480,7 @@
         lax.dynamic_slice(w_up, (p * up_deep, (me_2 % 4) * quarter), (up_deep, quarter))
         for p in range(up_parts)
     ]
-    tok_new, (gains, shifts, out_mine), up_send = fenced(
-        [tok_new, [gains, shifts, out_mine], up_send]
-    )
+    tok_new, (gains, shifts), up_send = fenced([tok_new, [gains, shifts], up_send])
     tok_flips = with_flips(tok.parts)
     tok.came(tok_new)
 
@@ -1481,6 +1496,7 @@
     )
 
     up_mine.append(across(up_send[1]))
+    far_send = dims(grad_y_other, w_down, 1, 1).astype(BF16)
     all_norm, query_t, key, key_t, value_t, pair = project_chunks(
         who, with_flips(tok_last), *constants, first=chips - 1, earlier=head_values
     )
@@ -1488,8 +1504,8 @@
     rest = jnp.concatenate(
         [v[None, :] for v in (gain_two, bias_two, bias_down, bias_up)], axis=1
     )
-    out_t, sent, lse, *up_mine, rest, me_5, grad_y_other = fence(
-        out_t, sent, lse, *up_mine, rest, me, grad_y_other
+    out_t, sent, lse, *up_mine, rest, me_5, far_send = fence(
+        out_t, sent, lse, *up_mine, rest, me, far_send
     )
 
     attended = lax.all_to_all(sent, "ctx", 0, 0, tiled=True)
@@ -1500,22 +1516,22 @@
         cut(w_qkv, (me_5 % 2) * qkv_half + k * (qkv_half // 2), qkv_half // 2, 0)
         for k in range(2)
     ]
-    qkv_mine = [across(qkv_send[0])]
-    far_grad = across(dims(grad_y_other, w_down, 1, 1).astype(BF16))
+    out_mine = across(cut(w_out, (me_5 % 2) * out_half, out_half, 0))
+    far_grad = across(far_send)
     near_grad = dims(after(grad_y_b, lse), w_down, 1, 1)
-    out_pieces = (w_out, out_mine, flip(out_mine))
     pieces = [with_flips([v]) for v in up_mine]
-    rest_5 = [rest_other, me_5, qkv_send[1], qkv_mine[0]]
+    rest_5 = [out_mine, rest_other, me_5, qkv_send[1], qkv_send[0]]
     (attended, up_side[0], near_grad), rest_5, *pieces = fenced(
         [[attended, up_side[0], near_grad], rest_5, *pieces]
     )
-    rest_other, me_6, qkv_send[1], qkv_mine[0] = rest_5
+    out_mine, rest_other, me_6, qkv_send[1], qkv_send[0] = rest_5
 
     rest = by_shard(rest, rest_other, 0)
     gain_second = vector_of(rest, 0, half)
     bias_second = vector_of(rest, half, half)
     bias_output = vector_of(rest, width, half)
     bias_hidden = vector_of(rest, width + half, hidden // 2)
+    out_pieces = (w_out, out_mine, flip(out_mine))
     resid, normal_two, scale_two, norm_two_b = middle(
         who, attended, out_pieces, own_tokens, gain_second, bias_second
     )
@@ -1547,7 +1563,7 @@
 
     grad_att = grad_att.reshape(HEADS, head_size, rows)
     grad_att = lax.all_to_all(grad_att, "ctx", 0, 0, tiled=True)
-    qkv_mine.append(across(after(qkv_send[1], up_other, down_other)))
+    qkv_mine = [across(after(qkv_send[0], up_other, down_other))]
     deep = width // (ctx_size * fsdp_size)
     out_part = jnp.dot(
         attended.reshape(width, rows), grad_resid_b, preferred_element_type=F32
@@ -1559,11 +1575,12 @@
     grad_att, down_send, out_part = fence(grad_att, down_send, out_part)
 
     out_part = halve(out_part, 1, shard, across)
+    qkv_mine.append(across(after(qkv_send[1], out_part)))
     mixed, mixed_sent = attend_back(
         place, query_t, grad_att, out_t, lse, key, key_t, pair, cos, sin, rows
     )
-    mixed, mixed_sent, out_part, qkv_mine[1] = fence(
-        mixed, mixed_sent, out_part, qkv_mine[1]
+    mixed, mixed_sent, out_part, qkv_mine[0] = fence(
+        mixed, mixed_sent, out_part, qkv_mine[0]
     )
 
     mixed_got = lax.all_to_all(mixed_sent, "ctx", 0, 0, tiled=True)

time: 324 us -> 316 us (0.975)
  waiting for transfers between devices: 81 us -> 72.1 us
    ppermute x18, waiting for transfers between devices: 27 us -> 18.2 us  [across(): return lax.ppermute(values, 'fsdp', [(0, 1), (1, 0)])]
    ppermute x15, waiting for transfers between devices: 38 us -> 41.9 us  [hop(): lax.ppermute(values, 'ctx', [(2 * order[at] + c, 2 * order[(at + step) %...]
    unnamed x130 -> x126, local copies, waits for them, and re-layouts: 10.4 us -> 9.76 us
  transfers between devices with their start and end apart: 69 -> 69, of which waited for: 25 -> 24; matrix products, arithmetic and copies ran while one was open for 15% -> 15% of each run, Pallas kernels for 30% -> 30%
where the time goes in v1:
time: 316 us; the launch traced here: 315 us
  Pallas kernels  101 us (32%)
  waiting for transfers between devices  72.1 us (23%)
  starting transfers between devices  70.2 us (22%)
  local copies, waits for them, and re-layouts  25.3 us (8%)
  matrix products  16.6 us (5%)
  between operations  16.3 us (5%)
  other arithmetic  13.3 us (4%)
    ppermute x15, waiting for transfers between devices, hop(): lax.ppermute(values, 'ctx', [(2 * order[at] + c, 2 * order[(at + step) %...  41.9 us
    ppermute x18, starting transfers between devices, across(): return lax.ppermute(values, 'fsdp', [(0, 1), (1, 0)])  19.8 us
    pallas_call x1, Pallas kernels, attend_back(): pl.pallas_call(functools.partial(attend_back_kernel, chunk, rows, head_si...  18.8 us
    ppermute x18, waiting for transfers between devices, across(): return lax.ppermute(values, 'fsdp', [(0, 1), (1, 0)])  18.2 us
    ppermute x15, starting transfers between devices, hop(): lax.ppermute(values, 'ctx', [(2 * order[at] + c, 2 * order[(at + step) %...  16.8 us
    pallas_call x3, Pallas kernels, expand_wide(): pl.pallas_call(functools.partial(wide_kernel, first, len(parts)), in_spec...  14.4 us
    pallas_call x2, Pallas kernels, project_chunks(): pl.pallas_call(functools.partial(project_chunks_kernel, rows, head_size,...  14.2 us
    ppermute x30, starting transfers between devices, flip(): lax.ppermute(values, 'ctx', [(i, i ^ 1 << bit) for i in range(ctx_size)])  13.4 us
  transfers between devices with their start and end apart: 69, of which 24 were waited for; matrix products, arithmetic and copies ran while one was open for 15% of the time, Pallas kernels for 30%

profile of v1, /device:TPU:0, one launch (start us, length us, event | category | flops | bytes accessed | tf_op | source)
XLA Modules:
  0.0 314.5 jit_solution(17820793767604986707)
XLA Ops:
  7.3 3.1 collective-permute-start
  11.1 1.2 fusion.27.place_ref
  17.2 1.8 fusion.5.refs_14_
  19.0 2.0 collective-permute-start.4
  21.0 1.6 collective-permute-start.2
  23.2 1.8 multiply_sine_fusion
  25.0 4.7 %collective-permute-done.5.refs_17_.refs_5_ = bf16[512,192]{1,0:T(8,128)(2,1)S(1)} collective-permute-done((bf16[512,192]{1,0:T(8,128)(2,1)S(1)}, bf16[512,192]{1,0:T(8,128)(2,1)S(1)}, u32[]{:S(2)}, u32[]{:S(2)}) %collective-permute-start.5) | collective-permute-done | bytes 196640 | tf_op jit(solution)/shard_map/ppermute | solution.py:1337
  30.7 1.7 collective-permute-start.11
  32.7 1.3 constant_dynamic-slice_fusion.22
  34.7 2.6 collective-permute-done.11.refs_10_
  37.3 1.8 collective-permute-done.12.refs_12_
  42.0 1.5 collective-permute-start.17
  43.6 1.6 collective-permute-start.16
  45.8 10.8 %project_chunks.2 = (bf16[2048,1024]{1,0:T(8,128)(2,1)}, bf16[128,2048]{1,0:T(8,128)(2,1)}, bf16[2048,128]{1,0:T(8,128)(2,1)}, bf16[64,2048]{1,0:T(8,128)(2,1)},...) custom-call(s32[2]{0:T(128)} %pad_add_fusion.who_ref, s32[1]{0:T(128)} %bitcast.110.ends_ref, s32[16]{0:T(128)} %copy-done.36, ...), custom_call_target="tpu_custom_call" | custom-call | flops 3758096384 | bytes 7340032 | tf_op jit(solution)/shard_map/project_chunks/pallas_call | solution.py:361
  56.7 1.6 collective-permute-start.20
  58.3 1.5 convolution_convert_fusion
  60.6 3.4 %project_chunks.3 = (bf16[2048,1024]{1,0:T(8,128)(2,1)}, bf16[128,2048]{1,0:T(8,128)(2,1)}, bf16[2048,128]{1,0:T(8,128)(2,1)}, bf16[64,2048]{1,0:T(8,128)(2,1)},...) custom-call(s32[2]{0:T(128)} %pad_add_fusion.who_ref, ...), custom_call_target="tpu_custom_call", output_to_operand_aliasing={{0}: (11, {}), {1}: (12, {}), {2}: (13, {}), {3}: (14, {}),... | custom-call | flops 536870912 | bytes 1048576 | tf_op jit(solution)/shard_map/project_chunks/pallas_call | solution.py:361
  64.0 12.6 %attend_head.1 = (f32[64,2048]{1,0:T(8,128)}, bf16[16,64,128]{2,1,0:T(8,128)(2,1)}, f32[1,2048]{1,0:T(1,128)}) custom-call(s32[16]{0:T(128)} %fusion.27.place_ref, bf16[128,2048]{1,0:T(8,128)(2,1)} %get-tuple-element.218.query_ref, bf16[2048,128]{1,0:T(8,128)(2,1)} %get-tuple-element.219.key_ref, bf16[64,2048]{1,0:T(8,128)(2,1)} %get-tuple-element.220.value_ref), custom_call_target="tpu_custom_call" | custom-call | flops 4294967296 | bytes 2097152 | tf_op jit(solution)/shard_map/attend_head/pallas_call | solution.py:413
  78.7 7.7 %all-to-all-start = ((bf16[16,64,128]{2,1,0:T(8,128)(2,1)}), bf16[16,64,128]{2,1,0:T(8,128)(2,1)S(1)}, u32[]{:S(2)}, u32[]{:S(2)}) async-start(bf16[16,64,128]{2,1,0:T(8,128)(2,1)} %get-tuple-element.229), calls=%async_computation | async-start | bytes 524288 | tf_op jit(solution)/shard_map/all_to_all | solution.py:1511
  86.7 2.6 constant_dynamic-slice_fusion.11
  89.7 4.7 %fusion.35.refs_8_ = f32[128,2048]{1,0:T(8,128)} fusion(bf16[128,1024]{1,0:T(8,128)(2,1)S(1)} %copy-done.20, bf16[2048,1024]{1,0:T(8,128)(2,1)} %param.20), kind=kOutput, calls=%fused_computation.135 | convolution fusion | flops 536870912 | bytes 5505024 | tf_op jit(solution)/shard_map/dot_general | solution.py:22
  94.4 1.9 collective-permute-start.28
  96.3 1.7 collective-permute-start.27
  102.8 3.6 %output_projection.1 = (f32[128,1024]{1,0:T(8,128)}, f32[128,1024]{1,0:T(8,128)}, f32[128,1]{1,0:T(8,128)}, bf16[128,1024]{1,0:T(8,128)(2,1)}) custom-call(s32[2]{0:T(128)} %pad_add_fusion.who_ref, bf16[16,64,128]{2,1,0:T(8,128)(2,1)} %copy-done.23, bf16[512,1024]{1,0:T(8,128)(2,1)} %refs_15_.1, bf16[256,1024]{1,0:T(8,128)(2,1)} %copy-done.41, ...), custom_call_target="tpu_custom_call" | custom-call | flops 1073741824 | bytes 4194304 | tf_op jit(solution)/shard_map/output_projection/pallas_call | solution.py:606
  106.4 3.4 %collective-permute-done.27.refs_9_ = bf16[128,2048]{1,0:T(8,128)(2,1)} collective-permute-done((bf16[128,2048]{1,0:T(8,128)(2,1)S(1)}, bf16[128,2048]{1,0:T(8,128)(2,1)}, u32[]{:S(2)}, u32[]{:S(2)}) %collective-permute-start.27) | collective-permute-done | bytes 524320 | tf_op jit(solution)/shard_map/ppermute | solution.py:1337
  110.6 1.7 collective-permute-start.32
  113.5 11.1 %feed_forward.1 = (bf16[128,4096]{1,0:T(8,128)(2,1)}, f32[128,1024]{1,0:T(8,128)}, bf16[128,1024]{1,0:T(8,128)(2,1)}, bf16[16,64,128]{2,1,0:T(8,128)(2,1)}, f32[8,1024]{1,0:T(8,128)}) custom-call(s32[2]{0:T(128)} %pad_add_fusion.who_ref, bf16[128,1024]{1,0:T(8,128)(2,1)} %get-tuple-element.247.norm_ref, bf16[512,4096]{1,0:T(8,128)(2,1)} %own_ref.4, ...), custom_call_target="tpu_custom_call" | custom-call | flops 8589934592 | bytes 16777216 | tf_op jit(solution)/shard_map/feed_forward/pallas_call | solution.py:694
  124.9 1.7 fusion.8
  126.6 2.0 copy-done.4
  128.9 4.8 %all-to-all-start.1 = ((bf16[16,64,128]{2,1,0:T(8,128)(2,1)}), bf16[16,64,128]{2,1,0:T(8,128)(2,1)}, u32[]{:S(2)}, u32[]{:S(2)}) async-start(bf16[16,64,128]{2,1,0:T(8,128)(2,1)} %get-tuple-element.265), calls=%async_computation.1 | async-start | bytes 524288 | tf_op jit(solution)/shard_map/all_to_all | solution.py:1565
  134.4 1.7 collective-permute-start.35
  136.1 3.7 %constant_dynamic-slice_fusion.7 = bf16[1024,1024]{1,0:T(8,128)(2,1)} fusion(bf16[2048,1024]{1,0:T(8,128)(2,1)} %param.20, s32[]{:T(128)S(6)} %select_n.213), kind=kLoop, calls=%fused_computation.78 | loop fusion | bytes 4194308 | tf_op jit(solution)/shard_map/dynamic_slice | solution.py:1364
  139.9 1.6 bitcast_add_fusion
  141.4 4.7 %all-to-all-done.1.grad_ref = bf16[16,64,128]{2,1,0:T(8,128)(2,1)} async-done(((bf16[16,64,128]{2,1,0:T(8,128)(2,1)}), bf16[16,64,128]{2,1,0:T(8,128)(2,1)}, u32[]{:S(2)}, u32[]{:S(2)}) %all-to-all-start.1) | async-done | bytes 262176 | tf_op jit(solution)/shard_map/all_to_all | solution.py:1565
  146.2 2.0 collective-permute-start.34
  148.1 18.8 %attend_head_back.1 = (bf16[192,2048]{1,0:T(8,128)(2,1)}, bf16[16,192,128]{2,1,0:T(8,128)(2,1)}) custom-call(s32[16]{0:T(128)} %fusion.27.place_ref, bf16[128,2048]{1,0:T(8,128)(2,1)} %get-tuple-element.218.query_ref, bf16[16,64,128]{2,1,0:T(8,128)(2,1)} %all-to-all-done.1.grad_ref, f32[64,2048]{1,0:T(8,128)} %get-tuple-element.269.out_ref, ...), custom_call_target="tpu_custom_call" | custom-call | flops 10737418240 | bytes 4194304 | tf_op jit(solution)/shard_map/attend_head_back/pallas_call | solution.py:462
  168.1 7.2 %all-to-all-start.2 = ((bf16[16,192,128]{2,1,0:T(8,128)(2,1)}), bf16[16,192,128]{2,1,0:T(8,128)(2,1)S(1)}, u32[]{:S(2)}, u32[]{:S(2)}) async-start(bf16[16,192,128]{2,1,0:T(8,128)(2,1)} %get-tuple-element.289), calls=%async_computation.2 | async-start | bytes 1572864 | tf_op jit(solution)/shard_map/all_to_all | solution.py:1586
  175.6 3.4 %fusion.36 = f32[192,1024]{1,0:T(8,128)S(1)} fusion(bf16[192,2048]{1,0:T(8,128)(2,1)} %get-tuple-element.279, bf16[2048,1024]{1,0:T(8,128)(2,1)} %get-tuple-element.280), kind=kOutput, calls=%fused_computation.136 | convolution fusion | flops 805306368 | bytes 5767168 | tf_op jit(solution)/shard_map/dot_general | solution.py:1587
  179.4 2.0 collective-permute-start.37
  181.9 1.8 collective-permute-start.40
  183.7 3.1 collective-permute-done.36
  187.6 3.5 %collective-permute-done.37 = bf16[4,32,1024]{2,1,0:T(8,128)(2,1)S(1)} collective-permute-done((bf16[4,32,1024]{2,1,0:T(8,128)(2,1)S(1)}, bf16[4,32,1024]{2,1,0:T(8,128)(2,1)S(1)}, u32[]{:S(2)}, u32[]{:S(2)}) %collective-permute-start.37) | collective-permute-done | bytes 262176 | tf_op jit(solution)/shard_map/ppermute | solution.py:1343
  191.2 3.1 collective-permute-start.38
  194.2 11.9 %weight_slices.1 = (f32[2048,128]{1,0:T(8,128)}, bf16[2048,128]{1,0:T(8,128)(2,1)}) custom-call(s32[2]{0:T(128)} %pad_add_fusion.who_ref, bf16[2048,1024]{1,0:T(8,128)(2,1)} %all-gather.4.cloned.1.call-done.norm_ref, bf16[2048,1024]{1,0:T(8,128)(2,1)} %all-gather.6.cloned.1.call-done.grad_ref, bf16[512,256]{1,0:T(8,128)(2,1)} %get-tuple-element.285.up_own, ...), custom_call_target="tpu_custom_call" | custom-call | flops 4294967296 | bytes 12582912 | tf_op jit(solution)/shard_map/weight_slices/pallas_call | solution.py:533
  207.9 1.5 collective-permute-start.44
  210.3 6.3 %first_norm_back.1 = (bf16[128,1024]{1,0:T(8,128)(2,1)}, f32[12,1024]{1,0:T(8,128)}) custom-call(s32[2]{0:T(128)} %pad_add_fusion.who_ref, s32[1]{0:T(128)} %bitcast.112.ends_ref, bf16[16,192,128]{2,1,0:T(8,128)(2,1)} %copy-done.11, bf16[512,3072]{1,0:T(8,128)(2,1)} %own_ref.5, bf16[128,3072]{1,0:T(8,128)(2,1)} %copy-done.26, ...), custom_call_target="tpu_custom_call" | custom-call | flops 1610612736 | bytes 8388608 | tf_op jit(solution)/shard_map/first_norm_back/pallas_call | solution.py:762
  217.4 4.2 %collective-permute-done.39 = bf16[2048,128]{1,0:T(8,128)(2,1)S(1)} collective-permute-done((bf16[2048,128]{1,0:T(8,128)(2,1)}, bf16[2048,128]{1,0:T(8,128)(2,1)S(1)}, u32[]{:S(2)}, u32[]{:S(2)}) %collective-permute-start.39) | collective-permute-done | bytes 524320 | tf_op jit(solution)/shard_map/ppermute | solution.py:1337
  225.4 2.0 collective-permute-start.46
  227.4 19.4 %collective-permute-done.45.refs_2_ = bf16[2432,128]{1,0:T(8,128)(2,1)S(1)} collective-permute-done((bf16[2432,128]{1,0:T(8,128)(2,1)S(1)}, bf16[2432,128]{1,0:T(8,128)(2,1)S(1)}, u32[]{:S(2)}, u32[]{:S(2)}) %collective-permute-start.45) | collective-permute-done | bytes 622624 | tf_op jit(solution)/shard_map/ppermute | solution.py:1348
  246.7 6.1 %collective-permute-done.46.refs_4_ = bf16[2432,128]{1,0:T(8,128)(2,1)} collective-permute-done((bf16[2432,128]{1,0:T(8,128)(2,1)S(1)}, bf16[2432,128]{1,0:T(8,128)(2,1)}, u32[]{:S(2)}, u32[]{:S(2)}) %collective-permute-start.46) | collective-permute-done | bytes 622624 | tf_op jit(solution)/shard_map/ppermute | solution.py:1348
  253.3 2.0 collective-permute-start.48
  256.2 5.1 %expand_wide.3 = (f32[512,4096]{1,0:T(8,128)}, f32[2048,1024]{1,0:T(8,128)}, f32[512,1024]{1,0:T(8,128)}) custom-call(s32[16]{0:T(128)} %fusion.27.place_ref, bf16[2432,128]{1,0:T(8,128)(2,1)} %copy-done.6, bf16[2432,128]{1,0:T(8,128)(2,1)} %collective-permute-done.49.refs_1_, bf16[2432,128]{1,0:T(8,128)(2,1)} %copy-done.19, ...), custom_call_target="tpu_custom_call" | custom-call | flops 1867776 | bytes 11206656 | tf_op jit(solution)/shard_map/expand_wide/pallas_call | solution.py:936
  261.3 8.0 %collective-permute-done.47.refs_0_.refs_6_ = bf16[2432,128]{1,0:T(8,128)(2,1)S(1)} collective-permute-done((bf16[2432,128]{1,0:T(8,128)(2,1)S(1)}, bf16[2432,128]{1,0:T(8,128)(2,1)S(1)}, u32[]{:S(2)}, u32[]{:S(2)}) %collective-permute-start.47) | collective-permute-done | bytes 622624 | tf_op jit(solution)/shard_map/ppermute | solution.py:1348
  269.6 1.8 collective-permute-done.52
  271.8 1.7 collective-permute-start.54
  273.6 5.4 %expand_last.1 = f32[512,3072]{1,0:T(8,128)} custom-call(bf16[16,192,512]{2,1,0:T(8,128)(2,1)} %bitcast.115), custom_call_target="tpu_custom_call" | custom-call | flops 1572864 | bytes 9437184 | tf_op jit(solution)/shard_map/expand_last/pallas_call | solution.py:977
  279.1 2.2 fusion.12
  281.3 2.1 fusion.10
  285.0 2.8 collective-permute-done.53.refs_4_.refs_10_
  288.7 1.8 collective-permute-start.60
  292.4 6.3 %expand_wide.4 = (f32[512,4096]{1,0:T(8,128)}, f32[2048,1024]{1,0:T(8,128)}, f32[512,1024]{1,0:T(8,128)}) custom-call(s32[16]{0:T(128)} %fusion.27.place_ref, bf16[2432,128]{1,0:T(8,128)(2,1)} %copy-done.12, bf16[2432,128]{1,0:T(8,128)(2,1)} %copy-done.14, ...), custom_call_target="tpu_custom_call", output_to_operand_aliasing={{0}: (9, {}), {1}: (10, {}), {2}: (11, {})} | custom-call | flops 2490368 | bytes 14942208 | tf_op jit(solution)/shard_map/expand_wide/pallas_call | solution.py:936
  299.7 2.0 collective-permute-done.62.refs_1_.refs_15_
  302.6 2.4 small_gradients.1
  304.9 3.0 expand_wide.5
  (285 shorter events, 40.4 us)
Async XLA Ops:
  7.2 183.9 %all-gather.6.cloned.1.call-start = ((), (), s32[]{:S(2)}) async-start(), calls=%async_computation.4 | async-start | bytes 4456448 | tf_op jit(solution)/shard_map/all_gather | solution.py:1340
  7.3 11.7 %collective-permute-start = (bf16[128,1024]{1,0:T(8,128)(2,1)}, bf16[128,1024]{1,0:T(8,128)(2,1)S(1)}, u32[]{:S(2)}, u32[]{:S(2)}) collective-permute-start(bf16[128,1024]{1,0:T(8,128)(2,1)} %bitcast.119), channel_id=1, source_target_pairs={{0,8},{2,10},{8,16},{10,18},{16,24},{18,26},{24,28},{26,30},{28,20... | collective-permute-start | bytes 786440 | tf_op jit(solution)/shard_map/ppermute | solution.py:1348
  10.4 8.6 %collective-permute-start.1 = (bf16[128,1024]{1,0:T(8,128)(2,1)}, bf16[128,1024]{1,0:T(8,128)(2,1)S(1)}, u32[]{:S(2)}, u32[]{:S(2)}) collective-permute-start(bf16[128,1024]{1,0:T(8,128)(2,1)} %bitcast.120), channel_id=1, source_target_pairs={{0,4},{2,6},{8,0},{10,2},{16,8},{18,10},{24,16},{26,18},{28,24},{3... | collective-permute-start | bytes 786440 | tf_op jit(solution)/shard_map/ppermute | solution.py:1348
  19.0 6.0 %collective-permute-start.4 = (bf16[1,1026]{1,0:T(2,128)(2,1)S(1)}, bf16[1,1026]{1,0:T(2,128)(2,1)S(1)}, u32[]{:S(2)}, u32[]{:S(2)}) collective-permute-start(bf16[1,1026]{1,0:T(2,128)(2,1)S(1)} %concatenate.53), channel_id=1, source_target_pairs={{0,1},{1,0},{2,3},{3,2},{4,5},{5,4},{6,7},{7,6},{8,9},{9,8},{10,11... | collective-permute-start | bytes 6164 | tf_op jit(solution)/shard_map/ppermute | solution.py:1337
  21.0 8.7 %collective-permute-start.2 = (bf16[128,1024]{1,0:T(8,128)(2,1)S(1)}, bf16[128,1024]{1,0:T(8,128)(2,1)}, u32[]{:S(2)}, u32[]{:S(2)}) collective-permute-start(bf16[128,1024]{1,0:T(8,128)(2,1)S(1)} %collective-permute-done.refs_2_), channel_id=1, source_target_pairs={{0,8},{2,10},{8,16},{10,18},{16,24},{18,26},{24,28},{26,30},{28,20... | collective-permute-start | bytes 786440 | tf_op jit(solution)/shard_map/ppermute | solution.py:1348
  22.6 7.1 %collective-permute-start.3 = (bf16[128,1024]{1,0:T(8,128)(2,1)S(1)}, bf16[128,1024]{1,0:T(8,128)(2,1)}, u32[]{:S(2)}, u32[]{:S(2)}) collective-permute-start(bf16[128,1024]{1,0:T(8,128)(2,1)S(1)} %collective-permute-done.1.refs_4_), channel_id=1, source_target_pairs={{0,4},{2,6},{8,0},{10,2},{16,8},{18,10},{24,16},{26,18},{28,24},{3... | collective-permute-start | bytes 786440 | tf_op jit(solution)/shard_map/ppermute | solution.py:1348
  23.0 6.6 %collective-permute-start.5 = (bf16[512,192]{1,0:T(8,128)(2,1)S(1)}, bf16[512,192]{1,0:T(8,128)(2,1)S(1)}, u32[]{:S(2)}, u32[]{:S(2)}) collective-permute-start(bf16[512,192]{1,0:T(8,128)(2,1)S(1)} %pad_maximum_fusion.refs_16_.refs_4_), channel_id=1, source_target_pairs={{0,1},{1,0},{2,3},{3,2},{4,5},{5,4},{6,7},{7,6},{8,9},{9,8},{10,11... | collective-permute-start | bytes 589832 | tf_op jit(solution)/shard_map/ppermute | solution.py:1337
  30.2 3.9 %collective-permute-start.13 = (f32[1,2048]{1,0:T(1,128)S(1)}, f32[1,2048]{1,0:T(1,128)S(1)}, u32[]{:S(2)}, u32[]{:S(2)}) collective-permute-start(f32[1,2048]{1,0:T(1,128)S(1)} %constant_dynamic-slice_fusion.16), channel_id=1, source_target_pairs={{0,1},{1,0},{2,3},{3,2},{4,5},{5,4},{6,7},{7,6},{8,9},{9,8},{10,11... | collective-permute-start | bytes 24584 | tf_op jit(solution)/shard_map/ppermute | solution.py:1337
  30.7 6.6 %collective-permute-start.11 = (bf16[128,1024]{1,0:T(8,128)(2,1)}, bf16[128,1024]{1,0:T(8,128)(2,1)S(1)}, u32[]{:S(2)}, u32[]{:S(2)}) collective-permute-start(bf16[128,1024]{1,0:T(8,128)(2,1)} %collective-permute-done.2.refs_6_), channel_id=1, source_target_pairs={{0,8},{2,10},{8,16},{10,18},{16,24},{18,26},{24,28},{26,30},{28,20... | collective-permute-start | bytes 786440 | tf_op jit(solution)/shard_map/ppermute | solution.py:1348
  32.4 6.7 %collective-permute-start.12 = (bf16[128,1024]{1,0:T(8,128)(2,1)}, bf16[128,1024]{1,0:T(8,128)(2,1)}, u32[]{:S(2)}, u32[]{:S(2)}) collective-permute-start(bf16[128,1024]{1,0:T(8,128)(2,1)} %collective-permute-done.3.refs_8_), channel_id=1, source_target_pairs={{0,4},{2,6},{8,0},{10,2},{16,8},{18,10},{24,16},{26,18},{28,24},{3... | collective-permute-start | bytes 786440 | tf_op jit(solution)/shard_map/ppermute | solution.py:1348
  39.8 3.8 %collective-permute-start.10 = (bf16[128,1024]{1,0:T(8,128)(2,1)}, bf16[128,1024]{1,0:T(8,128)(2,1)}, u32[]{:S(2)}, u32[]{:S(2)}) collective-permute-start(bf16[128,1024]{1,0:T(8,128)(2,1)} %collective-permute-done.3.refs_8_), channel_id=1, source_target_pairs={{0,2},{2,0},{4,6},{6,4},{8,10},{10,8},{12,14},{14,12},{16,18},{18,... | collective-permute-start | bytes 786440 | tf_op jit(solution)/shard_map/ppermute | solution.py:1343
  40.2 4.9 %collective-permute-start.9 = (bf16[128,1024]{1,0:T(8,128)(2,1)}, bf16[128,1024]{1,0:T(8,128)(2,1)}, u32[]{:S(2)}, u32[]{:S(2)}) collective-permute-start(bf16[128,1024]{1,0:T(8,128)(2,1)} %collective-permute-done.2.refs_6_), channel_id=1, source_target_pairs={{0,2},{2,0},{4,6},{6,4},{8,10},{10,8},{12,14},{14,12},{16,18},{18,... | collective-permute-start | bytes 786440 | tf_op jit(solution)/shard_map/ppermute | solution.py:1343
  40.7 5.0 %collective-permute-start.14 = (bf16[128,1024]{1,0:T(8,128)(2,1)S(1)}, bf16[128,1024]{1,0:T(8,128)(2,1)}, u32[]{:S(2)}, u32[]{:S(2)}) collective-permute-start(bf16[128,1024]{1,0:T(8,128)(2,1)S(1)} %collective-permute-done.11.refs_10_), channel_id=1, source_target_pairs={{0,2},{2,0},{4,6},{6,4},{8,10},{10,8},{12,14},{14,12},{16,18},{18,... | collective-permute-start | bytes 786440 | tf_op jit(solution)/shard_map/ppermute | solution.py:1343
  41.8 3.9 %collective-permute-start.15 = (bf16[128,1024]{1,0:T(8,128)(2,1)}, bf16[128,1024]{1,0:T(8,128)(2,1)}, u32[]{:S(2)}, u32[]{:S(2)}) collective-permute-start(bf16[128,1024]{1,0:T(8,128)(2,1)} %collective-permute-done.12.refs_12_), channel_id=1, source_target_pairs={{0,2},{2,0},{4,6},{6,4},{8,10},{10,8},{12,14},{14,12},{16,18},{18,... | collective-permute-start | bytes 786440 | tf_op jit(solution)/shard_map/ppermute | solution.py:1343
  42.0 14.6 %collective-permute-start.17 = (bf16[128,1024]{1,0:T(8,128)(2,1)}, bf16[128,1024]{1,0:T(8,128)(2,1)S(1)}, u32[]{:S(2)}, u32[]{:S(2)}) collective-permute-start(bf16[128,1024]{1,0:T(8,128)(2,1)} %fusion.5.refs_14_), channel_id=1, source_target_pairs={{0,1},{1,0},{2,3},{3,2},{4,5},{5,4},{6,7},{7,6},{8,9},{9,8},{10,11... | collective-permute-start | bytes 786440 | tf_op jit(solution)/shard_map/ppermute | solution.py:1337
  43.6 13.0 %collective-permute-start.16 = (bf16[128,1024]{1,0:T(8,128)(2,1)S(1)}, bf16[128,1024]{1,0:T(8,128)(2,1)S(1)}, u32[]{:S(2)}, u32[]{:S(2)}) collective-permute-start(bf16[128,1024]{1,0:T(8,128)(2,1)S(1)} %collective-permute-done.11.refs_10_), channel_id=1, source_target_pairs={{0,8},{2,10},{8,16},{10,18},{16,24},{18,26},{24,28},{26,30},{28,20... | collective-permute-start | bytes 786440 | tf_op jit(solution)/shard_map/ppermute | solution.py:1348
  45.2 31.5 %collective-permute-start.19 = (bf16[256,1024]{1,0:T(8,128)(2,1)S(1)}, bf16[256,1024]{1,0:T(8,128)(2,1)S(1)}, u32[]{:S(2)}, u32[]{:S(2)}) collective-permute-start(bf16[256,1024]{1,0:T(8,128)(2,1)S(1)} %get-tuple-element.225), channel_id=1, source_target_pairs={{0,1},{1,0},{2,3},{3,2},{4,5},{5,4},{6,7},{7,6},{8,9},{9,8},{10,11... | collective-permute-start | bytes 1572872 | tf_op jit(solution)/shard_map/ppermute | solution.py:1337
  56.6 3.2 %collective-permute-start.18 = (bf16[128,1024]{1,0:T(8,128)(2,1)S(1)}, bf16[128,1024]{1,0:T(8,128)(2,1)S(1)}, u32[]{:S(2)}, u32[]{:S(2)}) collective-permute-start(bf16[128,1024]{1,0:T(8,128)(2,1)S(1)} %collective-permute-done.16.refs_0_), channel_id=1, source_target_pairs={{0,2},{2,0},{4,6},{6,4},{8,10},{10,8},{12,14},{14,12},{16,18},{18,... | collective-permute-start | bytes 786440 | tf_op jit(solution)/shard_map/ppermute | solution.py:1343
  56.7 19.9 %collective-permute-start.20 = (bf16[256,1024]{1,0:T(8,128)(2,1)S(1)}, bf16[256,1024]{1,0:T(8,128)(2,1)}, u32[]{:S(2)}, u32[]{:S(2)}) collective-permute-start(bf16[256,1024]{1,0:T(8,128)(2,1)S(1)} %get-tuple-element.226), channel_id=1, source_target_pairs={{0,1},{1,0},{2,3},{3,2},{4,5},{5,4},{6,7},{7,6},{8,9},{9,8},{10,11... | collective-permute-start | bytes 1572872 | tf_op jit(solution)/shard_map/ppermute | solution.py:1337
  77.5 20.5 %collective-permute-start.21 = (bf16[256,1024]{1,0:T(8,128)(2,1)}, bf16[256,1024]{1,0:T(8,128)(2,1)}, u32[]{:S(2)}, u32[]{:S(2)}) collective-permute-start(bf16[256,1024]{1,0:T(8,128)(2,1)} %copy-done.40), channel_id=1, source_target_pairs={{0,4},{2,6},{4,0},{6,2},{8,12},{10,14},{12,8},{14,10},{16,20},{18,... | collective-permute-start | bytes 1572872 | tf_op jit(solution)/shard_map/ppermute | solution.py:1343
  77.9 20.2 %collective-permute-start.24 = (bf16[256,1024]{1,0:T(8,128)(2,1)}, bf16[256,1024]{1,0:T(8,128)(2,1)}, u32[]{:S(2)}, u32[]{:S(2)}) collective-permute-start(bf16[256,1024]{1,0:T(8,128)(2,1)} %copy-done.40), channel_id=1, source_target_pairs={{0,2},{2,0},{4,6},{6,4},{8,10},{10,8},{12,14},{14,12},{16,18},{18,... | collective-permute-start | bytes 1572872 | tf_op jit(solution)/shard_map/ppermute | solution.py:1343
  77.9 18.4 %collective-permute-start.22 = (bf16[256,1024]{1,0:T(8,128)(2,1)S(1)}, bf16[256,1024]{1,0:T(8,128)(2,1)S(1)}, u32[]{:S(2)}, u32[]{:S(2)}) collective-permute-start(bf16[256,1024]{1,0:T(8,128)(2,1)S(1)} %constant_dynamic-slice_fusion.13), channel_id=1, source_target_pairs={{0,1},{1,0},{2,3},{3,2},{4,5},{5,4},{6,7},{7,6},{8,9},{9,8},{10,11... | collective-permute-start | bytes 1572872 | tf_op jit(solution)/shard_map/ppermute | solution.py:1337
  78.5 19.5 %collective-permute-start.25 = (bf16[256,1024]{1,0:T(8,128)(2,1)}, bf16[256,1024]{1,0:T(8,128)(2,1)S(1)}, u32[]{:S(2)}, u32[]{:S(2)}) collective-permute-start(bf16[256,1024]{1,0:T(8,128)(2,1)} %collective-permute-done.20.refs_4_), channel_id=1, source_target_pairs={{0,2},{2,0},{4,6},{6,4},{8,10},{10,8},{12,14},{14,12},{16,18},{18,... | collective-permute-start | bytes 1572872 | tf_op jit(solution)/shard_map/ppermute | solution.py:1343
  78.7 19.3 %all-to-all-start = ((bf16[16,64,128]{2,1,0:T(8,128)(2,1)}), bf16[16,64,128]{2,1,0:T(8,128)(2,1)S(1)}, u32[]{:S(2)}, u32[]{:S(2)}) async-start(bf16[16,64,128]{2,1,0:T(8,128)(2,1)} %get-tuple-element.229), calls=%async_computation | async-start | bytes 524288 | tf_op jit(solution)/shard_map/all_to_all | solution.py:1511
  86.4 104.7 %all-gather.4.cloned.1.call-start = ((), (), s32[]{:S(2)}) async-start(), calls=%async_computation.3 | async-start | bytes 4456448 | tf_op jit(solution)/shard_map/all_gather | solution.py:1340
  89.3 5.1 %collective-permute-start.23 = (bf16[1,3584]{1,0:T(2,128)(2,1)S(1)}, bf16[1,3584]{1,0:T(2,128)(2,1)S(1)}, u32[]{:S(2)}, u32[]{:S(2)}) collective-permute-start(bf16[1,3584]{1,0:T(2,128)(2,1)S(1)} %pad_maximum_fusion.4), channel_id=1, source_target_pairs={{0,1},{1,0},{2,3},{3,2},{4,5},{5,4},{6,7},{7,6},{8,9},{9,8},{10,11... | collective-permute-start | bytes 21512 | tf_op jit(solution)/shard_map/ppermute | solution.py:1337
  94.4 15.4 %collective-permute-start.28 = (bf16[256,1024]{1,0:T(8,128)(2,1)}, bf16[256,1024]{1,0:T(8,128)(2,1)}, u32[]{:S(2)}, u32[]{:S(2)}) collective-permute-start(bf16[256,1024]{1,0:T(8,128)(2,1)} %collective-permute-done.20.refs_4_), channel_id=1, source_target_pairs={{0,4},{2,6},{4,0},{6,2},{8,12},{10,14},{12,8},{14,10},{16,20},{18,... | collective-permute-start | bytes 1572872 | tf_op jit(solution)/shard_map/ppermute | solution.py:1343
  96.3 13.5 %collective-permute-start.27 = (bf16[128,2048]{1,0:T(8,128)(2,1)S(1)}, bf16[128,2048]{1,0:T(8,128)(2,1)}, u32[]{:S(2)}, u32[]{:S(2)}) collective-permute-start(bf16[128,2048]{1,0:T(8,128)(2,1)S(1)} %convolution_convert_fusion), channel_id=1, source_target_pairs={{0,1},{1,0},{2,3},{3,2},{4,5},{5,4},{6,7},{7,6},{8,9},{9,8},{10,11... | collective-permute-start | bytes 1572872 | tf_op jit(solution)/shard_map/ppermute | solution.py:1337
  98.0 4.7 %collective-permute-start.26 = (bf16[256,1024]{1,0:T(8,128)(2,1)S(1)}, bf16[256,1024]{1,0:T(8,128)(2,1)}, u32[]{:S(2)}, u32[]{:S(2)}) collective-permute-start(bf16[256,1024]{1,0:T(8,128)(2,1)S(1)} %collective-permute-done.22.mine_ref.refs_16_), channel_id=1, source_target_pairs={{0,2},{2,0},{4,6},{6,4},{8,10},{10,8},{12,14},{14,12},{16,18},{18,... | collective-permute-start | bytes 1572872 | tf_op jit(solution)/shard_map/ppermute | solution.py:1343
  98.2 11.6 %collective-permute-start.29 = (bf16[256,1024]{1,0:T(8,128)(2,1)}, bf16[256,1024]{1,0:T(8,128)(2,1)S(1)}, u32[]{:S(2)}, u32[]{:S(2)}) collective-permute-start(bf16[256,1024]{1,0:T(8,128)(2,1)} %collective-permute-done.21.refs_2_), channel_id=1, source_target_pairs={{0,2},{2,0},{4,6},{6,4},{8,10},{10,8},{12,14},{14,12},{16,18},{18,... | collective-permute-start | bytes 1572872 | tf_op jit(solution)/shard_map/ppermute | solution.py:1343
  109.8 2.8 collective-permute-start.30
  110.6 13.9 %collective-permute-start.32 = (bf16[128,1024]{1,0:T(8,128)(2,1)S(1)}, bf16[128,1024]{1,0:T(8,128)(2,1)S(1)}, u32[]{:S(2)}, u32[]{:S(2)}) collective-permute-start(bf16[128,1024]{1,0:T(8,128)(2,1)S(1)} %constant_dynamic-slice_fusion.8.down_own), channel_id=1, source_target_pairs={{0,1},{1,0},{2,3},{3,2},{4,5},{5,4},{6,7},{7,6},{8,9},{9,8},{10,11... | collective-permute-start | bytes 786440 | tf_op jit(solution)/shard_map/ppermute | solution.py:1337
  112.3 12.6 %collective-permute-start.31 = (bf16[512,256]{1,0:T(8,128)(2,1)S(1)}, bf16[512,256]{1,0:T(8,128)(2,1)S(1)}, u32[]{:S(2)}, u32[]{:S(2)}) collective-permute-start(bf16[512,256]{1,0:T(8,128)(2,1)S(1)} %get-tuple-element.262), channel_id=1, source_target_pairs={{0,1},{1,0},{2,3},{3,2},{4,5},{5,4},{6,7},{7,6},{8,9},{9,8},{10,11... | collective-permute-start | bytes 786440 | tf_op jit(solution)/shard_map/ppermute | solution.py:1337
  128.8 11.0 %collective-permute-start.33 = (bf16[8,2,32,1024]{3,2,1,0:T(8,128)(2,1)S(1)}, bf16[8,2,32,1024]{3,2,1,0:T(8,128)(2,1)}, u32[]{:S(2)}, u32[]{:S(2)}) collective-permute-start(bf16[8,2,32,1024]{3,2,1,0:T(8,128)(2,1)S(1)} %fusion.2), channel_id=1, source_target_pairs={{0,2},{2,0},{4,6},{6,4},{8,10},{10,8},{12,14},{14,12},{16,18},{18,... | collective-permute-start | bytes 3145736 | tf_op jit(solution)/shard_map/ppermute | solution.py:1343
  128.9 17.2 %all-to-all-start.1 = ((bf16[16,64,128]{2,1,0:T(8,128)(2,1)}), bf16[16,64,128]{2,1,0:T(8,128)(2,1)}, u32[]{:S(2)}, u32[]{:S(2)}) async-start(bf16[16,64,128]{2,1,0:T(8,128)(2,1)} %get-tuple-element.265), calls=%async_computation.1 | async-start | bytes 524288 | tf_op jit(solution)/shard_map/all_to_all | solution.py:1565
  134.4 33.7 %collective-permute-start.35 = (bf16[128,3072]{1,0:T(8,128)(2,1)}, bf16[128,3072]{1,0:T(8,128)(2,1)S(1)}, u32[]{:S(2)}, u32[]{:S(2)}) collective-permute-start(bf16[128,3072]{1,0:T(8,128)(2,1)} %get-tuple-element.278), channel_id=1, source_target_pairs={{0,1},{1,0},{2,3},{3,2},{4,5},{5,4},{6,7},{7,6},{8,9},{9,8},{10,11... | collective-permute-start | bytes 2359304 | tf_op jit(solution)/shard_map/ppermute | solution.py:1337
  146.2 20.8 %collective-permute-start.34 = (bf16[8,32,1024]{2,1,0:T(8,128)(2,1)S(1)}, bf16[8,32,1024]{2,1,0:T(8,128)(2,1)S(1)}, u32[]{:S(2)}, u32[]{:S(2)}) collective-permute-start(bf16[8,32,1024]{2,1,0:T(8,128)(2,1)S(1)} %fusion.3), channel_id=1, source_target_pairs={{0,1},{1,0},{2,3},{3,2},{4,5},{5,4},{6,7},{7,6},{8,9},{9,8},{10,11... | collective-permute-start | bytes 1572872 | tf_op jit(solution)/shard_map/ppermute | solution.py:1337
  168.1 38.0 %all-to-all-start.2 = ((bf16[16,192,128]{2,1,0:T(8,128)(2,1)}), bf16[16,192,128]{2,1,0:T(8,128)(2,1)S(1)}, u32[]{:S(2)}, u32[]{:S(2)}) async-start(bf16[16,192,128]{2,1,0:T(8,128)(2,1)} %get-tuple-element.289), calls=%async_computation.2 | async-start | bytes 1572864 | tf_op jit(solution)/shard_map/all_to_all | solution.py:1586
  175.3 96.0 %all-gather.8.cloned.1.call-start = ((), (), s32[]{:S(2)}) async-start(), calls=%async_computation.5 | async-start | bytes 3342336 | tf_op jit(solution)/shard_map/all_gather | solution.py:1340
  179.1 7.8 %collective-permute-start.36 = (bf16[192,512]{1,0:T(8,128)(2,1)S(1)}, bf16[192,512]{1,0:T(8,128)(2,1)S(1)}, u32[]{:S(2)}, u32[]{:S(2)}) collective-permute-start(bf16[192,512]{1,0:T(8,128)(2,1)S(1)} %dynamic-slice_convert_fusion.2), channel_id=1, source_target_pairs={{0,1},{1,0},{2,3},{3,2},{4,5},{5,4},{6,7},{7,6},{8,9},{9,8},{10,11... | collective-permute-start | bytes 589832 | tf_op jit(solution)/shard_map/ppermute | solution.py:1337
  179.4 11.7 %collective-permute-start.37 = (bf16[4,32,1024]{2,1,0:T(8,128)(2,1)S(1)}, bf16[4,32,1024]{2,1,0:T(8,128)(2,1)S(1)}, u32[]{:S(2)}, u32[]{:S(2)}) collective-permute-start(bf16[4,32,1024]{2,1,0:T(8,128)(2,1)S(1)} %fusion.7), channel_id=1, source_target_pairs={{0,4},{2,6},{4,0},{6,2},{8,12},{10,14},{12,8},{14,10},{16,20},{18,... | collective-permute-start | bytes 786440 | tf_op jit(solution)/shard_map/ppermute | solution.py:1343
  181.9 24.2 %collective-permute-start.40 = (bf16[128,3072]{1,0:T(8,128)(2,1)}, bf16[128,3072]{1,0:T(8,128)(2,1)}, u32[]{:S(2)}, u32[]{:S(2)}) collective-permute-start(bf16[128,3072]{1,0:T(8,128)(2,1)} %get-tuple-element.296), channel_id=1, source_target_pairs={{0,1},{1,0},{2,3},{3,2},{4,5},{5,4},{6,7},{7,6},{8,9},{9,8},{10,11... | collective-permute-start | bytes 2359304 | tf_op jit(solution)/shard_map/ppermute | solution.py:1337
  191.2 14.9 %collective-permute-start.38 = (bf16[2,32,1024]{2,1,0:T(8,128)(2,1)S(1)}, bf16[2,32,1024]{2,1,0:T(8,128)(2,1)S(1)}, u32[]{:S(2)}, u32[]{:S(2)}) collective-permute-start(bf16[2,32,1024]{2,1,0:T(8,128)(2,1)S(1)} %fusion.14), channel_id=1, source_target_pairs={{0,8},{2,10},{4,12},{6,14},{8,0},{10,2},{12,4},{14,6},{16,24},{18,... | collective-permute-start | bytes 393224 | tf_op jit(solution)/shard_map/ppermute | solution.py:1343
  206.2 3.3 %collective-permute-start.41 = (bf16[128,3072]{1,0:T(8,128)(2,1)S(1)}, bf16[128,3072]{1,0:T(8,128)(2,1)S(1)}, u32[]{:S(2)}, u32[]{:S(2)}) collective-permute-start(bf16[128,3072]{1,0:T(8,128)(2,1)S(1)} %collective-permute-done.35.mine_0), channel_id=1, source_target_pairs={{0,2},{2,0},{4,6},{6,4},{8,10},{10,8},{12,14},{14,12},{16,18},{18,... | collective-permute-start | bytes 2359304 | tf_op jit(solution)/shard_map/ppermute | solution.py:1343
  206.2 3.7 %collective-permute-start.42 = (bf16[128,3072]{1,0:T(8,128)(2,1)}, bf16[128,3072]{1,0:T(8,128)(2,1)}, u32[]{:S(2)}, u32[]{:S(2)}) collective-permute-start(bf16[128,3072]{1,0:T(8,128)(2,1)} %collective-permute-done.40.mine_1), channel_id=1, source_target_pairs={{0,2},{2,0},{4,6},{6,4},{8,10},{10,8},{12,14},{14,12},{16,18},{18,... | collective-permute-start | bytes 2359304 | tf_op jit(solution)/shard_map/ppermute | solution.py:1343
  206.7 14.8 %collective-permute-start.39 = (bf16[2048,128]{1,0:T(8,128)(2,1)}, bf16[2048,128]{1,0:T(8,128)(2,1)S(1)}, u32[]{:S(2)}, u32[]{:S(2)}) collective-permute-start(bf16[2048,128]{1,0:T(8,128)(2,1)} %get-tuple-element.292), channel_id=1, source_target_pairs={{0,1},{1,0},{2,3},{3,2},{4,5},{5,4},{6,7},{7,6},{8,9},{9,8},{10,11... | collective-permute-start | bytes 1572872 | tf_op jit(solution)/shard_map/ppermute | solution.py:1337
  207.9 9.5 %collective-permute-start.44 = (bf16[1,32,1024]{2,1,0:T(8,128)(2,1)S(1)}, bf16[1,32,1024]{2,1,0:T(8,128)(2,1)S(1)}, u32[]{:S(2)}, u32[]{:S(2)}) collective-permute-start(bf16[1,32,1024]{2,1,0:T(8,128)(2,1)S(1)} %dynamic-slice_convert_fusion.3), channel_id=1, source_target_pairs={{0,16},{2,18},{4,20},{6,22},{8,24},{10,26},{12,28},{14,30},{16,0},... | collective-permute-start | bytes 196616 | tf_op jit(solution)/shard_map/ppermute | solution.py:1343
  216.6 5.7 %collective-permute-start.43 = (f32[12,1024]{1,0:T(8,128)}, f32[12,1024]{1,0:T(8,128)S(1)}, u32[]{:S(2)}, u32[]{:S(2)}) collective-permute-start(f32[12,1024]{1,0:T(8,128)} %get-tuple-element.305), channel_id=1, source_target_pairs={{0,1},{1,0},{2,3},{3,2},{4,5},{5,4},{6,7},{7,6},{8,9},{9,8},{10,11... | collective-permute-start | bytes 147464 | tf_op jit(solution)/shard_map/ppermute | solution.py:1337
  224.2 47.2 %collective-permute-start.52 = (bf16[1024,1024]{1,0:T(8,128)(2,1)}, bf16[1024,1024]{1,0:T(8,128)(2,1)}, u32[]{:S(2)}, u32[]{:S(2)}) collective-permute-start(bf16[1024,1024]{1,0:T(8,128)(2,1)} %constant_dynamic-slice_fusion.7), channel_id=1, source_target_pairs={{0,1},{1,0},{2,3},{3,2},{4,5},{5,4},{6,7},{7,6},{8,9},{9,8},{10,11... | collective-permute-start | bytes 6291464 | tf_op jit(solution)/shard_map/ppermute | solution.py:1337
  225.3 21.4 %collective-permute-start.45 = (bf16[2432,128]{1,0:T(8,128)(2,1)S(1)}, bf16[2432,128]{1,0:T(8,128)(2,1)S(1)}, u32[]{:S(2)}, u32[]{:S(2)}) collective-permute-start(bf16[2432,128]{1,0:T(8,128)(2,1)S(1)} %constant_dynamic-update-slice_fusion.refs_0_), channel_id=1, source_target_pairs={{0,8},{2,10},{8,16},{10,18},{16,24},{18,26},{24,28},{26,30},{28,20... | collective-permute-start | bytes 1867784 | tf_op jit(solution)/shard_map/ppermute | solution.py:1348
  225.4 27.5 %collective-permute-start.46 = (bf16[2432,128]{1,0:T(8,128)(2,1)S(1)}, bf16[2432,128]{1,0:T(8,128)(2,1)}, u32[]{:S(2)}, u32[]{:S(2)}) collective-permute-start(bf16[2432,128]{1,0:T(8,128)(2,1)S(1)} %constant_dynamic-update-slice_fusion.refs_0_), channel_id=1, source_target_pairs={{0,4},{2,6},{8,0},{10,2},{16,8},{18,10},{24,16},{26,18},{28,24},{3... | collective-permute-start | bytes 1867784 | tf_op jit(solution)/shard_map/ppermute | solution.py:1348
  227.4 26.0 %collective-permute-start.49 = (bf16[2432,128]{1,0:T(8,128)(2,1)S(1)}, bf16[2432,128]{1,0:T(8,128)(2,1)}, u32[]{:S(2)}, u32[]{:S(2)}) collective-permute-start(bf16[2432,128]{1,0:T(8,128)(2,1)S(1)} %constant_dynamic-update-slice_fusion.refs_0_), channel_id=1, source_target_pairs={{0,2},{2,0},{4,6},{6,4},{8,10},{10,8},{12,14},{14,12},{16,18},{18,... | collective-permute-start | bytes 1867784 | tf_op jit(solution)/shard_map/ppermute | solution.py:1343
  252.8 3.2 %collective-permute-start.50 = (bf16[2432,128]{1,0:T(8,128)(2,1)S(1)}, bf16[2432,128]{1,0:T(8,128)(2,1)}, u32[]{:S(2)}, u32[]{:S(2)}) collective-permute-start(bf16[2432,128]{1,0:T(8,128)(2,1)S(1)} %collective-permute-done.45.refs_2_), channel_id=1, source_target_pairs={{0,2},{2,0},{4,6},{6,4},{8,10},{10,8},{12,14},{14,12},{16,18},{18,... | collective-permute-start | bytes 1867784 | tf_op jit(solution)/shard_map/ppermute | solution.py:1343
  252.8 3.3 %collective-permute-start.51 = (bf16[2432,128]{1,0:T(8,128)(2,1)}, bf16[2432,128]{1,0:T(8,128)(2,1)}, u32[]{:S(2)}, u32[]{:S(2)}) collective-permute-start(bf16[2432,128]{1,0:T(8,128)(2,1)} %collective-permute-done.46.refs_4_), channel_id=1, source_target_pairs={{0,2},{2,0},{4,6},{6,4},{8,10},{10,8},{12,14},{14,12},{16,18},{18,... | collective-permute-start | bytes 1867784 | tf_op jit(solution)/shard_map/ppermute | solution.py:1343
  253.3 15.9 %collective-permute-start.47 = (bf16[2432,128]{1,0:T(8,128)(2,1)S(1)}, bf16[2432,128]{1,0:T(8,128)(2,1)S(1)}, u32[]{:S(2)}, u32[]{:S(2)}) collective-permute-start(bf16[2432,128]{1,0:T(8,128)(2,1)S(1)} %collective-permute-done.45.refs_2_), channel_id=1, source_target_pairs={{0,8},{2,10},{8,16},{10,18},{16,24},{18,26},{24,28},{26,30},{28,20... | collective-permute-start | bytes 1867784 | tf_op jit(solution)/shard_map/ppermute | solution.py:1348
  253.3 16.2 %collective-permute-start.48 = (bf16[2432,128]{1,0:T(8,128)(2,1)}, bf16[2432,128]{1,0:T(8,128)(2,1)S(1)}, u32[]{:S(2)}, u32[]{:S(2)}) collective-permute-start(bf16[2432,128]{1,0:T(8,128)(2,1)} %collective-permute-done.46.refs_4_), channel_id=1, source_target_pairs={{0,4},{2,6},{8,0},{10,2},{16,8},{18,10},{24,16},{26,18},{28,24},{3... | collective-permute-start | bytes 1867784 | tf_op jit(solution)/shard_map/ppermute | solution.py:1348
  271.3 10.0 %collective-permute-start.55 = (bf16[1024,1024]{1,0:T(8,128)(2,1)}, bf16[1024,1024]{1,0:T(8,128)(2,1)}, u32[]{:S(2)}, u32[]{:S(2)}) collective-permute-start(bf16[1024,1024]{1,0:T(8,128)(2,1)} %collective-permute-done.52), channel_id=1, source_target_pairs={{0,2},{2,0},{4,6},{6,4},{8,10},{10,8},{12,14},{14,12},{16,18},{18,... | collective-permute-start | bytes 6291464 | tf_op jit(solution)/shard_map/ppermute | solution.py:1343
  271.3 16.4 %collective-permute-start.53 = (bf16[2432,128]{1,0:T(8,128)(2,1)S(1)}, bf16[2432,128]{1,0:T(8,128)(2,1)S(1)}, u32[]{:S(2)}, u32[]{:S(2)}) collective-permute-start(bf16[2432,128]{1,0:T(8,128)(2,1)S(1)} %collective-permute-done.47.refs_0_.refs_6_), channel_id=1, source_target_pairs={{0,8},{2,10},{8,16},{10,18},{16,24},{18,26},{24,28},{26,30},{28,20... | collective-permute-start | bytes 1867784 | tf_op jit(solution)/shard_map/ppermute | solution.py:1348
  271.5 16.5 %collective-permute-start.56 = (bf16[2432,128]{1,0:T(8,128)(2,1)S(1)}, bf16[2432,128]{1,0:T(8,128)(2,1)S(1)}, u32[]{:S(2)}, u32[]{:S(2)}) collective-permute-start(bf16[2432,128]{1,0:T(8,128)(2,1)S(1)} %collective-permute-done.47.refs_0_.refs_6_), channel_id=1, source_target_pairs={{0,2},{2,0},{4,6},{6,4},{8,10},{10,8},{12,14},{14,12},{16,18},{18,... | collective-permute-start | bytes 1867784 | tf_op jit(solution)/shard_map/ppermute | solution.py:1343
  271.8 16.2 %collective-permute-start.54 = (bf16[2432,128]{1,0:T(8,128)(2,1)S(1)}, bf16[2432,128]{1,0:T(8,128)(2,1)S(1)}, u32[]{:S(2)}, u32[]{:S(2)}) collective-permute-start(bf16[2432,128]{1,0:T(8,128)(2,1)S(1)} %collective-permute-done.48.refs_2_.refs_8_), channel_id=1, source_target_pairs={{0,4},{2,6},{8,0},{10,2},{16,8},{18,10},{24,16},{26,18},{28,24},{3... | collective-permute-start | bytes 1867784 | tf_op jit(solution)/shard_map/ppermute | solution.py:1348
  273.6 14.4 %collective-permute-start.57 = (bf16[2432,128]{1,0:T(8,128)(2,1)S(1)}, bf16[2432,128]{1,0:T(8,128)(2,1)S(1)}, u32[]{:S(2)}, u32[]{:S(2)}) collective-permute-start(bf16[2432,128]{1,0:T(8,128)(2,1)S(1)} %collective-permute-done.48.refs_2_.refs_8_), channel_id=1, source_target_pairs={{0,2},{2,0},{4,6},{6,4},{8,10},{10,8},{12,14},{14,12},{16,18},{18,... | collective-permute-start | bytes 1867784 | tf_op jit(solution)/shard_map/ppermute | solution.py:1343
  288.1 2.9 collective-permute-start.59
  288.7 10.0 %collective-permute-start.60 = (bf16[1216,128]{1,0:T(8,128)(2,1)S(1)}, bf16[1216,128]{1,0:T(8,128)(2,1)S(1)}, u32[]{:S(2)}, u32[]{:S(2)}) collective-permute-start(bf16[1216,128]{1,0:T(8,128)(2,1)S(1)} %slice.128), channel_id=1, source_target_pairs={{0,8},{2,10},{8,16},{10,18},{16,24},{18,26},{24,28},{26,30},{28,20... | collective-permute-start | bytes 933896 | tf_op jit(solution)/shard_map/ppermute | solution.py:1348
  290.5 9.1 %collective-permute-start.61 = (bf16[1216,128]{1,0:T(8,128)(2,1)S(1)}, bf16[1216,128]{1,0:T(8,128)(2,1)S(1)}, u32[]{:S(2)}, u32[]{:S(2)}) collective-permute-start(bf16[1216,128]{1,0:T(8,128)(2,1)S(1)} %slice.129), channel_id=1, source_target_pairs={{0,4},{2,6},{8,0},{10,2},{16,8},{18,10},{24,16},{26,18},{28,24},{3... | collective-permute-start | bytes 933896 | tf_op jit(solution)/shard_map/ppermute | solution.py:1348
  (57 other events, 634.5 us)
Sparse Core Ops, SparseCore 0:
  39.3 51.3 all-gather.5
  110.0 52.6 all-gather.3
  208.0 48.9 all-gather.7

commit v2 on v1

--- a/solution.py
+++ b/solution.py
@@ -1432,7 +1432,10 @@
     tok_new = tok.go()
     packed_other = across(packed)
     w_head_other = across(w_head)
-    base = after(base, packed)
+    me_1 = after(me, packed)
+    place = jnp.asarray(place_table)[me_1]
+    who = jnp.stack([me_1, shard]).astype(jnp.int32)
+    base = place * rows
     all_index = (base[:, None] + jnp.arange(rows, dtype=jnp.int32)[None, :]).reshape(-1)
     all_position = positions(ends, all_index, segments(ends, all_index))
     half_width = head_size // 2
@@ -1565,11 +1568,16 @@
     grad_att = lax.all_to_all(grad_att, "ctx", 0, 0, tiled=True)
     qkv_mine = [across(after(qkv_send[0], up_other, down_other))]
     deep = width // (ctx_size * fsdp_size)
-    out_part = jnp.dot(
-        attended.reshape(width, rows), grad_resid_b, preferred_element_type=F32
-    )
-    out_part = out_part.reshape(chips, fsdp_size, 2, deep, width)
-    out_part = halve(out_part, 2, core, flip)
+    by_core = attended.reshape(chips, fsdp_size, 2, deep, rows)
+
+    def out_rows_of(which):
+        some = lax.dynamic_index_in_dim(by_core, which, 2, keepdims=False)
+        return jnp.dot(
+            some.reshape(half, rows), grad_resid_b, preferred_element_type=F32
+        )
+
+    out_part = out_rows_of(core) + flip(out_rows_of(1 - core).astype(BF16)).astype(F32)
+    out_part = out_part.reshape(chips, fsdp_size, deep, width)
     down_half = w_down.shape[0] // 2
     down_send = cut(w_down, (me_8 % 2) * down_half, down_half, 0)
     grad_att, down_send, out_part = fence(grad_att, down_send, out_part)

time: 316 us -> 312 us (0.987)
    ppermute x18, waiting for transfers between devices: 18.2 us -> 14.9 us  [across(): return lax.ppermute(values, 'fsdp', [(0, 1), (1, 0)])]
    unnamed x126 -> x124, local copies, waits for them, and re-layouts: 9.76 us -> 9.23 us
  transfers between devices with their start and end apart: 69 -> 69, of which waited for: 24 -> 26; matrix products, arithmetic and copies ran while one was open for 15% -> 15% of each run, Pallas kernels for 30% -> 31%
where the time goes in v2:
time: 312 us; the launch traced here: 311 us
  Pallas kernels  101 us (32%)
  waiting for transfers between devices  69.7 us (22%)
  starting transfers between devices  69.4 us (22%)
  local copies, waits for them, and re-layouts  25 us (8%)
  matrix products  17.8 us (6%)
  between operations  16.3 us (5%)
  other arithmetic  11.8 us (4%)
    ppermute x15, waiting for transfers between devices, hop(): lax.ppermute(values, 'ctx', [(2 * order[at] + c, 2 * order[(at + step) %...  43.6 us
    ppermute x18, starting transfers between devices, across(): return lax.ppermute(values, 'fsdp', [(0, 1), (1, 0)])  20.1 us
    pallas_call x1, Pallas kernels, attend_back(): pl.pallas_call(functools.partial(attend_back_kernel, chunk, rows, head_si...  18.8 us
    ppermute x15, starting transfers between devices, hop(): lax.ppermute(values, 'ctx', [(2 * order[at] + c, 2 * order[(at + step) %...  16.8 us
    ppermute x18, waiting for transfers between devices, across(): return lax.ppermute(values, 'fsdp', [(0, 1), (1, 0)])  14.9 us
    pallas_call x3, Pallas kernels, expand_wide(): pl.pallas_call(functools.partial(wide_kernel, first, len(parts)), in_spec...  14.4 us
    pallas_call x2, Pallas kernels, project_chunks(): pl.pallas_call(functools.partial(project_chunks_kernel, rows, head_size,...  14.1 us
    ppermute x30, starting transfers between devices, flip(): lax.ppermute(values, 'ctx', [(i, i ^ 1 << bit) for i in range(ctx_size)])  13.4 us
  transfers between devices with their start and end apart: 69, of which 26 were waited for; matrix products, arithmetic and copies ran while one was open for 15% of the time, Pallas kernels for 31%

profile of v2, /device:TPU:0, one launch (start us, length us, event | category | flops | bytes accessed | tf_op | source)
XLA Modules:
  0.0 310.7 jit_solution(9192349320077879396)
XLA Ops:
  7.3 3.1 collective-permute-start
  14.7 1.8 fusion.4.refs_14_
  16.8 1.5 collective-permute-done.1.refs_4_
  18.3 1.5 collective-permute-start.4
  19.8 1.6 collective-permute-start.2
  23.2 1.8 multiply_sine_fusion
  25.0 1.2 fusion.24.place_ref
  26.8 1.5 collective-permute-done.5.refs_17_.refs_5_
  29.4 1.6 collective-permute-start.11
  31.4 1.3 constant_dynamic-slice_fusion.24
  33.4 2.6 collective-permute-done.11.refs_10_
  36.0 1.7 collective-permute-done.12.refs_12_
  40.6 1.6 collective-permute-start.17
  42.2 1.6 collective-permute-start.16
  44.4 10.7 %project_chunks.2 = (bf16[2048,1024]{1,0:T(8,128)(2,1)}, bf16[128,2048]{1,0:T(8,128)(2,1)}, bf16[2048,128]{1,0:T(8,128)(2,1)}, bf16[64,2048]{1,0:T(8,128)(2,1)},...) custom-call(s32[2]{0:T(128)} %pad_add_fusion.who_ref, s32[1]{0:T(128)} %bitcast.103.ends_ref, s32[16]{0:T(128)} %copy-done.35, ...), custom_call_target="tpu_custom_call" | custom-call | flops 3758096384 | bytes 7340032 | tf_op jit(solution)/shard_map/project_chunks/pallas_call | solution.py:361
  55.2 1.6 collective-permute-start.20
  56.8 1.5 convolution_convert_fusion
  59.1 3.4 %project_chunks.3 = (bf16[2048,1024]{1,0:T(8,128)(2,1)}, bf16[128,2048]{1,0:T(8,128)(2,1)}, bf16[2048,128]{1,0:T(8,128)(2,1)}, bf16[64,2048]{1,0:T(8,128)(2,1)},...) custom-call(s32[2]{0:T(128)} %pad_add_fusion.who_ref, ...), custom_call_target="tpu_custom_call", output_to_operand_aliasing={{0}: (11, {}), {1}: (12, {}), {2}: (13, {}), {3}: (14, {}),... | custom-call | flops 536870912 | bytes 1048576 | tf_op jit(solution)/shard_map/project_chunks/pallas_call | solution.py:361
  62.5 12.7 %attend_head.1 = (f32[64,2048]{1,0:T(8,128)}, bf16[16,64,128]{2,1,0:T(8,128)(2,1)}, f32[1,2048]{1,0:T(1,128)}) custom-call(s32[16]{0:T(128)} %fusion.24.place_ref, bf16[128,2048]{1,0:T(8,128)(2,1)} %get-tuple-element.218.query_ref, bf16[2048,128]{1,0:T(8,128)(2,1)} %get-tuple-element.219.key_ref, bf16[64,2048]{1,0:T(8,128)(2,1)} %get-tuple-element.220.value_ref), custom_call_target="tpu_custom_call" | custom-call | flops 4294967296 | bytes 2097152 | tf_op jit(solution)/shard_map/attend_head/pallas_call | solution.py:413
  77.4 7.6 %all-to-all-start = ((bf16[16,64,128]{2,1,0:T(8,128)(2,1)}), bf16[16,64,128]{2,1,0:T(8,128)(2,1)S(1)}, u32[]{:S(2)}, u32[]{:S(2)}) async-start(bf16[16,64,128]{2,1,0:T(8,128)(2,1)} %get-tuple-element.229), calls=%async_computation | async-start | bytes 524288 | tf_op jit(solution)/shard_map/all_to_all | solution.py:1514
  85.2 2.6 constant_dynamic-slice_fusion.13
  88.3 4.7 %fusion.32.refs_8_ = f32[128,2048]{1,0:T(8,128)} fusion(bf16[128,1024]{1,0:T(8,128)(2,1)S(1)} %copy-done.18, bf16[2048,1024]{1,0:T(8,128)(2,1)} %param.20), kind=kOutput, calls=%fused_computation.134 | convolution fusion | flops 536870912 | bytes 5505024 | tf_op jit(solution)/shard_map/dot_general | solution.py:22
  92.9 1.9 collective-permute-start.28
  94.8 1.7 collective-permute-start.27
  101.3 3.6 %output_projection.1 = (f32[128,1024]{1,0:T(8,128)}, f32[128,1024]{1,0:T(8,128)}, f32[128,1]{1,0:T(8,128)}, bf16[128,1024]{1,0:T(8,128)(2,1)}) custom-call(s32[2]{0:T(128)} %pad_add_fusion.who_ref, bf16[16,64,128]{2,1,0:T(8,128)(2,1)} %copy-done.24, bf16[512,1024]{1,0:T(8,128)(2,1)} %refs_15_.1, bf16[256,1024]{1,0:T(8,128)(2,1)} %copy-done.40, ...), custom_call_target="tpu_custom_call" | custom-call | flops 1073741824 | bytes 4194304 | tf_op jit(solution)/shard_map/output_projection/pallas_call | solution.py:606
  104.9 3.5 %collective-permute-done.27.refs_9_ = bf16[128,2048]{1,0:T(8,128)(2,1)} collective-permute-done((bf16[128,2048]{1,0:T(8,128)(2,1)S(1)}, bf16[128,2048]{1,0:T(8,128)(2,1)}, u32[]{:S(2)}, u32[]{:S(2)}) %collective-permute-start.27) | collective-permute-done | bytes 524320 | tf_op jit(solution)/shard_map/ppermute | solution.py:1337
  110.2 1.7 collective-permute-start.32
  113.1 11.1 %feed_forward.1 = (bf16[128,4096]{1,0:T(8,128)(2,1)}, f32[128,1024]{1,0:T(8,128)}, bf16[128,1024]{1,0:T(8,128)(2,1)}, bf16[16,64,128]{2,1,0:T(8,128)(2,1)}, f32[8,1024]{1,0:T(8,128)}) custom-call(s32[2]{0:T(128)} %pad_add_fusion.who_ref, bf16[128,1024]{1,0:T(8,128)(2,1)} %get-tuple-element.247.norm_ref, bf16[512,4096]{1,0:T(8,128)(2,1)} %own_ref.4, ...), custom_call_target="tpu_custom_call" | custom-call | flops 8589934592 | bytes 16777216 | tf_op jit(solution)/shard_map/feed_forward/pallas_call | solution.py:694
  125.2 1.4 convolution_convert_fusion.1
  126.7 4.7 %all-to-all-start.1 = ((bf16[16,64,128]{2,1,0:T(8,128)(2,1)}), bf16[16,64,128]{2,1,0:T(8,128)(2,1)}, u32[]{:S(2)}, u32[]{:S(2)}) async-start(bf16[16,64,128]{2,1,0:T(8,128)(2,1)} %get-tuple-element.265), calls=%async_computation.1 | async-start | bytes 524288 | tf_op jit(solution)/shard_map/all_to_all | solution.py:1568
  132.1 1.7 collective-permute-start.35
  133.8 3.1 constant_dynamic-slice_fusion.9
  137.9 1.6 convert_add_fusion
  139.5 3.8 %all-to-all-done.1.grad_ref = bf16[16,64,128]{2,1,0:T(8,128)(2,1)} async-done(((bf16[16,64,128]{2,1,0:T(8,128)(2,1)}), bf16[16,64,128]{2,1,0:T(8,128)(2,1)}, u32[]{:S(2)}, u32[]{:S(2)}) %all-to-all-start.1) | async-done | bytes 262176 | tf_op jit(solution)/shard_map/all_to_all | solution.py:1568
  143.4 1.9 collective-permute-start.34
  145.3 18.8 %attend_head_back.1 = (bf16[192,2048]{1,0:T(8,128)(2,1)}, bf16[16,192,128]{2,1,0:T(8,128)(2,1)}) custom-call(s32[16]{0:T(128)} %fusion.24.place_ref, bf16[128,2048]{1,0:T(8,128)(2,1)} %get-tuple-element.218.query_ref, bf16[16,64,128]{2,1,0:T(8,128)(2,1)} %all-to-all-done.1.grad_ref, f32[64,2048]{1,0:T(8,128)} %get-tuple-element.269.out_ref, ...), custom_call_target="tpu_custom_call" | custom-call | flops 10737418240 | bytes 4194304 | tf_op jit(solution)/shard_map/attend_head_back/pallas_call | solution.py:462
  165.2 6.3 %all-to-all-start.2 = ((bf16[16,192,128]{2,1,0:T(8,128)(2,1)}), bf16[16,192,128]{2,1,0:T(8,128)(2,1)S(1)}, u32[]{:S(2)}, u32[]{:S(2)}) async-start(bf16[16,192,128]{2,1,0:T(8,128)(2,1)} %get-tuple-element.289), calls=%async_computation.2 | async-start | bytes 1572864 | tf_op jit(solution)/shard_map/all_to_all | solution.py:1594
  171.8 3.4 %fusion.33 = f32[192,1024]{1,0:T(8,128)S(1)} fusion(bf16[192,2048]{1,0:T(8,128)(2,1)} %get-tuple-element.279, bf16[2048,1024]{1,0:T(8,128)(2,1)} %get-tuple-element.280), kind=kOutput, calls=%fused_computation.135 | convolution fusion | flops 805306368 | bytes 5767168 | tf_op jit(solution)/shard_map/dot_general | solution.py:1595
  175.9 2.0 collective-permute-start.37
  178.4 1.5 collective-permute-start.40
  180.0 3.1 collective-permute-done.36
  183.8 3.5 %collective-permute-done.37 = bf16[4,32,1024]{2,1,0:T(8,128)(2,1)S(1)} collective-permute-done((bf16[4,32,1024]{2,1,0:T(8,128)(2,1)S(1)}, bf16[4,32,1024]{2,1,0:T(8,128)(2,1)S(1)}, u32[]{:S(2)}, u32[]{:S(2)}) %collective-permute-start.37) | collective-permute-done | bytes 262176 | tf_op jit(solution)/shard_map/ppermute | solution.py:1343
  187.5 3.1 collective-permute-start.38
  190.6 11.8 %weight_slices.1 = (f32[2048,128]{1,0:T(8,128)}, bf16[2048,128]{1,0:T(8,128)(2,1)}) custom-call(s32[2]{0:T(128)} %pad_add_fusion.who_ref, bf16[2048,1024]{1,0:T(8,128)(2,1)} %all-gather.4.cloned.1.call-done.norm_ref, bf16[2048,1024]{1,0:T(8,128)(2,1)} %all-gather.6.cloned.1.call-done.grad_ref, bf16[512,256]{1,0:T(8,128)(2,1)} %get-tuple-element.285.up_own, ...), custom_call_target="tpu_custom_call" | custom-call | flops 4294967296 | bytes 12582912 | tf_op jit(solution)/shard_map/weight_slices/pallas_call | solution.py:533
  204.3 1.3 collective-permute-start.44
  206.5 6.3 %first_norm_back.1 = (bf16[128,1024]{1,0:T(8,128)(2,1)}, f32[12,1024]{1,0:T(8,128)}) custom-call(s32[2]{0:T(128)} %pad_add_fusion.who_ref, s32[1]{0:T(128)} %bitcast.105.ends_ref, bf16[16,192,128]{2,1,0:T(8,128)(2,1)} %copy-done.9, bf16[512,3072]{1,0:T(8,128)(2,1)} %own_ref.5, bf16[128,3072]{1,0:T(8,128)(2,1)} %copy-done.25, ...), custom_call_target="tpu_custom_call" | custom-call | flops 1610612736 | bytes 8388608 | tf_op jit(solution)/shard_map/first_norm_back/pallas_call | solution.py:762
  213.7 4.1 %collective-permute-done.39 = bf16[2048,128]{1,0:T(8,128)(2,1)S(1)} collective-permute-done((bf16[2048,128]{1,0:T(8,128)(2,1)}, bf16[2048,128]{1,0:T(8,128)(2,1)S(1)}, u32[]{:S(2)}, u32[]{:S(2)}) %collective-permute-start.39) | collective-permute-done | bytes 524320 | tf_op jit(solution)/shard_map/ppermute | solution.py:1337
  221.7 2.0 collective-permute-start.46
  223.7 19.1 %collective-permute-done.45.refs_2_ = bf16[2432,128]{1,0:T(8,128)(2,1)S(1)} collective-permute-done((bf16[2432,128]{1,0:T(8,128)(2,1)S(1)}, bf16[2432,128]{1,0:T(8,128)(2,1)S(1)}, u32[]{:S(2)}, u32[]{:S(2)}) %collective-permute-start.45) | collective-permute-done | bytes 622624 | tf_op jit(solution)/shard_map/ppermute | solution.py:1348
  242.9 6.4 %collective-permute-done.46.refs_4_ = bf16[2432,128]{1,0:T(8,128)(2,1)} collective-permute-done((bf16[2432,128]{1,0:T(8,128)(2,1)S(1)}, bf16[2432,128]{1,0:T(8,128)(2,1)}, u32[]{:S(2)}, u32[]{:S(2)}) %collective-permute-start.46) | collective-permute-done | bytes 622624 | tf_op jit(solution)/shard_map/ppermute | solution.py:1348
  249.8 2.0 collective-permute-start.48
  252.6 5.1 %expand_wide.3 = (f32[512,4096]{1,0:T(8,128)}, f32[2048,1024]{1,0:T(8,128)}, f32[512,1024]{1,0:T(8,128)}) custom-call(s32[16]{0:T(128)} %fusion.24.place_ref, bf16[2432,128]{1,0:T(8,128)(2,1)} %copy-done.4, bf16[2432,128]{1,0:T(8,128)(2,1)} %collective-permute-done.49.refs_1_, bf16[2432,128]{1,0:T(8,128)(2,1)} %copy-done.17, ...), custom_call_target="tpu_custom_call" | custom-call | flops 1867776 | bytes 11206656 | tf_op jit(solution)/shard_map/expand_wide/pallas_call | solution.py:936
  257.7 8.0 %collective-permute-done.47.refs_0_.refs_6_ = bf16[2432,128]{1,0:T(8,128)(2,1)S(1)} collective-permute-done((bf16[2432,128]{1,0:T(8,128)(2,1)S(1)}, bf16[2432,128]{1,0:T(8,128)(2,1)S(1)}, u32[]{:S(2)}, u32[]{:S(2)}) %collective-permute-start.47) | collective-permute-done | bytes 622624 | tf_op jit(solution)/shard_map/ppermute | solution.py:1348
  266.0 1.7 collective-permute-done.52
  268.2 1.7 collective-permute-start.54
  270.0 5.4 %expand_last.1 = f32[512,3072]{1,0:T(8,128)} custom-call(bf16[16,192,512]{2,1,0:T(8,128)(2,1)} %bitcast.110), custom_call_target="tpu_custom_call" | custom-call | flops 1572864 | bytes 9437184 | tf_op jit(solution)/shard_map/expand_last/pallas_call | solution.py:977
  275.4 2.2 fusion.9
  277.6 2.1 fusion.7
  281.4 2.7 collective-permute-done.53.refs_4_.refs_10_
  284.9 1.7 collective-permute-start.60
  288.7 6.3 %expand_wide.4 = (f32[512,4096]{1,0:T(8,128)}, f32[2048,1024]{1,0:T(8,128)}, f32[512,1024]{1,0:T(8,128)}) custom-call(s32[16]{0:T(128)} %fusion.24.place_ref, bf16[2432,128]{1,0:T(8,128)(2,1)} %copy-done.10, bf16[2432,128]{1,0:T(8,128)(2,1)} %copy-done.12, ...), custom_call_target="tpu_custom_call", output_to_operand_aliasing={{0}: (9, {}), {1}: (10, {}), {2}: (11, {})} | custom-call | flops 2490368 | bytes 14942208 | tf_op jit(solution)/shard_map/expand_wide/pallas_call | solution.py:936
  295.9 2.0 collective-permute-done.62.refs_1_.refs_15_
  298.8 2.4 small_gradients.1
  301.2 3.0 expand_wide.5
  (283 shorter events, 44.6 us)
Async XLA Ops:
  7.2 180.2 %all-gather.6.cloned.1.call-start = ((), (), s32[]{:S(2)}) async-start(), calls=%async_computation.4 | async-start | bytes 4456448 | tf_op jit(solution)/shard_map/all_gather | solution.py:1340
  7.3 9.5 %collective-permute-start = (bf16[128,1024]{1,0:T(8,128)(2,1)}, bf16[128,1024]{1,0:T(8,128)(2,1)S(1)}, u32[]{:S(2)}, u32[]{:S(2)}) collective-permute-start(bf16[128,1024]{1,0:T(8,128)(2,1)} %bitcast.116), channel_id=1, source_target_pairs={{0,8},{2,10},{8,16},{10,18},{16,24},{18,26},{24,28},{26,30},{28,20... | collective-permute-start | bytes 786440 | tf_op jit(solution)/shard_map/ppermute | solution.py:1348
  10.4 8.0 %collective-permute-start.1 = (bf16[128,1024]{1,0:T(8,128)(2,1)}, bf16[128,1024]{1,0:T(8,128)(2,1)S(1)}, u32[]{:S(2)}, u32[]{:S(2)}) collective-permute-start(bf16[128,1024]{1,0:T(8,128)(2,1)} %bitcast.117), channel_id=1, source_target_pairs={{0,4},{2,6},{8,0},{10,2},{16,8},{18,10},{24,16},{26,18},{28,24},{3... | collective-permute-start | bytes 786440 | tf_op jit(solution)/shard_map/ppermute | solution.py:1348
  18.3 8.4 %collective-permute-start.4 = (bf16[1,1026]{1,0:T(2,128)(2,1)S(1)}, bf16[1,1026]{1,0:T(2,128)(2,1)S(1)}, u32[]{:S(2)}, u32[]{:S(2)}) collective-permute-start(bf16[1,1026]{1,0:T(2,128)(2,1)S(1)} %concatenate.53), channel_id=1, source_target_pairs={{0,1},{1,0},{2,3},{3,2},{4,5},{5,4},{6,7},{7,6},{8,9},{9,8},{10,11... | collective-permute-start | bytes 6164 | tf_op jit(solution)/shard_map/ppermute | solution.py:1337
  19.8 8.4 %collective-permute-start.2 = (bf16[128,1024]{1,0:T(8,128)(2,1)S(1)}, bf16[128,1024]{1,0:T(8,128)(2,1)}, u32[]{:S(2)}, u32[]{:S(2)}) collective-permute-start(bf16[128,1024]{1,0:T(8,128)(2,1)S(1)} %collective-permute-done.refs_2_), channel_id=1, source_target_pairs={{0,8},{2,10},{8,16},{10,18},{16,24},{18,26},{24,28},{26,30},{28,20... | collective-permute-start | bytes 786440 | tf_op jit(solution)/shard_map/ppermute | solution.py:1348
  21.4 6.8 %collective-permute-start.3 = (bf16[128,1024]{1,0:T(8,128)(2,1)S(1)}, bf16[128,1024]{1,0:T(8,128)(2,1)}, u32[]{:S(2)}, u32[]{:S(2)}) collective-permute-start(bf16[128,1024]{1,0:T(8,128)(2,1)S(1)} %collective-permute-done.1.refs_4_), channel_id=1, source_target_pairs={{0,4},{2,6},{8,0},{10,2},{16,8},{18,10},{24,16},{26,18},{28,24},{3... | collective-permute-start | bytes 786440 | tf_op jit(solution)/shard_map/ppermute | solution.py:1348
  21.9 6.4 %collective-permute-start.5 = (bf16[512,192]{1,0:T(8,128)(2,1)S(1)}, bf16[512,192]{1,0:T(8,128)(2,1)S(1)}, u32[]{:S(2)}, u32[]{:S(2)}) collective-permute-start(bf16[512,192]{1,0:T(8,128)(2,1)S(1)} %pad_maximum_fusion.refs_16_.refs_4_), channel_id=1, source_target_pairs={{0,1},{1,0},{2,3},{3,2},{4,5},{5,4},{6,7},{7,6},{8,9},{9,8},{10,11... | collective-permute-start | bytes 589832 | tf_op jit(solution)/shard_map/ppermute | solution.py:1337
  28.8 3.9 %collective-permute-start.13 = (f32[1,2048]{1,0:T(1,128)S(1)}, f32[1,2048]{1,0:T(1,128)S(1)}, u32[]{:S(2)}, u32[]{:S(2)}) collective-permute-start(f32[1,2048]{1,0:T(1,128)S(1)} %constant_dynamic-slice_fusion.18), channel_id=1, source_target_pairs={{0,1},{1,0},{2,3},{3,2},{4,5},{5,4},{6,7},{7,6},{8,9},{9,8},{10,11... | collective-permute-start | bytes 24584 | tf_op jit(solution)/shard_map/ppermute | solution.py:1337
  29.4 6.6 %collective-permute-start.11 = (bf16[128,1024]{1,0:T(8,128)(2,1)}, bf16[128,1024]{1,0:T(8,128)(2,1)S(1)}, u32[]{:S(2)}, u32[]{:S(2)}) collective-permute-start(bf16[128,1024]{1,0:T(8,128)(2,1)} %collective-permute-done.2.refs_6_), channel_id=1, source_target_pairs={{0,8},{2,10},{8,16},{10,18},{16,24},{18,26},{24,28},{26,30},{28,20... | collective-permute-start | bytes 786440 | tf_op jit(solution)/shard_map/ppermute | solution.py:1348
  31.0 6.7 %collective-permute-start.12 = (bf16[128,1024]{1,0:T(8,128)(2,1)}, bf16[128,1024]{1,0:T(8,128)(2,1)}, u32[]{:S(2)}, u32[]{:S(2)}) collective-permute-start(bf16[128,1024]{1,0:T(8,128)(2,1)} %collective-permute-done.3.refs_8_), channel_id=1, source_target_pairs={{0,4},{2,6},{8,0},{10,2},{16,8},{18,10},{24,16},{26,18},{28,24},{3... | collective-permute-start | bytes 786440 | tf_op jit(solution)/shard_map/ppermute | solution.py:1348
  38.4 3.8 %collective-permute-start.10 = (bf16[128,1024]{1,0:T(8,128)(2,1)}, bf16[128,1024]{1,0:T(8,128)(2,1)}, u32[]{:S(2)}, u32[]{:S(2)}) collective-permute-start(bf16[128,1024]{1,0:T(8,128)(2,1)} %collective-permute-done.3.refs_8_), channel_id=1, source_target_pairs={{0,2},{2,0},{4,6},{6,4},{8,10},{10,8},{12,14},{14,12},{16,18},{18,... | collective-permute-start | bytes 786440 | tf_op jit(solution)/shard_map/ppermute | solution.py:1343
  38.8 5.0 %collective-permute-start.9 = (bf16[128,1024]{1,0:T(8,128)(2,1)}, bf16[128,1024]{1,0:T(8,128)(2,1)}, u32[]{:S(2)}, u32[]{:S(2)}) collective-permute-start(bf16[128,1024]{1,0:T(8,128)(2,1)} %collective-permute-done.2.refs_6_), channel_id=1, source_target_pairs={{0,2},{2,0},{4,6},{6,4},{8,10},{10,8},{12,14},{14,12},{16,18},{18,... | collective-permute-start | bytes 786440 | tf_op jit(solution)/shard_map/ppermute | solution.py:1343
  39.3 5.0 %collective-permute-start.14 = (bf16[128,1024]{1,0:T(8,128)(2,1)S(1)}, bf16[128,1024]{1,0:T(8,128)(2,1)}, u32[]{:S(2)}, u32[]{:S(2)}) collective-permute-start(bf16[128,1024]{1,0:T(8,128)(2,1)S(1)} %collective-permute-done.11.refs_10_), channel_id=1, source_target_pairs={{0,2},{2,0},{4,6},{6,4},{8,10},{10,8},{12,14},{14,12},{16,18},{18,... | collective-permute-start | bytes 786440 | tf_op jit(solution)/shard_map/ppermute | solution.py:1343
  40.4 3.9 %collective-permute-start.15 = (bf16[128,1024]{1,0:T(8,128)(2,1)}, bf16[128,1024]{1,0:T(8,128)(2,1)}, u32[]{:S(2)}, u32[]{:S(2)}) collective-permute-start(bf16[128,1024]{1,0:T(8,128)(2,1)} %collective-permute-done.12.refs_12_), channel_id=1, source_target_pairs={{0,2},{2,0},{4,6},{6,4},{8,10},{10,8},{12,14},{14,12},{16,18},{18,... | collective-permute-start | bytes 786440 | tf_op jit(solution)/shard_map/ppermute | solution.py:1343
  40.6 14.5 %collective-permute-start.17 = (bf16[128,1024]{1,0:T(8,128)(2,1)}, bf16[128,1024]{1,0:T(8,128)(2,1)S(1)}, u32[]{:S(2)}, u32[]{:S(2)}) collective-permute-start(bf16[128,1024]{1,0:T(8,128)(2,1)} %fusion.4.refs_14_), channel_id=1, source_target_pairs={{0,1},{1,0},{2,3},{3,2},{4,5},{5,4},{6,7},{7,6},{8,9},{9,8},{10,11... | collective-permute-start | bytes 786440 | tf_op jit(solution)/shard_map/ppermute | solution.py:1337
  42.2 12.9 %collective-permute-start.16 = (bf16[128,1024]{1,0:T(8,128)(2,1)S(1)}, bf16[128,1024]{1,0:T(8,128)(2,1)S(1)}, u32[]{:S(2)}, u32[]{:S(2)}) collective-permute-start(bf16[128,1024]{1,0:T(8,128)(2,1)S(1)} %collective-permute-done.11.refs_10_), channel_id=1, source_target_pairs={{0,8},{2,10},{8,16},{10,18},{16,24},{18,26},{24,28},{26,30},{28,20... | collective-permute-start | bytes 786440 | tf_op jit(solution)/shard_map/ppermute | solution.py:1348
  43.8 31.4 %collective-permute-start.19 = (bf16[256,1024]{1,0:T(8,128)(2,1)S(1)}, bf16[256,1024]{1,0:T(8,128)(2,1)S(1)}, u32[]{:S(2)}, u32[]{:S(2)}) collective-permute-start(bf16[256,1024]{1,0:T(8,128)(2,1)S(1)} %get-tuple-element.225), channel_id=1, source_target_pairs={{0,1},{1,0},{2,3},{3,2},{4,5},{5,4},{6,7},{7,6},{8,9},{9,8},{10,11... | collective-permute-start | bytes 1572872 | tf_op jit(solution)/shard_map/ppermute | solution.py:1337
  55.1 3.2 %collective-permute-start.18 = (bf16[128,1024]{1,0:T(8,128)(2,1)S(1)}, bf16[128,1024]{1,0:T(8,128)(2,1)S(1)}, u32[]{:S(2)}, u32[]{:S(2)}) collective-permute-start(bf16[128,1024]{1,0:T(8,128)(2,1)S(1)} %collective-permute-done.16.refs_0_), channel_id=1, source_target_pairs={{0,2},{2,0},{4,6},{6,4},{8,10},{10,8},{12,14},{14,12},{16,18},{18,... | collective-permute-start | bytes 786440 | tf_op jit(solution)/shard_map/ppermute | solution.py:1343
  55.2 20.0 %collective-permute-start.20 = (bf16[256,1024]{1,0:T(8,128)(2,1)S(1)}, bf16[256,1024]{1,0:T(8,128)(2,1)}, u32[]{:S(2)}, u32[]{:S(2)}) collective-permute-start(bf16[256,1024]{1,0:T(8,128)(2,1)S(1)} %get-tuple-element.226), channel_id=1, source_target_pairs={{0,1},{1,0},{2,3},{3,2},{4,5},{5,4},{6,7},{7,6},{8,9},{9,8},{10,11... | collective-permute-start | bytes 1572872 | tf_op jit(solution)/shard_map/ppermute | solution.py:1337
  76.0 20.5 %collective-permute-start.21 = (bf16[256,1024]{1,0:T(8,128)(2,1)}, bf16[256,1024]{1,0:T(8,128)(2,1)}, u32[]{:S(2)}, u32[]{:S(2)}) collective-permute-start(bf16[256,1024]{1,0:T(8,128)(2,1)} %copy-done.39), channel_id=1, source_target_pairs={{0,4},{2,6},{4,0},{6,2},{8,12},{10,14},{12,8},{14,10},{16,20},{18,... | collective-permute-start | bytes 1572872 | tf_op jit(solution)/shard_map/ppermute | solution.py:1343
  76.5 20.0 %collective-permute-start.24 = (bf16[256,1024]{1,0:T(8,128)(2,1)}, bf16[256,1024]{1,0:T(8,128)(2,1)}, u32[]{:S(2)}, u32[]{:S(2)}) collective-permute-start(bf16[256,1024]{1,0:T(8,128)(2,1)} %copy-done.39), channel_id=1, source_target_pairs={{0,2},{2,0},{4,6},{6,4},{8,10},{10,8},{12,14},{14,12},{16,18},{18,... | collective-permute-start | bytes 1572872 | tf_op jit(solution)/shard_map/ppermute | solution.py:1343
  76.6 18.2 %collective-permute-start.22 = (bf16[256,1024]{1,0:T(8,128)(2,1)S(1)}, bf16[256,1024]{1,0:T(8,128)(2,1)S(1)}, u32[]{:S(2)}, u32[]{:S(2)}) collective-permute-start(bf16[256,1024]{1,0:T(8,128)(2,1)S(1)} %constant_dynamic-slice_fusion.15), channel_id=1, source_target_pairs={{0,1},{1,0},{2,3},{3,2},{4,5},{5,4},{6,7},{7,6},{8,9},{9,8},{10,11... | collective-permute-start | bytes 1572872 | tf_op jit(solution)/shard_map/ppermute | solution.py:1337
  77.2 19.4 %collective-permute-start.25 = (bf16[256,1024]{1,0:T(8,128)(2,1)}, bf16[256,1024]{1,0:T(8,128)(2,1)S(1)}, u32[]{:S(2)}, u32[]{:S(2)}) collective-permute-start(bf16[256,1024]{1,0:T(8,128)(2,1)} %collective-permute-done.20.refs_4_), channel_id=1, source_target_pairs={{0,2},{2,0},{4,6},{6,4},{8,10},{10,8},{12,14},{14,12},{16,18},{18,... | collective-permute-start | bytes 1572872 | tf_op jit(solution)/shard_map/ppermute | solution.py:1343
  77.4 19.1 %all-to-all-start = ((bf16[16,64,128]{2,1,0:T(8,128)(2,1)}), bf16[16,64,128]{2,1,0:T(8,128)(2,1)S(1)}, u32[]{:S(2)}, u32[]{:S(2)}) async-start(bf16[16,64,128]{2,1,0:T(8,128)(2,1)} %get-tuple-element.229), calls=%async_computation | async-start | bytes 524288 | tf_op jit(solution)/shard_map/all_to_all | solution.py:1514
  85.0 102.4 %all-gather.4.cloned.1.call-start = ((), (), s32[]{:S(2)}) async-start(), calls=%async_computation.3 | async-start | bytes 4456448 | tf_op jit(solution)/shard_map/all_gather | solution.py:1340
  87.9 5.1 %collective-permute-start.23 = (bf16[1,3584]{1,0:T(2,128)(2,1)S(1)}, bf16[1,3584]{1,0:T(2,128)(2,1)S(1)}, u32[]{:S(2)}, u32[]{:S(2)}) collective-permute-start(bf16[1,3584]{1,0:T(2,128)(2,1)S(1)} %pad_maximum_fusion.4), channel_id=1, source_target_pairs={{0,1},{1,0},{2,3},{3,2},{4,5},{5,4},{6,7},{7,6},{8,9},{9,8},{10,11... | collective-permute-start | bytes 21512 | tf_op jit(solution)/shard_map/ppermute | solution.py:1337
  92.9 15.4 %collective-permute-start.28 = (bf16[256,1024]{1,0:T(8,128)(2,1)}, bf16[256,1024]{1,0:T(8,128)(2,1)}, u32[]{:S(2)}, u32[]{:S(2)}) collective-permute-start(bf16[256,1024]{1,0:T(8,128)(2,1)} %collective-permute-done.20.refs_4_), channel_id=1, source_target_pairs={{0,4},{2,6},{4,0},{6,2},{8,12},{10,14},{12,8},{14,10},{16,20},{18,... | collective-permute-start | bytes 1572872 | tf_op jit(solution)/shard_map/ppermute | solution.py:1343
  94.8 13.6 %collective-permute-start.27 = (bf16[128,2048]{1,0:T(8,128)(2,1)S(1)}, bf16[128,2048]{1,0:T(8,128)(2,1)}, u32[]{:S(2)}, u32[]{:S(2)}) collective-permute-start(bf16[128,2048]{1,0:T(8,128)(2,1)S(1)} %convolution_convert_fusion), channel_id=1, source_target_pairs={{0,1},{1,0},{2,3},{3,2},{4,5},{5,4},{6,7},{7,6},{8,9},{9,8},{10,11... | collective-permute-start | bytes 1572872 | tf_op jit(solution)/shard_map/ppermute | solution.py:1337
  96.6 4.7 %collective-permute-start.26 = (bf16[256,1024]{1,0:T(8,128)(2,1)S(1)}, bf16[256,1024]{1,0:T(8,128)(2,1)}, u32[]{:S(2)}, u32[]{:S(2)}) collective-permute-start(bf16[256,1024]{1,0:T(8,128)(2,1)S(1)} %collective-permute-done.22.mine_ref.refs_16_), channel_id=1, source_target_pairs={{0,2},{2,0},{4,6},{6,4},{8,10},{10,8},{12,14},{14,12},{16,18},{18,... | collective-permute-start | bytes 1572872 | tf_op jit(solution)/shard_map/ppermute | solution.py:1343
  96.7 11.7 %collective-permute-start.29 = (bf16[256,1024]{1,0:T(8,128)(2,1)}, bf16[256,1024]{1,0:T(8,128)(2,1)S(1)}, u32[]{:S(2)}, u32[]{:S(2)}) collective-permute-start(bf16[256,1024]{1,0:T(8,128)(2,1)} %collective-permute-done.21.refs_2_), channel_id=1, source_target_pairs={{0,2},{2,0},{4,6},{6,4},{8,10},{10,8},{12,14},{14,12},{16,18},{18,... | collective-permute-start | bytes 1572872 | tf_op jit(solution)/shard_map/ppermute | solution.py:1343
  108.4 3.8 %collective-permute-start.30 = (bf16[256,1024]{1,0:T(8,128)(2,1)}, bf16[256,1024]{1,0:T(8,128)(2,1)S(1)}, u32[]{:S(2)}, u32[]{:S(2)}) collective-permute-start(bf16[256,1024]{1,0:T(8,128)(2,1)} %collective-permute-done.28.refs_6_), channel_id=1, source_target_pairs={{0,2},{2,0},{4,6},{6,4},{8,10},{10,8},{12,14},{14,12},{16,18},{18,... | collective-permute-start | bytes 1572872 | tf_op jit(solution)/shard_map/ppermute | solution.py:1343
  110.2 14.0 %collective-permute-start.32 = (bf16[128,1024]{1,0:T(8,128)(2,1)S(1)}, bf16[128,1024]{1,0:T(8,128)(2,1)S(1)}, u32[]{:S(2)}, u32[]{:S(2)}) collective-permute-start(bf16[128,1024]{1,0:T(8,128)(2,1)S(1)} %constant_dynamic-slice_fusion.10.down_own), channel_id=1, source_target_pairs={{0,1},{1,0},{2,3},{3,2},{4,5},{5,4},{6,7},{7,6},{8,9},{9,8},{10,11... | collective-permute-start | bytes 786440 | tf_op jit(solution)/shard_map/ppermute | solution.py:1337
  111.8 12.7 %collective-permute-start.31 = (bf16[512,256]{1,0:T(8,128)(2,1)S(1)}, bf16[512,256]{1,0:T(8,128)(2,1)S(1)}, u32[]{:S(2)}, u32[]{:S(2)}) collective-permute-start(bf16[512,256]{1,0:T(8,128)(2,1)S(1)} %get-tuple-element.262), channel_id=1, source_target_pairs={{0,1},{1,0},{2,3},{3,2},{4,5},{5,4},{6,7},{7,6},{8,9},{9,8},{10,11... | collective-permute-start | bytes 786440 | tf_op jit(solution)/shard_map/ppermute | solution.py:1337
  126.6 10.3 %collective-permute-start.33 = (bf16[512,1024]{1,0:T(8,128)(2,1)S(1)}, bf16[512,1024]{1,0:T(8,128)(2,1)S(1)}, u32[]{:S(2)}, u32[]{:S(2)}) collective-permute-start(bf16[512,1024]{1,0:T(8,128)(2,1)S(1)} %convolution_convert_fusion.1), channel_id=1, source_target_pairs={{0,2},{2,0},{4,6},{6,4},{8,10},{10,8},{12,14},{14,12},{16,18},{18,... | collective-permute-start | bytes 3145736 | tf_op jit(solution)/shard_map/ppermute | solution.py:1343
  126.7 16.6 %all-to-all-start.1 = ((bf16[16,64,128]{2,1,0:T(8,128)(2,1)}), bf16[16,64,128]{2,1,0:T(8,128)(2,1)}, u32[]{:S(2)}, u32[]{:S(2)}) async-start(bf16[16,64,128]{2,1,0:T(8,128)(2,1)} %get-tuple-element.265), calls=%async_computation.1 | async-start | bytes 524288 | tf_op jit(solution)/shard_map/all_to_all | solution.py:1568
  132.1 33.1 %collective-permute-start.35 = (bf16[128,3072]{1,0:T(8,128)(2,1)}, bf16[128,3072]{1,0:T(8,128)(2,1)S(1)}, u32[]{:S(2)}, u32[]{:S(2)}) collective-permute-start(bf16[128,3072]{1,0:T(8,128)(2,1)} %get-tuple-element.278), channel_id=1, source_target_pairs={{0,1},{1,0},{2,3},{3,2},{4,5},{5,4},{6,7},{7,6},{8,9},{9,8},{10,11... | collective-permute-start | bytes 2359304 | tf_op jit(solution)/shard_map/ppermute | solution.py:1337
  143.4 20.7 %collective-permute-start.34 = (bf16[8,32,1024]{2,1,0:T(8,128)(2,1)S(1)}, bf16[8,32,1024]{2,1,0:T(8,128)(2,1)S(1)}, u32[]{:S(2)}, u32[]{:S(2)}) collective-permute-start(bf16[8,32,1024]{2,1,0:T(8,128)(2,1)S(1)} %fusion.2), channel_id=1, source_target_pairs={{0,1},{1,0},{2,3},{3,2},{4,5},{5,4},{6,7},{7,6},{8,9},{9,8},{10,11... | collective-permute-start | bytes 1572872 | tf_op jit(solution)/shard_map/ppermute | solution.py:1337
  165.2 37.2 %all-to-all-start.2 = ((bf16[16,192,128]{2,1,0:T(8,128)(2,1)}), bf16[16,192,128]{2,1,0:T(8,128)(2,1)S(1)}, u32[]{:S(2)}, u32[]{:S(2)}) async-start(bf16[16,192,128]{2,1,0:T(8,128)(2,1)} %get-tuple-element.289), calls=%async_computation.2 | async-start | bytes 1572864 | tf_op jit(solution)/shard_map/all_to_all | solution.py:1594
  171.6 96.1 %all-gather.8.cloned.1.call-start = ((), (), s32[]{:S(2)}) async-start(), calls=%async_computation.5 | async-start | bytes 3342336 | tf_op jit(solution)/shard_map/all_gather | solution.py:1340
  175.3 7.8 %collective-permute-start.36 = (bf16[192,512]{1,0:T(8,128)(2,1)S(1)}, bf16[192,512]{1,0:T(8,128)(2,1)S(1)}, u32[]{:S(2)}, u32[]{:S(2)}) collective-permute-start(bf16[192,512]{1,0:T(8,128)(2,1)S(1)} %dynamic-slice_convert_fusion.2), channel_id=1, source_target_pairs={{0,1},{1,0},{2,3},{3,2},{4,5},{5,4},{6,7},{7,6},{8,9},{9,8},{10,11... | collective-permute-start | bytes 589832 | tf_op jit(solution)/shard_map/ppermute | solution.py:1337
  175.9 11.4 %collective-permute-start.37 = (bf16[4,32,1024]{2,1,0:T(8,128)(2,1)S(1)}, bf16[4,32,1024]{2,1,0:T(8,128)(2,1)S(1)}, u32[]{:S(2)}, u32[]{:S(2)}) collective-permute-start(bf16[4,32,1024]{2,1,0:T(8,128)(2,1)S(1)} %fusion.6), channel_id=1, source_target_pairs={{0,4},{2,6},{4,0},{6,2},{8,12},{10,14},{12,8},{14,10},{16,20},{18,... | collective-permute-start | bytes 786440 | tf_op jit(solution)/shard_map/ppermute | solution.py:1343
  178.4 24.0 %collective-permute-start.40 = (bf16[128,3072]{1,0:T(8,128)(2,1)}, bf16[128,3072]{1,0:T(8,128)(2,1)}, u32[]{:S(2)}, u32[]{:S(2)}) collective-permute-start(bf16[128,3072]{1,0:T(8,128)(2,1)} %get-tuple-element.296), channel_id=1, source_target_pairs={{0,1},{1,0},{2,3},{3,2},{4,5},{5,4},{6,7},{7,6},{8,9},{9,8},{10,11... | collective-permute-start | bytes 2359304 | tf_op jit(solution)/shard_map/ppermute | solution.py:1337
  187.5 15.0 %collective-permute-start.38 = (bf16[2,32,1024]{2,1,0:T(8,128)(2,1)S(1)}, bf16[2,32,1024]{2,1,0:T(8,128)(2,1)S(1)}, u32[]{:S(2)}, u32[]{:S(2)}) collective-permute-start(bf16[2,32,1024]{2,1,0:T(8,128)(2,1)S(1)} %fusion.11), channel_id=1, source_target_pairs={{0,8},{2,10},{4,12},{6,14},{8,0},{10,2},{12,4},{14,6},{16,24},{18,... | collective-permute-start | bytes 393224 | tf_op jit(solution)/shard_map/ppermute | solution.py:1343
  202.5 3.1 %collective-permute-start.41 = (bf16[128,3072]{1,0:T(8,128)(2,1)S(1)}, bf16[128,3072]{1,0:T(8,128)(2,1)S(1)}, u32[]{:S(2)}, u32[]{:S(2)}) collective-permute-start(bf16[128,3072]{1,0:T(8,128)(2,1)S(1)} %collective-permute-done.35.mine_0), channel_id=1, source_target_pairs={{0,2},{2,0},{4,6},{6,4},{8,10},{10,8},{12,14},{14,12},{16,18},{18,... | collective-permute-start | bytes 2359304 | tf_op jit(solution)/shard_map/ppermute | solution.py:1343
  202.6 3.7 %collective-permute-start.42 = (bf16[128,3072]{1,0:T(8,128)(2,1)}, bf16[128,3072]{1,0:T(8,128)(2,1)}, u32[]{:S(2)}, u32[]{:S(2)}) collective-permute-start(bf16[128,3072]{1,0:T(8,128)(2,1)} %collective-permute-done.40.mine_1), channel_id=1, source_target_pairs={{0,2},{2,0},{4,6},{6,4},{8,10},{10,8},{12,14},{14,12},{16,18},{18,... | collective-permute-start | bytes 2359304 | tf_op jit(solution)/shard_map/ppermute | solution.py:1343
  203.1 14.8 %collective-permute-start.39 = (bf16[2048,128]{1,0:T(8,128)(2,1)}, bf16[2048,128]{1,0:T(8,128)(2,1)S(1)}, u32[]{:S(2)}, u32[]{:S(2)}) collective-permute-start(bf16[2048,128]{1,0:T(8,128)(2,1)} %get-tuple-element.292), channel_id=1, source_target_pairs={{0,1},{1,0},{2,3},{3,2},{4,5},{5,4},{6,7},{7,6},{8,9},{9,8},{10,11... | collective-permute-start | bytes 1572872 | tf_op jit(solution)/shard_map/ppermute | solution.py:1337
  204.3 9.4 %collective-permute-start.44 = (bf16[1,32,1024]{2,1,0:T(8,128)(2,1)S(1)}, bf16[1,32,1024]{2,1,0:T(8,128)(2,1)S(1)}, u32[]{:S(2)}, u32[]{:S(2)}) collective-permute-start(bf16[1,32,1024]{2,1,0:T(8,128)(2,1)S(1)} %dynamic-slice_convert_fusion.3), channel_id=1, source_target_pairs={{0,16},{2,18},{4,20},{6,22},{8,24},{10,26},{12,28},{14,30},{16,0},... | collective-permute-start | bytes 196616 | tf_op jit(solution)/shard_map/ppermute | solution.py:1343
  212.7 5.8 %collective-permute-start.43 = (f32[12,1024]{1,0:T(8,128)}, f32[12,1024]{1,0:T(8,128)S(1)}, u32[]{:S(2)}, u32[]{:S(2)}) collective-permute-start(f32[12,1024]{1,0:T(8,128)} %get-tuple-element.305), channel_id=1, source_target_pairs={{0,1},{1,0},{2,3},{3,2},{4,5},{5,4},{6,7},{7,6},{8,9},{9,8},{10,11... | collective-permute-start | bytes 147464 | tf_op jit(solution)/shard_map/ppermute | solution.py:1337
  220.5 47.2 %collective-permute-start.52 = (bf16[1024,1024]{1,0:T(8,128)(2,1)}, bf16[1024,1024]{1,0:T(8,128)(2,1)}, u32[]{:S(2)}, u32[]{:S(2)}) collective-permute-start(bf16[1024,1024]{1,0:T(8,128)(2,1)} %constant_dynamic-slice_fusion.9), channel_id=1, source_target_pairs={{0,1},{1,0},{2,3},{3,2},{4,5},{5,4},{6,7},{7,6},{8,9},{9,8},{10,11... | collective-permute-start | bytes 6291464 | tf_op jit(solution)/shard_map/ppermute | solution.py:1337
  221.7 21.2 %collective-permute-start.45 = (bf16[2432,128]{1,0:T(8,128)(2,1)S(1)}, bf16[2432,128]{1,0:T(8,128)(2,1)S(1)}, u32[]{:S(2)}, u32[]{:S(2)}) collective-permute-start(bf16[2432,128]{1,0:T(8,128)(2,1)S(1)} %constant_dynamic-update-slice_fusion.refs_0_), channel_id=1, source_target_pairs={{0,8},{2,10},{8,16},{10,18},{16,24},{18,26},{24,28},{26,30},{28,20... | collective-permute-start | bytes 1867784 | tf_op jit(solution)/shard_map/ppermute | solution.py:1348
  221.7 27.5 %collective-permute-start.46 = (bf16[2432,128]{1,0:T(8,128)(2,1)S(1)}, bf16[2432,128]{1,0:T(8,128)(2,1)}, u32[]{:S(2)}, u32[]{:S(2)}) collective-permute-start(bf16[2432,128]{1,0:T(8,128)(2,1)S(1)} %constant_dynamic-update-slice_fusion.refs_0_), channel_id=1, source_target_pairs={{0,4},{2,6},{8,0},{10,2},{16,8},{18,10},{24,16},{26,18},{28,24},{3... | collective-permute-start | bytes 1867784 | tf_op jit(solution)/shard_map/ppermute | solution.py:1348
  223.7 26.1 %collective-permute-start.49 = (bf16[2432,128]{1,0:T(8,128)(2,1)S(1)}, bf16[2432,128]{1,0:T(8,128)(2,1)}, u32[]{:S(2)}, u32[]{:S(2)}) collective-permute-start(bf16[2432,128]{1,0:T(8,128)(2,1)S(1)} %constant_dynamic-update-slice_fusion.refs_0_), channel_id=1, source_target_pairs={{0,2},{2,0},{4,6},{6,4},{8,10},{10,8},{12,14},{14,12},{16,18},{18,... | collective-permute-start | bytes 1867784 | tf_op jit(solution)/shard_map/ppermute | solution.py:1343
  249.3 3.2 %collective-permute-start.50 = (bf16[2432,128]{1,0:T(8,128)(2,1)S(1)}, bf16[2432,128]{1,0:T(8,128)(2,1)}, u32[]{:S(2)}, u32[]{:S(2)}) collective-permute-start(bf16[2432,128]{1,0:T(8,128)(2,1)S(1)} %collective-permute-done.45.refs_2_), channel_id=1, source_target_pairs={{0,2},{2,0},{4,6},{6,4},{8,10},{10,8},{12,14},{14,12},{16,18},{18,... | collective-permute-start | bytes 1867784 | tf_op jit(solution)/shard_map/ppermute | solution.py:1343
  249.3 3.3 %collective-permute-start.51 = (bf16[2432,128]{1,0:T(8,128)(2,1)}, bf16[2432,128]{1,0:T(8,128)(2,1)}, u32[]{:S(2)}, u32[]{:S(2)}) collective-permute-start(bf16[2432,128]{1,0:T(8,128)(2,1)} %collective-permute-done.46.refs_4_), channel_id=1, source_target_pairs={{0,2},{2,0},{4,6},{6,4},{8,10},{10,8},{12,14},{14,12},{16,18},{18,... | collective-permute-start | bytes 1867784 | tf_op jit(solution)/shard_map/ppermute | solution.py:1343
  249.8 15.9 %collective-permute-start.47 = (bf16[2432,128]{1,0:T(8,128)(2,1)S(1)}, bf16[2432,128]{1,0:T(8,128)(2,1)S(1)}, u32[]{:S(2)}, u32[]{:S(2)}) collective-permute-start(bf16[2432,128]{1,0:T(8,128)(2,1)S(1)} %collective-permute-done.45.refs_2_), channel_id=1, source_target_pairs={{0,8},{2,10},{8,16},{10,18},{16,24},{18,26},{24,28},{26,30},{28,20... | collective-permute-start | bytes 1867784 | tf_op jit(solution)/shard_map/ppermute | solution.py:1348
  249.8 16.2 %collective-permute-start.48 = (bf16[2432,128]{1,0:T(8,128)(2,1)}, bf16[2432,128]{1,0:T(8,128)(2,1)S(1)}, u32[]{:S(2)}, u32[]{:S(2)}) collective-permute-start(bf16[2432,128]{1,0:T(8,128)(2,1)} %collective-permute-done.46.refs_4_), channel_id=1, source_target_pairs={{0,4},{2,6},{8,0},{10,2},{16,8},{18,10},{24,16},{26,18},{28,24},{3... | collective-permute-start | bytes 1867784 | tf_op jit(solution)/shard_map/ppermute | solution.py:1348
  267.6 10.0 %collective-permute-start.55 = (bf16[1024,1024]{1,0:T(8,128)(2,1)}, bf16[1024,1024]{1,0:T(8,128)(2,1)}, u32[]{:S(2)}, u32[]{:S(2)}) collective-permute-start(bf16[1024,1024]{1,0:T(8,128)(2,1)} %collective-permute-done.52), channel_id=1, source_target_pairs={{0,2},{2,0},{4,6},{6,4},{8,10},{10,8},{12,14},{14,12},{16,18},{18,... | collective-permute-start | bytes 6291464 | tf_op jit(solution)/shard_map/ppermute | solution.py:1343
  267.7 16.4 %collective-permute-start.53 = (bf16[2432,128]{1,0:T(8,128)(2,1)S(1)}, bf16[2432,128]{1,0:T(8,128)(2,1)S(1)}, u32[]{:S(2)}, u32[]{:S(2)}) collective-permute-start(bf16[2432,128]{1,0:T(8,128)(2,1)S(1)} %collective-permute-done.47.refs_0_.refs_6_), channel_id=1, source_target_pairs={{0,8},{2,10},{8,16},{10,18},{16,24},{18,26},{24,28},{26,30},{28,20... | collective-permute-start | bytes 1867784 | tf_op jit(solution)/shard_map/ppermute | solution.py:1348
  267.8 16.5 %collective-permute-start.56 = (bf16[2432,128]{1,0:T(8,128)(2,1)S(1)}, bf16[2432,128]{1,0:T(8,128)(2,1)S(1)}, u32[]{:S(2)}, u32[]{:S(2)}) collective-permute-start(bf16[2432,128]{1,0:T(8,128)(2,1)S(1)} %collective-permute-done.47.refs_0_.refs_6_), channel_id=1, source_target_pairs={{0,2},{2,0},{4,6},{6,4},{8,10},{10,8},{12,14},{14,12},{16,18},{18,... | collective-permute-start | bytes 1867784 | tf_op jit(solution)/shard_map/ppermute | solution.py:1343
  268.2 16.1 %collective-permute-start.54 = (bf16[2432,128]{1,0:T(8,128)(2,1)S(1)}, bf16[2432,128]{1,0:T(8,128)(2,1)S(1)}, u32[]{:S(2)}, u32[]{:S(2)}) collective-permute-start(bf16[2432,128]{1,0:T(8,128)(2,1)S(1)} %collective-permute-done.48.refs_2_.refs_8_), channel_id=1, source_target_pairs={{0,4},{2,6},{8,0},{10,2},{16,8},{18,10},{24,16},{26,18},{28,24},{3... | collective-permute-start | bytes 1867784 | tf_op jit(solution)/shard_map/ppermute | solution.py:1348
  269.9 14.4 %collective-permute-start.57 = (bf16[2432,128]{1,0:T(8,128)(2,1)S(1)}, bf16[2432,128]{1,0:T(8,128)(2,1)S(1)}, u32[]{:S(2)}, u32[]{:S(2)}) collective-permute-start(bf16[2432,128]{1,0:T(8,128)(2,1)S(1)} %collective-permute-done.48.refs_2_.refs_8_), channel_id=1, source_target_pairs={{0,2},{2,0},{4,6},{6,4},{8,10},{10,8},{12,14},{14,12},{16,18},{18,... | collective-permute-start | bytes 1867784 | tf_op jit(solution)/shard_map/ppermute | solution.py:1343
  284.4 2.9 collective-permute-start.59
  284.9 10.0 %collective-permute-start.60 = (bf16[1216,128]{1,0:T(8,128)(2,1)S(1)}, bf16[1216,128]{1,0:T(8,128)(2,1)S(1)}, u32[]{:S(2)}, u32[]{:S(2)}) collective-permute-start(bf16[1216,128]{1,0:T(8,128)(2,1)S(1)} %slice.128), channel_id=1, source_target_pairs={{0,8},{2,10},{8,16},{10,18},{16,24},{18,26},{24,28},{26,30},{28,20... | collective-permute-start | bytes 933896 | tf_op jit(solution)/shard_map/ppermute | solution.py:1348
  286.7 9.1 %collective-permute-start.61 = (bf16[1216,128]{1,0:T(8,128)(2,1)S(1)}, bf16[1216,128]{1,0:T(8,128)(2,1)S(1)}, u32[]{:S(2)}, u32[]{:S(2)}) collective-permute-start(bf16[1216,128]{1,0:T(8,128)(2,1)S(1)} %slice.129), channel_id=1, source_target_pairs={{0,4},{2,6},{8,0},{10,2},{16,8},{18,10},{24,16},{26,18},{28,24},{3... | collective-permute-start | bytes 933896 | tf_op jit(solution)/shard_map/ppermute | solution.py:1348
  (56 other events, 585.4 us)
Sparse Core Ops, SparseCore 0:
  37.8 50.4 all-gather.5
  108.5 51.9 all-gather.3
  204.3 49.0 all-gather.7

commit v3 on v2

--- a/solution.py
+++ b/solution.py
@@ -384,7 +384,7 @@
     count = key.shape[0]
     head_size = value_t.shape[0]
     block = min(count, 2 * rows)
-    chunk = min(count, 512)
+    chunk = min(count, 1024)
     blocks = count // block
 
     def before(i):
@@ -433,7 +433,7 @@
     head_size = key_t.shape[0]
     half = head_size // 2
     block = min(count, 2 * rows)
-    chunk = min(count, 512)
+    chunk = min(count, 1024)
     grid_spec = pltpu.PrefetchScalarGridSpec(
         num_scalar_prefetch=1,
         grid=(count // block,),

time: 312 us -> 312 us (level)
  transfers between devices with their start and end apart: 69 -> 69, of which waited for: 26 -> 28; matrix products, arithmetic and copies ran while one was open for 15% -> 15% of each run, Pallas kernels for 31% -> 30%
where the time goes in v3:
time: 312 us; the launch traced here: 310 us
  Pallas kernels  99.5 us (32%)
  waiting for transfers between devices  70.8 us (23%)
  starting transfers between devices  68.9 us (22%)
  local copies, waits for them, and re-layouts  24.8 us (8%)
  matrix products  17.8 us (6%)
  between operations  16.3 us (5%)
  other arithmetic  11.8 us (4%)
    ppermute x15, waiting for transfers between devices, hop(): lax.ppermute(values, 'ctx', [(2 * order[at] + c, 2 * order[(at + step) %...  43.7 us
    ppermute x18, starting transfers between devices, across(): return lax.ppermute(values, 'fsdp', [(0, 1), (1, 0)])  19.5 us
    pallas_call x1, Pallas kernels, attend_back(): pl.pallas_call(functools.partial(attend_back_kernel, chunk, rows, head_si...  18.3 us
    ppermute x15, starting transfers between devices, hop(): lax.ppermute(values, 'ctx', [(2 * order[at] + c, 2 * order[(at + step) %...  16.8 us
    ppermute x18, waiting for transfers between devices, across(): return lax.ppermute(values, 'fsdp', [(0, 1), (1, 0)])  15.1 us
    pallas_call x3, Pallas kernels, expand_wide(): pl.pallas_call(functools.partial(wide_kernel, first, len(parts)), in_spec...  14.4 us
    pallas_call x2, Pallas kernels, project_chunks(): pl.pallas_call(functools.partial(project_chunks_kernel, rows, head_size,...  14.1 us
    ppermute x30, starting transfers between devices, flip(): lax.ppermute(values, 'ctx', [(i, i ^ 1 << bit) for i in range(ctx_size)])  13.5 us
  transfers between devices with their start and end apart: 69, of which 28 were waited for; matrix products, arithmetic and copies ran while one was open for 15% of the time, Pallas kernels for 30%

profile of v3, /device:TPU:0, one launch (start us, length us, event | category | flops | bytes accessed | tf_op | source)
XLA Modules:
  0.0 310.0 jit_solution(16522528796291821884)
XLA Ops:
  7.3 3.1 collective-permute-start
  11.1 1.2 constant_dynamic-slice_fusion.23
  14.7 1.8 fusion.4.refs_14_
  16.8 1.5 collective-permute-done.1.refs_4_
  18.3 1.5 collective-permute-start.4
  19.8 1.6 collective-permute-start.2
  23.2 1.8 multiply_sine_fusion
  25.0 1.2 fusion.24.place_ref
  26.8 1.5 collective-permute-done.5.refs_17_.refs_5_
  29.4 1.6 collective-permute-start.11
  31.4 1.3 constant_dynamic-slice_fusion.24
  33.4 2.6 collective-permute-done.11.refs_10_
  36.0 1.7 collective-permute-done.12.refs_12_
  40.6 1.6 collective-permute-start.17
  42.2 1.6 collective-permute-start.16
  44.4 10.7 %project_chunks.2 = (bf16[2048,1024]{1,0:T(8,128)(2,1)}, bf16[128,2048]{1,0:T(8,128)(2,1)}, bf16[2048,128]{1,0:T(8,128)(2,1)}, bf16[64,2048]{1,0:T(8,128)(2,1)},...) custom-call(s32[2]{0:T(128)} %pad_add_fusion.who_ref, s32[1]{0:T(128)} %bitcast.103.ends_ref, s32[16]{0:T(128)} %copy-done.35, ...), custom_call_target="tpu_custom_call" | custom-call | flops 3758096384 | bytes 7340032 | tf_op jit(solution)/shard_map/project_chunks/pallas_call | solution.py:361
  55.2 1.6 collective-permute-start.20
  56.8 1.5 convolution_convert_fusion
  59.1 3.4 %project_chunks.3 = (bf16[2048,1024]{1,0:T(8,128)(2,1)}, bf16[128,2048]{1,0:T(8,128)(2,1)}, bf16[2048,128]{1,0:T(8,128)(2,1)}, bf16[64,2048]{1,0:T(8,128)(2,1)},...) custom-call(s32[2]{0:T(128)} %pad_add_fusion.who_ref, ...), custom_call_target="tpu_custom_call", output_to_operand_aliasing={{0}: (11, {}), {1}: (12, {}), {2}: (13, {}), {3}: (14, {}),... | custom-call | flops 536870912 | bytes 1048576 | tf_op jit(solution)/shard_map/project_chunks/pallas_call | solution.py:361
  62.5 12.0 %attend_head.1 = (f32[64,2048]{1,0:T(8,128)}, bf16[16,64,128]{2,1,0:T(8,128)(2,1)}, f32[1,2048]{1,0:T(1,128)}) custom-call(s32[16]{0:T(128)} %fusion.24.place_ref, bf16[128,2048]{1,0:T(8,128)(2,1)} %get-tuple-element.218.query_ref, bf16[2048,128]{1,0:T(8,128)(2,1)} %get-tuple-element.219.key_ref, bf16[64,2048]{1,0:T(8,128)(2,1)} %get-tuple-element.220.value_ref), custom_call_target="tpu_custom_call" | custom-call | flops 4294967296 | bytes 2097152 | tf_op jit(solution)/shard_map/attend_head/pallas_call | solution.py:413
  76.7 7.6 %all-to-all-start = ((bf16[16,64,128]{2,1,0:T(8,128)(2,1)}), bf16[16,64,128]{2,1,0:T(8,128)(2,1)S(1)}, u32[]{:S(2)}, u32[]{:S(2)}) async-start(bf16[16,64,128]{2,1,0:T(8,128)(2,1)} %get-tuple-element.229), calls=%async_computation | async-start | bytes 524288 | tf_op jit(solution)/shard_map/all_to_all | solution.py:1514
  84.6 2.6 constant_dynamic-slice_fusion.13
  87.6 4.7 %fusion.32.refs_8_ = f32[128,2048]{1,0:T(8,128)} fusion(bf16[128,1024]{1,0:T(8,128)(2,1)S(1)} %copy-done.18, bf16[2048,1024]{1,0:T(8,128)(2,1)} %param.20), kind=kOutput, calls=%fused_computation.134 | convolution fusion | flops 536870912 | bytes 5505024 | tf_op jit(solution)/shard_map/dot_general | solution.py:22
  92.2 1.9 collective-permute-start.28
  94.2 1.7 collective-permute-start.27
  100.6 3.6 %output_projection.1 = (f32[128,1024]{1,0:T(8,128)}, f32[128,1024]{1,0:T(8,128)}, f32[128,1]{1,0:T(8,128)}, bf16[128,1024]{1,0:T(8,128)(2,1)}) custom-call(s32[2]{0:T(128)} %pad_add_fusion.who_ref, bf16[16,64,128]{2,1,0:T(8,128)(2,1)} %copy-done.24, bf16[512,1024]{1,0:T(8,128)(2,1)} %refs_15_.1, bf16[256,1024]{1,0:T(8,128)(2,1)} %copy-done.40, ...), custom_call_target="tpu_custom_call" | custom-call | flops 1073741824 | bytes 4194304 | tf_op jit(solution)/shard_map/output_projection/pallas_call | solution.py:606
  104.3 3.4 %collective-permute-done.27.refs_9_ = bf16[128,2048]{1,0:T(8,128)(2,1)} collective-permute-done((bf16[128,2048]{1,0:T(8,128)(2,1)S(1)}, bf16[128,2048]{1,0:T(8,128)(2,1)}, u32[]{:S(2)}, u32[]{:S(2)}) %collective-permute-start.27) | collective-permute-done | bytes 524320 | tf_op jit(solution)/shard_map/ppermute | solution.py:1337
  109.5 1.7 collective-permute-start.32
  112.4 11.1 %feed_forward.1 = (bf16[128,4096]{1,0:T(8,128)(2,1)}, f32[128,1024]{1,0:T(8,128)}, bf16[128,1024]{1,0:T(8,128)(2,1)}, bf16[16,64,128]{2,1,0:T(8,128)(2,1)}, f32[8,1024]{1,0:T(8,128)}) custom-call(s32[2]{0:T(128)} %pad_add_fusion.who_ref, bf16[128,1024]{1,0:T(8,128)(2,1)} %get-tuple-element.247.norm_ref, bf16[512,4096]{1,0:T(8,128)(2,1)} %own_ref.4, ...), custom_call_target="tpu_custom_call" | custom-call | flops 8589934592 | bytes 16777216 | tf_op jit(solution)/shard_map/feed_forward/pallas_call | solution.py:694
  124.5 1.4 convolution_convert_fusion.1
  126.0 4.8 %all-to-all-start.1 = ((bf16[16,64,128]{2,1,0:T(8,128)(2,1)}), bf16[16,64,128]{2,1,0:T(8,128)(2,1)}, u32[]{:S(2)}, u32[]{:S(2)}) async-start(bf16[16,64,128]{2,1,0:T(8,128)(2,1)} %get-tuple-element.265), calls=%async_computation.1 | async-start | bytes 524288 | tf_op jit(solution)/shard_map/all_to_all | solution.py:1568
  131.5 1.7 collective-permute-start.35
  133.2 3.1 %constant_dynamic-slice_fusion.9 = bf16[1024,1024]{1,0:T(8,128)(2,1)} fusion(bf16[2048,1024]{1,0:T(8,128)(2,1)} %param.20, s32[]{:T(128)S(6)} %select_n.213), kind=kLoop, calls=%fused_computation.77 | loop fusion | bytes 4194308 | tf_op jit(solution)/shard_map/dynamic_slice | solution.py:1364
  137.3 1.6 convert_add_fusion
  138.9 3.6 %all-to-all-done.1.grad_ref = bf16[16,64,128]{2,1,0:T(8,128)(2,1)} async-done(((bf16[16,64,128]{2,1,0:T(8,128)(2,1)}), bf16[16,64,128]{2,1,0:T(8,128)(2,1)}, u32[]{:S(2)}, u32[]{:S(2)}) %all-to-all-start.1) | async-done | bytes 262176 | tf_op jit(solution)/shard_map/all_to_all | solution.py:1568
  142.6 1.9 collective-permute-start.34
  144.5 18.3 %attend_head_back.1 = (bf16[192,2048]{1,0:T(8,128)(2,1)}, bf16[16,192,128]{2,1,0:T(8,128)(2,1)}) custom-call(s32[16]{0:T(128)} %fusion.24.place_ref, bf16[128,2048]{1,0:T(8,128)(2,1)} %get-tuple-element.218.query_ref, bf16[16,64,128]{2,1,0:T(8,128)(2,1)} %all-to-all-done.1.grad_ref, f32[64,2048]{1,0:T(8,128)} %get-tuple-element.269.out_ref, ...), custom_call_target="tpu_custom_call" | custom-call | flops 10737418240 | bytes 4194304 | tf_op jit(solution)/shard_map/attend_head_back/pallas_call | solution.py:462
  164.0 6.2 %all-to-all-start.2 = ((bf16[16,192,128]{2,1,0:T(8,128)(2,1)}), bf16[16,192,128]{2,1,0:T(8,128)(2,1)S(1)}, u32[]{:S(2)}, u32[]{:S(2)}) async-start(bf16[16,192,128]{2,1,0:T(8,128)(2,1)} %get-tuple-element.289), calls=%async_computation.2 | async-start | bytes 1572864 | tf_op jit(solution)/shard_map/all_to_all | solution.py:1594
  170.5 3.4 %fusion.33 = f32[192,1024]{1,0:T(8,128)S(1)} fusion(bf16[192,2048]{1,0:T(8,128)(2,1)} %get-tuple-element.279, bf16[2048,1024]{1,0:T(8,128)(2,1)} %get-tuple-element.280), kind=kOutput, calls=%fused_computation.135 | convolution fusion | flops 805306368 | bytes 5767168 | tf_op jit(solution)/shard_map/dot_general | solution.py:1595
  173.9 1.3 collective-permute-start.36
  175.3 2.0 collective-permute-start.37
  178.6 3.1 collective-permute-done.36
  182.4 3.8 %collective-permute-done.37 = bf16[4,32,1024]{2,1,0:T(8,128)(2,1)S(1)} collective-permute-done((bf16[4,32,1024]{2,1,0:T(8,128)(2,1)S(1)}, bf16[4,32,1024]{2,1,0:T(8,128)(2,1)S(1)}, u32[]{:S(2)}, u32[]{:S(2)}) %collective-permute-start.37) | collective-permute-done | bytes 262176 | tf_op jit(solution)/shard_map/ppermute | solution.py:1343
  186.3 3.4 %collective-permute-start.38 = (bf16[2,32,1024]{2,1,0:T(8,128)(2,1)S(1)}, bf16[2,32,1024]{2,1,0:T(8,128)(2,1)S(1)}, u32[]{:S(2)}, u32[]{:S(2)}) collective-permute-start(bf16[2,32,1024]{2,1,0:T(8,128)(2,1)S(1)} %fusion.11), channel_id=1, source_target_pairs={{0,8},{2,10},{4,12},{6,14},{8,0},{10,2},{12,4},{14,6},{16,24},{18,... | collective-permute-start | bytes 393224 | tf_op jit(solution)/shard_map/ppermute | solution.py:1343
  189.7 11.8 %weight_slices.1 = (f32[2048,128]{1,0:T(8,128)}, bf16[2048,128]{1,0:T(8,128)(2,1)}) custom-call(s32[2]{0:T(128)} %pad_add_fusion.who_ref, bf16[2048,1024]{1,0:T(8,128)(2,1)} %all-gather.4.cloned.1.call-done.norm_ref, bf16[2048,1024]{1,0:T(8,128)(2,1)} %all-gather.6.cloned.1.call-done.grad_ref, bf16[512,256]{1,0:T(8,128)(2,1)} %get-tuple-element.285.up_own, ...), custom_call_target="tpu_custom_call" | custom-call | flops 4294967296 | bytes 12582912 | tf_op jit(solution)/shard_map/weight_slices/pallas_call | solution.py:533
  205.4 6.3 %first_norm_back.1 = (bf16[128,1024]{1,0:T(8,128)(2,1)}, f32[12,1024]{1,0:T(8,128)}) custom-call(s32[2]{0:T(128)} %pad_add_fusion.who_ref, s32[1]{0:T(128)} %bitcast.105.ends_ref, bf16[16,192,128]{2,1,0:T(8,128)(2,1)} %copy-done.9, bf16[512,3072]{1,0:T(8,128)(2,1)} %own_ref.5, bf16[128,3072]{1,0:T(8,128)(2,1)} %copy-done.25, ...), custom_call_target="tpu_custom_call" | custom-call | flops 1610612736 | bytes 8388608 | tf_op jit(solution)/shard_map/first_norm_back/pallas_call | solution.py:762
  212.6 4.4 %collective-permute-done.39 = bf16[2048,128]{1,0:T(8,128)(2,1)S(1)} collective-permute-done((bf16[2048,128]{1,0:T(8,128)(2,1)}, bf16[2048,128]{1,0:T(8,128)(2,1)S(1)}, u32[]{:S(2)}, u32[]{:S(2)}) %collective-permute-start.39) | collective-permute-done | bytes 524320 | tf_op jit(solution)/shard_map/ppermute | solution.py:1337
  220.6 2.0 collective-permute-start.46
  222.6 18.5 %collective-permute-done.45.refs_2_ = bf16[2432,128]{1,0:T(8,128)(2,1)S(1)} collective-permute-done((bf16[2432,128]{1,0:T(8,128)(2,1)S(1)}, bf16[2432,128]{1,0:T(8,128)(2,1)S(1)}, u32[]{:S(2)}, u32[]{:S(2)}) %collective-permute-start.45) | collective-permute-done | bytes 622624 | tf_op jit(solution)/shard_map/ppermute | solution.py:1348
  241.2 7.2 %collective-permute-done.46.refs_4_ = bf16[2432,128]{1,0:T(8,128)(2,1)} collective-permute-done((bf16[2432,128]{1,0:T(8,128)(2,1)S(1)}, bf16[2432,128]{1,0:T(8,128)(2,1)}, u32[]{:S(2)}, u32[]{:S(2)}) %collective-permute-start.46) | collective-permute-done | bytes 622624 | tf_op jit(solution)/shard_map/ppermute | solution.py:1348
  248.9 2.0 collective-permute-start.48
  251.9 5.1 %expand_wide.3 = (f32[512,4096]{1,0:T(8,128)}, f32[2048,1024]{1,0:T(8,128)}, f32[512,1024]{1,0:T(8,128)}) custom-call(s32[16]{0:T(128)} %fusion.24.place_ref, bf16[2432,128]{1,0:T(8,128)(2,1)} %copy-done.4, bf16[2432,128]{1,0:T(8,128)(2,1)} %collective-permute-done.49.refs_1_, bf16[2432,128]{1,0:T(8,128)(2,1)} %copy-done.17, ...), custom_call_target="tpu_custom_call" | custom-call | flops 1867776 | bytes 11206656 | tf_op jit(solution)/shard_map/expand_wide/pallas_call | solution.py:936
  257.1 7.7 %collective-permute-done.47.refs_0_.refs_6_ = bf16[2432,128]{1,0:T(8,128)(2,1)S(1)} collective-permute-done((bf16[2432,128]{1,0:T(8,128)(2,1)S(1)}, bf16[2432,128]{1,0:T(8,128)(2,1)S(1)}, u32[]{:S(2)}, u32[]{:S(2)}) %collective-permute-start.47) | collective-permute-done | bytes 622624 | tf_op jit(solution)/shard_map/ppermute | solution.py:1348
  265.1 1.7 collective-permute-done.52
  267.3 1.7 collective-permute-start.54
  269.1 5.4 %expand_last.1 = f32[512,3072]{1,0:T(8,128)} custom-call(bf16[16,192,512]{2,1,0:T(8,128)(2,1)} %bitcast.110), custom_call_target="tpu_custom_call" | custom-call | flops 1572864 | bytes 9437184 | tf_op jit(solution)/shard_map/expand_last/pallas_call | solution.py:977
  274.5 2.2 fusion.9
  276.8 2.1 fusion.7
  280.5 2.7 collective-permute-done.53.refs_4_.refs_10_
  284.1 1.6 collective-permute-start.60
  287.8 6.3 %expand_wide.4 = (f32[512,4096]{1,0:T(8,128)}, f32[2048,1024]{1,0:T(8,128)}, f32[512,1024]{1,0:T(8,128)}) custom-call(s32[16]{0:T(128)} %fusion.24.place_ref, bf16[2432,128]{1,0:T(8,128)(2,1)} %copy-done.10, bf16[2432,128]{1,0:T(8,128)(2,1)} %copy-done.12, ...), custom_call_target="tpu_custom_call", output_to_operand_aliasing={{0}: (9, {}), {1}: (10, {}), {2}: (11, {})} | custom-call | flops 2490368 | bytes 14942208 | tf_op jit(solution)/shard_map/expand_wide/pallas_call | solution.py:936
  295.1 2.0 collective-permute-done.62.refs_1_.refs_15_
  298.0 2.4 small_gradients.1
  300.4 3.0 expand_wide.5
  (283 shorter events, 44.8 us)
Async XLA Ops:
  7.2 179.0 %all-gather.6.cloned.1.call-start = ((), (), s32[]{:S(2)}) async-start(), calls=%async_computation.4 | async-start | bytes 4456448 | tf_op jit(solution)/shard_map/all_gather | solution.py:1340
  7.3 9.5 %collective-permute-start = (bf16[128,1024]{1,0:T(8,128)(2,1)}, bf16[128,1024]{1,0:T(8,128)(2,1)S(1)}, u32[]{:S(2)}, u32[]{:S(2)}) collective-permute-start(bf16[128,1024]{1,0:T(8,128)(2,1)} %bitcast.116), channel_id=1, source_target_pairs={{0,8},{2,10},{8,16},{10,18},{16,24},{18,26},{24,28},{26,30},{28,20... | collective-permute-start | bytes 786440 | tf_op jit(solution)/shard_map/ppermute | solution.py:1348
  10.4 8.0 %collective-permute-start.1 = (bf16[128,1024]{1,0:T(8,128)(2,1)}, bf16[128,1024]{1,0:T(8,128)(2,1)S(1)}, u32[]{:S(2)}, u32[]{:S(2)}) collective-permute-start(bf16[128,1024]{1,0:T(8,128)(2,1)} %bitcast.117), channel_id=1, source_target_pairs={{0,4},{2,6},{8,0},{10,2},{16,8},{18,10},{24,16},{26,18},{28,24},{3... | collective-permute-start | bytes 786440 | tf_op jit(solution)/shard_map/ppermute | solution.py:1348
  18.3 8.4 %collective-permute-start.4 = (bf16[1,1026]{1,0:T(2,128)(2,1)S(1)}, bf16[1,1026]{1,0:T(2,128)(2,1)S(1)}, u32[]{:S(2)}, u32[]{:S(2)}) collective-permute-start(bf16[1,1026]{1,0:T(2,128)(2,1)S(1)} %concatenate.53), channel_id=1, source_target_pairs={{0,1},{1,0},{2,3},{3,2},{4,5},{5,4},{6,7},{7,6},{8,9},{9,8},{10,11... | collective-permute-start | bytes 6164 | tf_op jit(solution)/shard_map/ppermute | solution.py:1337
  19.8 8.4 %collective-permute-start.2 = (bf16[128,1024]{1,0:T(8,128)(2,1)S(1)}, bf16[128,1024]{1,0:T(8,128)(2,1)}, u32[]{:S(2)}, u32[]{:S(2)}) collective-permute-start(bf16[128,1024]{1,0:T(8,128)(2,1)S(1)} %collective-permute-done.refs_2_), channel_id=1, source_target_pairs={{0,8},{2,10},{8,16},{10,18},{16,24},{18,26},{24,28},{26,30},{28,20... | collective-permute-start | bytes 786440 | tf_op jit(solution)/shard_map/ppermute | solution.py:1348
  21.4 6.8 %collective-permute-start.3 = (bf16[128,1024]{1,0:T(8,128)(2,1)S(1)}, bf16[128,1024]{1,0:T(8,128)(2,1)}, u32[]{:S(2)}, u32[]{:S(2)}) collective-permute-start(bf16[128,1024]{1,0:T(8,128)(2,1)S(1)} %collective-permute-done.1.refs_4_), channel_id=1, source_target_pairs={{0,4},{2,6},{8,0},{10,2},{16,8},{18,10},{24,16},{26,18},{28,24},{3... | collective-permute-start | bytes 786440 | tf_op jit(solution)/shard_map/ppermute | solution.py:1348
  21.9 6.4 %collective-permute-start.5 = (bf16[512,192]{1,0:T(8,128)(2,1)S(1)}, bf16[512,192]{1,0:T(8,128)(2,1)S(1)}, u32[]{:S(2)}, u32[]{:S(2)}) collective-permute-start(bf16[512,192]{1,0:T(8,128)(2,1)S(1)} %pad_maximum_fusion.refs_16_.refs_4_), channel_id=1, source_target_pairs={{0,1},{1,0},{2,3},{3,2},{4,5},{5,4},{6,7},{7,6},{8,9},{9,8},{10,11... | collective-permute-start | bytes 589832 | tf_op jit(solution)/shard_map/ppermute | solution.py:1337
  28.8 3.9 %collective-permute-start.13 = (f32[1,2048]{1,0:T(1,128)S(1)}, f32[1,2048]{1,0:T(1,128)S(1)}, u32[]{:S(2)}, u32[]{:S(2)}) collective-permute-start(f32[1,2048]{1,0:T(1,128)S(1)} %constant_dynamic-slice_fusion.18), channel_id=1, source_target_pairs={{0,1},{1,0},{2,3},{3,2},{4,5},{5,4},{6,7},{7,6},{8,9},{9,8},{10,11... | collective-permute-start | bytes 24584 | tf_op jit(solution)/shard_map/ppermute | solution.py:1337
  29.4 6.6 %collective-permute-start.11 = (bf16[128,1024]{1,0:T(8,128)(2,1)}, bf16[128,1024]{1,0:T(8,128)(2,1)S(1)}, u32[]{:S(2)}, u32[]{:S(2)}) collective-permute-start(bf16[128,1024]{1,0:T(8,128)(2,1)} %collective-permute-done.2.refs_6_), channel_id=1, source_target_pairs={{0,8},{2,10},{8,16},{10,18},{16,24},{18,26},{24,28},{26,30},{28,20... | collective-permute-start | bytes 786440 | tf_op jit(solution)/shard_map/ppermute | solution.py:1348
  31.0 6.7 %collective-permute-start.12 = (bf16[128,1024]{1,0:T(8,128)(2,1)}, bf16[128,1024]{1,0:T(8,128)(2,1)}, u32[]{:S(2)}, u32[]{:S(2)}) collective-permute-start(bf16[128,1024]{1,0:T(8,128)(2,1)} %collective-permute-done.3.refs_8_), channel_id=1, source_target_pairs={{0,4},{2,6},{8,0},{10,2},{16,8},{18,10},{24,16},{26,18},{28,24},{3... | collective-permute-start | bytes 786440 | tf_op jit(solution)/shard_map/ppermute | solution.py:1348
  38.4 3.8 %collective-permute-start.10 = (bf16[128,1024]{1,0:T(8,128)(2,1)}, bf16[128,1024]{1,0:T(8,128)(2,1)}, u32[]{:S(2)}, u32[]{:S(2)}) collective-permute-start(bf16[128,1024]{1,0:T(8,128)(2,1)} %collective-permute-done.3.refs_8_), channel_id=1, source_target_pairs={{0,2},{2,0},{4,6},{6,4},{8,10},{10,8},{12,14},{14,12},{16,18},{18,... | collective-permute-start | bytes 786440 | tf_op jit(solution)/shard_map/ppermute | solution.py:1343
  38.8 5.0 %collective-permute-start.9 = (bf16[128,1024]{1,0:T(8,128)(2,1)}, bf16[128,1024]{1,0:T(8,128)(2,1)}, u32[]{:S(2)}, u32[]{:S(2)}) collective-permute-start(bf16[128,1024]{1,0:T(8,128)(2,1)} %collective-permute-done.2.refs_6_), channel_id=1, source_target_pairs={{0,2},{2,0},{4,6},{6,4},{8,10},{10,8},{12,14},{14,12},{16,18},{18,... | collective-permute-start | bytes 786440 | tf_op jit(solution)/shard_map/ppermute | solution.py:1343
  39.3 5.0 %collective-permute-start.14 = (bf16[128,1024]{1,0:T(8,128)(2,1)S(1)}, bf16[128,1024]{1,0:T(8,128)(2,1)}, u32[]{:S(2)}, u32[]{:S(2)}) collective-permute-start(bf16[128,1024]{1,0:T(8,128)(2,1)S(1)} %collective-permute-done.11.refs_10_), channel_id=1, source_target_pairs={{0,2},{2,0},{4,6},{6,4},{8,10},{10,8},{12,14},{14,12},{16,18},{18,... | collective-permute-start | bytes 786440 | tf_op jit(solution)/shard_map/ppermute | solution.py:1343
  40.4 3.9 %collective-permute-start.15 = (bf16[128,1024]{1,0:T(8,128)(2,1)}, bf16[128,1024]{1,0:T(8,128)(2,1)}, u32[]{:S(2)}, u32[]{:S(2)}) collective-permute-start(bf16[128,1024]{1,0:T(8,128)(2,1)} %collective-permute-done.12.refs_12_), channel_id=1, source_target_pairs={{0,2},{2,0},{4,6},{6,4},{8,10},{10,8},{12,14},{14,12},{16,18},{18,... | collective-permute-start | bytes 786440 | tf_op jit(solution)/shard_map/ppermute | solution.py:1343
  40.6 14.5 %collective-permute-start.17 = (bf16[128,1024]{1,0:T(8,128)(2,1)}, bf16[128,1024]{1,0:T(8,128)(2,1)S(1)}, u32[]{:S(2)}, u32[]{:S(2)}) collective-permute-start(bf16[128,1024]{1,0:T(8,128)(2,1)} %fusion.4.refs_14_), channel_id=1, source_target_pairs={{0,1},{1,0},{2,3},{3,2},{4,5},{5,4},{6,7},{7,6},{8,9},{9,8},{10,11... | collective-permute-start | bytes 786440 | tf_op jit(solution)/shard_map/ppermute | solution.py:1337
  42.2 12.9 %collective-permute-start.16 = (bf16[128,1024]{1,0:T(8,128)(2,1)S(1)}, bf16[128,1024]{1,0:T(8,128)(2,1)S(1)}, u32[]{:S(2)}, u32[]{:S(2)}) collective-permute-start(bf16[128,1024]{1,0:T(8,128)(2,1)S(1)} %collective-permute-done.11.refs_10_), channel_id=1, source_target_pairs={{0,8},{2,10},{8,16},{10,18},{16,24},{18,26},{24,28},{26,30},{28,20... | collective-permute-start | bytes 786440 | tf_op jit(solution)/shard_map/ppermute | solution.py:1348
  43.8 30.7 %collective-permute-start.19 = (bf16[256,1024]{1,0:T(8,128)(2,1)S(1)}, bf16[256,1024]{1,0:T(8,128)(2,1)S(1)}, u32[]{:S(2)}, u32[]{:S(2)}) collective-permute-start(bf16[256,1024]{1,0:T(8,128)(2,1)S(1)} %get-tuple-element.225), channel_id=1, source_target_pairs={{0,1},{1,0},{2,3},{3,2},{4,5},{5,4},{6,7},{7,6},{8,9},{9,8},{10,11... | collective-permute-start | bytes 1572872 | tf_op jit(solution)/shard_map/ppermute | solution.py:1337
  55.1 3.2 %collective-permute-start.18 = (bf16[128,1024]{1,0:T(8,128)(2,1)S(1)}, bf16[128,1024]{1,0:T(8,128)(2,1)S(1)}, u32[]{:S(2)}, u32[]{:S(2)}) collective-permute-start(bf16[128,1024]{1,0:T(8,128)(2,1)S(1)} %collective-permute-done.16.refs_0_), channel_id=1, source_target_pairs={{0,2},{2,0},{4,6},{6,4},{8,10},{10,8},{12,14},{14,12},{16,18},{18,... | collective-permute-start | bytes 786440 | tf_op jit(solution)/shard_map/ppermute | solution.py:1343
  55.2 19.4 %collective-permute-start.20 = (bf16[256,1024]{1,0:T(8,128)(2,1)S(1)}, bf16[256,1024]{1,0:T(8,128)(2,1)}, u32[]{:S(2)}, u32[]{:S(2)}) collective-permute-start(bf16[256,1024]{1,0:T(8,128)(2,1)S(1)} %get-tuple-element.226), channel_id=1, source_target_pairs={{0,1},{1,0},{2,3},{3,2},{4,5},{5,4},{6,7},{7,6},{8,9},{9,8},{10,11... | collective-permute-start | bytes 1572872 | tf_op jit(solution)/shard_map/ppermute | solution.py:1337
  75.4 20.5 %collective-permute-start.21 = (bf16[256,1024]{1,0:T(8,128)(2,1)}, bf16[256,1024]{1,0:T(8,128)(2,1)}, u32[]{:S(2)}, u32[]{:S(2)}) collective-permute-start(bf16[256,1024]{1,0:T(8,128)(2,1)} %copy-done.39), channel_id=1, source_target_pairs={{0,4},{2,6},{4,0},{6,2},{8,12},{10,14},{12,8},{14,10},{16,20},{18,... | collective-permute-start | bytes 1572872 | tf_op jit(solution)/shard_map/ppermute | solution.py:1343
  75.9 20.0 %collective-permute-start.24 = (bf16[256,1024]{1,0:T(8,128)(2,1)}, bf16[256,1024]{1,0:T(8,128)(2,1)}, u32[]{:S(2)}, u32[]{:S(2)}) collective-permute-start(bf16[256,1024]{1,0:T(8,128)(2,1)} %copy-done.39), channel_id=1, source_target_pairs={{0,2},{2,0},{4,6},{6,4},{8,10},{10,8},{12,14},{14,12},{16,18},{18,... | collective-permute-start | bytes 1572872 | tf_op jit(solution)/shard_map/ppermute | solution.py:1343
  75.9 18.2 %collective-permute-start.22 = (bf16[256,1024]{1,0:T(8,128)(2,1)S(1)}, bf16[256,1024]{1,0:T(8,128)(2,1)S(1)}, u32[]{:S(2)}, u32[]{:S(2)}) collective-permute-start(bf16[256,1024]{1,0:T(8,128)(2,1)S(1)} %constant_dynamic-slice_fusion.15), channel_id=1, source_target_pairs={{0,1},{1,0},{2,3},{3,2},{4,5},{5,4},{6,7},{7,6},{8,9},{9,8},{10,11... | collective-permute-start | bytes 1572872 | tf_op jit(solution)/shard_map/ppermute | solution.py:1337
  76.5 19.4 %collective-permute-start.25 = (bf16[256,1024]{1,0:T(8,128)(2,1)}, bf16[256,1024]{1,0:T(8,128)(2,1)S(1)}, u32[]{:S(2)}, u32[]{:S(2)}) collective-permute-start(bf16[256,1024]{1,0:T(8,128)(2,1)} %collective-permute-done.20.refs_4_), channel_id=1, source_target_pairs={{0,2},{2,0},{4,6},{6,4},{8,10},{10,8},{12,14},{14,12},{16,18},{18,... | collective-permute-start | bytes 1572872 | tf_op jit(solution)/shard_map/ppermute | solution.py:1343
  76.7 19.1 %all-to-all-start = ((bf16[16,64,128]{2,1,0:T(8,128)(2,1)}), bf16[16,64,128]{2,1,0:T(8,128)(2,1)S(1)}, u32[]{:S(2)}, u32[]{:S(2)}) async-start(bf16[16,64,128]{2,1,0:T(8,128)(2,1)} %get-tuple-element.229), calls=%async_computation | async-start | bytes 524288 | tf_op jit(solution)/shard_map/all_to_all | solution.py:1514
  84.3 102.0 %all-gather.4.cloned.1.call-start = ((), (), s32[]{:S(2)}) async-start(), calls=%async_computation.3 | async-start | bytes 4456448 | tf_op jit(solution)/shard_map/all_gather | solution.py:1340
  87.2 5.0 %collective-permute-start.23 = (bf16[1,3584]{1,0:T(2,128)(2,1)S(1)}, bf16[1,3584]{1,0:T(2,128)(2,1)S(1)}, u32[]{:S(2)}, u32[]{:S(2)}) collective-permute-start(bf16[1,3584]{1,0:T(2,128)(2,1)S(1)} %pad_maximum_fusion.4), channel_id=1, source_target_pairs={{0,1},{1,0},{2,3},{3,2},{4,5},{5,4},{6,7},{7,6},{8,9},{9,8},{10,11... | collective-permute-start | bytes 21512 | tf_op jit(solution)/shard_map/ppermute | solution.py:1337
  92.2 15.5 %collective-permute-start.28 = (bf16[256,1024]{1,0:T(8,128)(2,1)}, bf16[256,1024]{1,0:T(8,128)(2,1)}, u32[]{:S(2)}, u32[]{:S(2)}) collective-permute-start(bf16[256,1024]{1,0:T(8,128)(2,1)} %collective-permute-done.20.refs_4_), channel_id=1, source_target_pairs={{0,4},{2,6},{4,0},{6,2},{8,12},{10,14},{12,8},{14,10},{16,20},{18,... | collective-permute-start | bytes 1572872 | tf_op jit(solution)/shard_map/ppermute | solution.py:1343
  94.2 13.5 %collective-permute-start.27 = (bf16[128,2048]{1,0:T(8,128)(2,1)S(1)}, bf16[128,2048]{1,0:T(8,128)(2,1)}, u32[]{:S(2)}, u32[]{:S(2)}) collective-permute-start(bf16[128,2048]{1,0:T(8,128)(2,1)S(1)} %convolution_convert_fusion), channel_id=1, source_target_pairs={{0,1},{1,0},{2,3},{3,2},{4,5},{5,4},{6,7},{7,6},{8,9},{9,8},{10,11... | collective-permute-start | bytes 1572872 | tf_op jit(solution)/shard_map/ppermute | solution.py:1337
  95.9 4.7 %collective-permute-start.26 = (bf16[256,1024]{1,0:T(8,128)(2,1)S(1)}, bf16[256,1024]{1,0:T(8,128)(2,1)}, u32[]{:S(2)}, u32[]{:S(2)}) collective-permute-start(bf16[256,1024]{1,0:T(8,128)(2,1)S(1)} %collective-permute-done.22.mine_ref.refs_16_), channel_id=1, source_target_pairs={{0,2},{2,0},{4,6},{6,4},{8,10},{10,8},{12,14},{14,12},{16,18},{18,... | collective-permute-start | bytes 1572872 | tf_op jit(solution)/shard_map/ppermute | solution.py:1343
  96.0 11.6 %collective-permute-start.29 = (bf16[256,1024]{1,0:T(8,128)(2,1)}, bf16[256,1024]{1,0:T(8,128)(2,1)S(1)}, u32[]{:S(2)}, u32[]{:S(2)}) collective-permute-start(bf16[256,1024]{1,0:T(8,128)(2,1)} %collective-permute-done.21.refs_2_), channel_id=1, source_target_pairs={{0,2},{2,0},{4,6},{6,4},{8,10},{10,8},{12,14},{14,12},{16,18},{18,... | collective-permute-start | bytes 1572872 | tf_op jit(solution)/shard_map/ppermute | solution.py:1343
  107.7 3.8 %collective-permute-start.30 = (bf16[256,1024]{1,0:T(8,128)(2,1)}, bf16[256,1024]{1,0:T(8,128)(2,1)S(1)}, u32[]{:S(2)}, u32[]{:S(2)}) collective-permute-start(bf16[256,1024]{1,0:T(8,128)(2,1)} %collective-permute-done.28.refs_6_), channel_id=1, source_target_pairs={{0,2},{2,0},{4,6},{6,4},{8,10},{10,8},{12,14},{14,12},{16,18},{18,... | collective-permute-start | bytes 1572872 | tf_op jit(solution)/shard_map/ppermute | solution.py:1343
  109.5 14.0 %collective-permute-start.32 = (bf16[128,1024]{1,0:T(8,128)(2,1)S(1)}, bf16[128,1024]{1,0:T(8,128)(2,1)S(1)}, u32[]{:S(2)}, u32[]{:S(2)}) collective-permute-start(bf16[128,1024]{1,0:T(8,128)(2,1)S(1)} %constant_dynamic-slice_fusion.10.down_own), channel_id=1, source_target_pairs={{0,1},{1,0},{2,3},{3,2},{4,5},{5,4},{6,7},{7,6},{8,9},{9,8},{10,11... | collective-permute-start | bytes 786440 | tf_op jit(solution)/shard_map/ppermute | solution.py:1337
  111.2 12.6 %collective-permute-start.31 = (bf16[512,256]{1,0:T(8,128)(2,1)S(1)}, bf16[512,256]{1,0:T(8,128)(2,1)S(1)}, u32[]{:S(2)}, u32[]{:S(2)}) collective-permute-start(bf16[512,256]{1,0:T(8,128)(2,1)S(1)} %get-tuple-element.262), channel_id=1, source_target_pairs={{0,1},{1,0},{2,3},{3,2},{4,5},{5,4},{6,7},{7,6},{8,9},{9,8},{10,11... | collective-permute-start | bytes 786440 | tf_op jit(solution)/shard_map/ppermute | solution.py:1337
  125.9 10.4 %collective-permute-start.33 = (bf16[512,1024]{1,0:T(8,128)(2,1)S(1)}, bf16[512,1024]{1,0:T(8,128)(2,1)S(1)}, u32[]{:S(2)}, u32[]{:S(2)}) collective-permute-start(bf16[512,1024]{1,0:T(8,128)(2,1)S(1)} %convolution_convert_fusion.1), channel_id=1, source_target_pairs={{0,2},{2,0},{4,6},{6,4},{8,10},{10,8},{12,14},{14,12},{16,18},{18,... | collective-permute-start | bytes 3145736 | tf_op jit(solution)/shard_map/ppermute | solution.py:1343
  126.0 16.5 %all-to-all-start.1 = ((bf16[16,64,128]{2,1,0:T(8,128)(2,1)}), bf16[16,64,128]{2,1,0:T(8,128)(2,1)}, u32[]{:S(2)}, u32[]{:S(2)}) async-start(bf16[16,64,128]{2,1,0:T(8,128)(2,1)} %get-tuple-element.265), calls=%async_computation.1 | async-start | bytes 524288 | tf_op jit(solution)/shard_map/all_to_all | solution.py:1568
  131.5 32.4 %collective-permute-start.35 = (bf16[128,3072]{1,0:T(8,128)(2,1)}, bf16[128,3072]{1,0:T(8,128)(2,1)S(1)}, u32[]{:S(2)}, u32[]{:S(2)}) collective-permute-start(bf16[128,3072]{1,0:T(8,128)(2,1)} %get-tuple-element.278), channel_id=1, source_target_pairs={{0,1},{1,0},{2,3},{3,2},{4,5},{5,4},{6,7},{7,6},{8,9},{9,8},{10,11... | collective-permute-start | bytes 2359304 | tf_op jit(solution)/shard_map/ppermute | solution.py:1337
  142.6 20.2 %collective-permute-start.34 = (bf16[8,32,1024]{2,1,0:T(8,128)(2,1)S(1)}, bf16[8,32,1024]{2,1,0:T(8,128)(2,1)S(1)}, u32[]{:S(2)}, u32[]{:S(2)}) collective-permute-start(bf16[8,32,1024]{2,1,0:T(8,128)(2,1)S(1)} %fusion.2), channel_id=1, source_target_pairs={{0,1},{1,0},{2,3},{3,2},{4,5},{5,4},{6,7},{7,6},{8,9},{9,8},{10,11... | collective-permute-start | bytes 1572872 | tf_op jit(solution)/shard_map/ppermute | solution.py:1337
  164.0 37.6 %all-to-all-start.2 = ((bf16[16,192,128]{2,1,0:T(8,128)(2,1)}), bf16[16,192,128]{2,1,0:T(8,128)(2,1)S(1)}, u32[]{:S(2)}, u32[]{:S(2)}) async-start(bf16[16,192,128]{2,1,0:T(8,128)(2,1)} %get-tuple-element.289), calls=%async_computation.2 | async-start | bytes 1572864 | tf_op jit(solution)/shard_map/all_to_all | solution.py:1594
  170.2 96.6 %all-gather.8.cloned.1.call-start = ((), (), s32[]{:S(2)}) async-start(), calls=%async_computation.5 | async-start | bytes 3342336 | tf_op jit(solution)/shard_map/all_gather | solution.py:1340
  173.9 7.8 %collective-permute-start.36 = (bf16[192,512]{1,0:T(8,128)(2,1)S(1)}, bf16[192,512]{1,0:T(8,128)(2,1)S(1)}, u32[]{:S(2)}, u32[]{:S(2)}) collective-permute-start(bf16[192,512]{1,0:T(8,128)(2,1)S(1)} %dynamic-slice_convert_fusion.2), channel_id=1, source_target_pairs={{0,1},{1,0},{2,3},{3,2},{4,5},{5,4},{6,7},{7,6},{8,9},{9,8},{10,11... | collective-permute-start | bytes 589832 | tf_op jit(solution)/shard_map/ppermute | solution.py:1337
  175.3 10.9 %collective-permute-start.37 = (bf16[4,32,1024]{2,1,0:T(8,128)(2,1)S(1)}, bf16[4,32,1024]{2,1,0:T(8,128)(2,1)S(1)}, u32[]{:S(2)}, u32[]{:S(2)}) collective-permute-start(bf16[4,32,1024]{2,1,0:T(8,128)(2,1)S(1)} %fusion.6), channel_id=1, source_target_pairs={{0,4},{2,6},{4,0},{6,2},{8,12},{10,14},{12,8},{14,10},{16,20},{18,... | collective-permute-start | bytes 786440 | tf_op jit(solution)/shard_map/ppermute | solution.py:1343
  177.8 23.8 %collective-permute-start.40 = (bf16[128,3072]{1,0:T(8,128)(2,1)}, bf16[128,3072]{1,0:T(8,128)(2,1)}, u32[]{:S(2)}, u32[]{:S(2)}) collective-permute-start(bf16[128,3072]{1,0:T(8,128)(2,1)} %get-tuple-element.296), channel_id=1, source_target_pairs={{0,1},{1,0},{2,3},{3,2},{4,5},{5,4},{6,7},{7,6},{8,9},{9,8},{10,11... | collective-permute-start | bytes 2359304 | tf_op jit(solution)/shard_map/ppermute | solution.py:1337
  186.3 15.2 %collective-permute-start.38 = (bf16[2,32,1024]{2,1,0:T(8,128)(2,1)S(1)}, bf16[2,32,1024]{2,1,0:T(8,128)(2,1)S(1)}, u32[]{:S(2)}, u32[]{:S(2)}) collective-permute-start(bf16[2,32,1024]{2,1,0:T(8,128)(2,1)S(1)} %fusion.11), channel_id=1, source_target_pairs={{0,8},{2,10},{4,12},{6,14},{8,0},{10,2},{12,4},{14,6},{16,24},{18,... | collective-permute-start | bytes 393224 | tf_op jit(solution)/shard_map/ppermute | solution.py:1343
  201.7 3.7 %collective-permute-start.42 = (bf16[128,3072]{1,0:T(8,128)(2,1)}, bf16[128,3072]{1,0:T(8,128)(2,1)}, u32[]{:S(2)}, u32[]{:S(2)}) collective-permute-start(bf16[128,3072]{1,0:T(8,128)(2,1)} %collective-permute-done.40.mine_1), channel_id=1, source_target_pairs={{0,2},{2,0},{4,6},{6,4},{8,10},{10,8},{12,14},{14,12},{16,18},{18,... | collective-permute-start | bytes 2359304 | tf_op jit(solution)/shard_map/ppermute | solution.py:1343
  202.2 14.8 %collective-permute-start.39 = (bf16[2048,128]{1,0:T(8,128)(2,1)}, bf16[2048,128]{1,0:T(8,128)(2,1)S(1)}, u32[]{:S(2)}, u32[]{:S(2)}) collective-permute-start(bf16[2048,128]{1,0:T(8,128)(2,1)} %get-tuple-element.292), channel_id=1, source_target_pairs={{0,1},{1,0},{2,3},{3,2},{4,5},{5,4},{6,7},{7,6},{8,9},{9,8},{10,11... | collective-permute-start | bytes 1572872 | tf_op jit(solution)/shard_map/ppermute | solution.py:1337
  203.2 9.4 %collective-permute-start.44 = (bf16[1,32,1024]{2,1,0:T(8,128)(2,1)S(1)}, bf16[1,32,1024]{2,1,0:T(8,128)(2,1)S(1)}, u32[]{:S(2)}, u32[]{:S(2)}) collective-permute-start(bf16[1,32,1024]{2,1,0:T(8,128)(2,1)S(1)} %dynamic-slice_convert_fusion.3), channel_id=1, source_target_pairs={{0,16},{2,18},{4,20},{6,22},{8,24},{10,26},{12,28},{14,30},{16,0},... | collective-permute-start | bytes 196616 | tf_op jit(solution)/shard_map/ppermute | solution.py:1343
  211.7 6.0 %collective-permute-start.43 = (f32[12,1024]{1,0:T(8,128)}, f32[12,1024]{1,0:T(8,128)S(1)}, u32[]{:S(2)}, u32[]{:S(2)}) collective-permute-start(f32[12,1024]{1,0:T(8,128)} %get-tuple-element.305), channel_id=1, source_target_pairs={{0,1},{1,0},{2,3},{3,2},{4,5},{5,4},{6,7},{7,6},{8,9},{9,8},{10,11... | collective-permute-start | bytes 147464 | tf_op jit(solution)/shard_map/ppermute | solution.py:1337
  219.6 47.2 %collective-permute-start.52 = (bf16[1024,1024]{1,0:T(8,128)(2,1)}, bf16[1024,1024]{1,0:T(8,128)(2,1)}, u32[]{:S(2)}, u32[]{:S(2)}) collective-permute-start(bf16[1024,1024]{1,0:T(8,128)(2,1)} %constant_dynamic-slice_fusion.9), channel_id=1, source_target_pairs={{0,1},{1,0},{2,3},{3,2},{4,5},{5,4},{6,7},{7,6},{8,9},{9,8},{10,11... | collective-permute-start | bytes 6291464 | tf_op jit(solution)/shard_map/ppermute | solution.py:1337
  220.6 20.6 %collective-permute-start.45 = (bf16[2432,128]{1,0:T(8,128)(2,1)S(1)}, bf16[2432,128]{1,0:T(8,128)(2,1)S(1)}, u32[]{:S(2)}, u32[]{:S(2)}) collective-permute-start(bf16[2432,128]{1,0:T(8,128)(2,1)S(1)} %constant_dynamic-update-slice_fusion.refs_0_), channel_id=1, source_target_pairs={{0,8},{2,10},{8,16},{10,18},{16,24},{18,26},{24,28},{26,30},{28,20... | collective-permute-start | bytes 1867784 | tf_op jit(solution)/shard_map/ppermute | solution.py:1348
  220.6 27.7 %collective-permute-start.46 = (bf16[2432,128]{1,0:T(8,128)(2,1)S(1)}, bf16[2432,128]{1,0:T(8,128)(2,1)}, u32[]{:S(2)}, u32[]{:S(2)}) collective-permute-start(bf16[2432,128]{1,0:T(8,128)(2,1)S(1)} %constant_dynamic-update-slice_fusion.refs_0_), channel_id=1, source_target_pairs={{0,4},{2,6},{8,0},{10,2},{16,8},{18,10},{24,16},{26,18},{28,24},{3... | collective-permute-start | bytes 1867784 | tf_op jit(solution)/shard_map/ppermute | solution.py:1348
  222.6 26.3 %collective-permute-start.49 = (bf16[2432,128]{1,0:T(8,128)(2,1)S(1)}, bf16[2432,128]{1,0:T(8,128)(2,1)}, u32[]{:S(2)}, u32[]{:S(2)}) collective-permute-start(bf16[2432,128]{1,0:T(8,128)(2,1)S(1)} %constant_dynamic-update-slice_fusion.refs_0_), channel_id=1, source_target_pairs={{0,2},{2,0},{4,6},{6,4},{8,10},{10,8},{12,14},{14,12},{16,18},{18,... | collective-permute-start | bytes 1867784 | tf_op jit(solution)/shard_map/ppermute | solution.py:1343
  248.4 3.3 %collective-permute-start.50 = (bf16[2432,128]{1,0:T(8,128)(2,1)S(1)}, bf16[2432,128]{1,0:T(8,128)(2,1)}, u32[]{:S(2)}, u32[]{:S(2)}) collective-permute-start(bf16[2432,128]{1,0:T(8,128)(2,1)S(1)} %collective-permute-done.45.refs_2_), channel_id=1, source_target_pairs={{0,2},{2,0},{4,6},{6,4},{8,10},{10,8},{12,14},{14,12},{16,18},{18,... | collective-permute-start | bytes 1867784 | tf_op jit(solution)/shard_map/ppermute | solution.py:1343
  248.4 3.6 %collective-permute-start.51 = (bf16[2432,128]{1,0:T(8,128)(2,1)}, bf16[2432,128]{1,0:T(8,128)(2,1)}, u32[]{:S(2)}, u32[]{:S(2)}) collective-permute-start(bf16[2432,128]{1,0:T(8,128)(2,1)} %collective-permute-done.46.refs_4_), channel_id=1, source_target_pairs={{0,2},{2,0},{4,6},{6,4},{8,10},{10,8},{12,14},{14,12},{16,18},{18,... | collective-permute-start | bytes 1867784 | tf_op jit(solution)/shard_map/ppermute | solution.py:1343
  248.9 15.9 %collective-permute-start.47 = (bf16[2432,128]{1,0:T(8,128)(2,1)S(1)}, bf16[2432,128]{1,0:T(8,128)(2,1)S(1)}, u32[]{:S(2)}, u32[]{:S(2)}) collective-permute-start(bf16[2432,128]{1,0:T(8,128)(2,1)S(1)} %collective-permute-done.45.refs_2_), channel_id=1, source_target_pairs={{0,8},{2,10},{8,16},{10,18},{16,24},{18,26},{24,28},{26,30},{28,20... | collective-permute-start | bytes 1867784 | tf_op jit(solution)/shard_map/ppermute | solution.py:1348
  248.9 16.2 %collective-permute-start.48 = (bf16[2432,128]{1,0:T(8,128)(2,1)}, bf16[2432,128]{1,0:T(8,128)(2,1)S(1)}, u32[]{:S(2)}, u32[]{:S(2)}) collective-permute-start(bf16[2432,128]{1,0:T(8,128)(2,1)} %collective-permute-done.46.refs_4_), channel_id=1, source_target_pairs={{0,4},{2,6},{8,0},{10,2},{16,8},{18,10},{24,16},{26,18},{28,24},{3... | collective-permute-start | bytes 1867784 | tf_op jit(solution)/shard_map/ppermute | solution.py:1348
  266.8 10.0 %collective-permute-start.55 = (bf16[1024,1024]{1,0:T(8,128)(2,1)}, bf16[1024,1024]{1,0:T(8,128)(2,1)}, u32[]{:S(2)}, u32[]{:S(2)}) collective-permute-start(bf16[1024,1024]{1,0:T(8,128)(2,1)} %collective-permute-done.52), channel_id=1, source_target_pairs={{0,2},{2,0},{4,6},{6,4},{8,10},{10,8},{12,14},{14,12},{16,18},{18,... | collective-permute-start | bytes 6291464 | tf_op jit(solution)/shard_map/ppermute | solution.py:1343
  266.8 16.4 %collective-permute-start.53 = (bf16[2432,128]{1,0:T(8,128)(2,1)S(1)}, bf16[2432,128]{1,0:T(8,128)(2,1)S(1)}, u32[]{:S(2)}, u32[]{:S(2)}) collective-permute-start(bf16[2432,128]{1,0:T(8,128)(2,1)S(1)} %collective-permute-done.47.refs_0_.refs_6_), channel_id=1, source_target_pairs={{0,8},{2,10},{8,16},{10,18},{16,24},{18,26},{24,28},{26,30},{28,20... | collective-permute-start | bytes 1867784 | tf_op jit(solution)/shard_map/ppermute | solution.py:1348
  267.0 16.5 %collective-permute-start.56 = (bf16[2432,128]{1,0:T(8,128)(2,1)S(1)}, bf16[2432,128]{1,0:T(8,128)(2,1)S(1)}, u32[]{:S(2)}, u32[]{:S(2)}) collective-permute-start(bf16[2432,128]{1,0:T(8,128)(2,1)S(1)} %collective-permute-done.47.refs_0_.refs_6_), channel_id=1, source_target_pairs={{0,2},{2,0},{4,6},{6,4},{8,10},{10,8},{12,14},{14,12},{16,18},{18,... | collective-permute-start | bytes 1867784 | tf_op jit(solution)/shard_map/ppermute | solution.py:1343
  267.3 16.1 %collective-permute-start.54 = (bf16[2432,128]{1,0:T(8,128)(2,1)S(1)}, bf16[2432,128]{1,0:T(8,128)(2,1)S(1)}, u32[]{:S(2)}, u32[]{:S(2)}) collective-permute-start(bf16[2432,128]{1,0:T(8,128)(2,1)S(1)} %collective-permute-done.48.refs_2_.refs_8_), channel_id=1, source_target_pairs={{0,4},{2,6},{8,0},{10,2},{16,8},{18,10},{24,16},{26,18},{28,24},{3... | collective-permute-start | bytes 1867784 | tf_op jit(solution)/shard_map/ppermute | solution.py:1348
  269.0 14.4 %collective-permute-start.57 = (bf16[2432,128]{1,0:T(8,128)(2,1)S(1)}, bf16[2432,128]{1,0:T(8,128)(2,1)S(1)}, u32[]{:S(2)}, u32[]{:S(2)}) collective-permute-start(bf16[2432,128]{1,0:T(8,128)(2,1)S(1)} %collective-permute-done.48.refs_2_.refs_8_), channel_id=1, source_target_pairs={{0,2},{2,0},{4,6},{6,4},{8,10},{10,8},{12,14},{14,12},{16,18},{18,... | collective-permute-start | bytes 1867784 | tf_op jit(solution)/shard_map/ppermute | solution.py:1343
  283.5 2.7 collective-permute-start.58
  283.5 2.9 collective-permute-start.59
  284.1 10.0 %collective-permute-start.60 = (bf16[1216,128]{1,0:T(8,128)(2,1)S(1)}, bf16[1216,128]{1,0:T(8,128)(2,1)S(1)}, u32[]{:S(2)}, u32[]{:S(2)}) collective-permute-start(bf16[1216,128]{1,0:T(8,128)(2,1)S(1)} %slice.128), channel_id=1, source_target_pairs={{0,8},{2,10},{8,16},{10,18},{16,24},{18,26},{24,28},{26,30},{28,20... | collective-permute-start | bytes 933896 | tf_op jit(solution)/shard_map/ppermute | solution.py:1348
  285.7 9.3 %collective-permute-start.61 = (bf16[1216,128]{1,0:T(8,128)(2,1)S(1)}, bf16[1216,128]{1,0:T(8,128)(2,1)S(1)}, u32[]{:S(2)}, u32[]{:S(2)}) collective-permute-start(bf16[1216,128]{1,0:T(8,128)(2,1)S(1)} %slice.129), channel_id=1, source_target_pairs={{0,4},{2,6},{8,0},{10,2},{16,8},{18,10},{24,16},{26,18},{28,24},{3... | collective-permute-start | bytes 933896 | tf_op jit(solution)/shard_map/ppermute | solution.py:1348
  (56 other events, 587.6 us)
Sparse Core Ops, SparseCore 0:
  37.8 50.4 all-gather.5
  107.8 52.1 all-gather.3
  203.2 49.3 all-gather.7
